TPU v7x, 512 devices: a whole 4x4x16 slice. The times are simulated.
512 devices in a mesh: wide: 64 (over z_hi, y, x, core), narrow: 8 (over z_lo).
Axes of the slice: x: 4, y: 4, z: 16 (z_hi: 2, z_lo: 8; z = z_hi * 8 + z_lo), core: 2. Of those that a mesh axis runs over, the one named last changes fastest.
Arguments:
- right_side: float32 [1024, 128, 128], P('wide', 'narrow'), may hold values from -8 to 8
- labels: int32 [128, 16, 16], P('wide', 'narrow'), may hold values from 0 to 15
- material_table: float32 [16], replicated, may hold values from 0.1 to 10
- robin_table: float32 [8], replicated, may hold values from 0.5 to 8
- robin_index: int32 [64, 8, 2], P('wide', 'narrow'), may hold values from 0 to 7
- coarse_rows: float32 [512, 512], P(('wide', 'narrow')), may hold values from -0.0014648438 to 0.0014648438
Outputs:
- solution: bfloat16 [1024, 128, 128], P('wide', 'narrow')
- residual: bfloat16 [1024, 128, 128], P('wide', 'narrow')
All inputs are finite; a program needn't handle non-finite values.
Results may differ from a plain program's by a relative error of at most 0.0015.
Values sent between devices are 32-bit elements; how exact they have to be, the bound alone decides.
No kernel may reach another device: no remote copies, remote signals or barrier semaphores. Data moves between devices by JAX's collectives and lax.ppermute only.
A program may use at most 64 MiB of HBM per device.

v0:
```python
import jax
import jax.numpy as jnp
from jax import lax
from jax.sharding import PartitionSpec as P

BLOCK = 8
SWEEPS = 4
ITERS = 2


reaction = 1.0


def padded(array, sides, width):
    edges = {}
    for axis, dim in sides:
        peers, length = (lax.axis_size(axis), array.shape[dim])
        up = [(i, (i + 1) % peers) for i in range(peers - 1)]
        last = lax.slice_in_dim(array, length - width, length, axis=dim)
        first = lax.slice_in_dim(array, 0, width, axis=dim)
        edges[dim] = (
            lax.ppermute(last, axis, up),
            lax.ppermute(first, axis, [(b, a) for a, b in up]),
        )
    done = []
    for _, dim in sides:
        low, high = edges[dim]
        around = [(width, width) if d in done else (0, 0) for d in range(array.ndim)]
        array = jnp.concatenate([jnp.pad(low, around), array, jnp.pad(high, around)], axis=dim)
        done.append(dim)
    return array


def shifted(array, axis, by):
    peers = lax.axis_size(axis)
    pairs = [(i, i + by) for i in range(peers) if 0 <= i + by < peers]
    return lax.ppermute(array, axis, pairs)


def spread_cells(blocks):
    size_a, size_b, size_c = blocks.shape
    grown_up = jnp.broadcast_to(
        blocks[:, None, :, None, :, None], (size_a, BLOCK, size_b, BLOCK, size_c, BLOCK)
    )
    return grown_up.reshape(size_a * BLOCK, size_b * BLOCK, size_c * BLOCK)


def spread_face(blocks):
    size_a, size_b = blocks.shape
    grown_up = jnp.broadcast_to(blocks[:, None, :, None], (size_a, BLOCK, size_b, BLOCK))
    return grown_up.reshape(size_a * BLOCK, size_b * BLOCK)


def face_conduct(kappa, west_k, east_k, south_k, north_k):
    west_v = jnp.concatenate([west_k[None], kappa[:-1]], 0)
    east_v = jnp.concatenate([kappa[1:], east_k[None]], 0)
    south_v = jnp.concatenate([south_k[:, None], kappa[:, :-1]], 1)
    north_v = jnp.concatenate([kappa[:, 1:], north_k[:, None]], 1)
    below_v = jnp.concatenate([kappa[:, :, :1], kappa[:, :, :-1]], 2)
    above_v = jnp.concatenate([kappa[:, :, 1:], kappa[:, :, -1:]], 2)
    return (
        0.5 * (kappa + west_v),
        0.5 * (kappa + east_v),
        0.5 * (kappa + south_v),
        0.5 * (kappa + north_v),
        0.5 * (kappa + below_v),
        0.5 * (kappa + above_v),
    )


def neighbour_sum(field_now, conduct, borders):
    zero_layer = jnp.zeros_like(field_now[:, :, :1])
    coupled = conduct[0] * jnp.concatenate([borders[0][None], field_now[:-1]], 0)
    coupled = coupled + conduct[1] * jnp.concatenate([field_now[1:], borders[1][None]], 0)
    coupled = coupled + conduct[2] * jnp.concatenate([borders[2][:, None], field_now[:, :-1]], 1)
    coupled = coupled + conduct[3] * jnp.concatenate([field_now[:, 1:], borders[3][:, None]], 1)
    coupled = coupled + conduct[4] * jnp.concatenate([zero_layer, field_now[:, :, :-1]], 2)
    return coupled + conduct[5] * jnp.concatenate([field_now[:, :, 1:], zero_layer], 2)


def side_marks(shape):
    index_x = lax.broadcasted_iota(jnp.int32, (shape[0], shape[1], 1), 0)
    index_y = lax.broadcasted_iota(jnp.int32, (shape[0], shape[1], 1), 1)
    return (
        (index_x == 0).astype(jnp.float32),
        (index_x == shape[0] - 1).astype(jnp.float32),
        (index_y == 0).astype(jnp.float32),
        (index_y == shape[1] - 1).astype(jnp.float32),
    )


def assemble_local(material):
    kappa_blocks, west_b, east_b, south_b, north_b, inside, robin_pair = material
    kappa = spread_cells(kappa_blocks)
    sides = (spread_face(west_b), spread_face(east_b), spread_face(south_b), spread_face(north_b))
    owned = (kappa[0], kappa[-1], kappa[:, 0], kappa[:, -1])
    chosen = [jnp.where(inside[side] > 0, sides[side], owned[side]) for side in range(4)]
    conduct = face_conduct(kappa, chosen[0], chosen[1], chosen[2], chosen[3])
    conduct_sum = conduct[0] + conduct[1] + conduct[2] + conduct[3] + conduct[4] + conduct[5]
    marks = side_marks(kappa.shape)
    robin_term = robin_pair[0] * (inside[0] * marks[0] + inside[1] * marks[1]) + robin_pair[1] * (
        inside[2] * marks[2] + inside[3] * marks[3]
    )
    parity = (
        lax.broadcasted_iota(jnp.int32, kappa.shape, 0)
        + lax.broadcasted_iota(jnp.int32, kappa.shape, 1)
        + lax.broadcasted_iota(jnp.int32, kappa.shape, 2)
    ) % 2
    return (conduct, conduct_sum, robin_term, parity)


def robin_source(traces, shape):
    marks = side_marks(shape)
    return (
        marks[0] * traces[0][None]
        + marks[1] * traces[1][None]
        + marks[2] * traces[2][:, None]
        + marks[3] * traces[3][:, None]
    )


def relax(field_now, source, conduct, diagonal, parity):
    blank_x = jnp.zeros_like(field_now[0])
    blank_y = jnp.zeros_like(field_now[:, 0])
    blanks = (blank_x, blank_x, blank_y, blank_y)
    for sweep_at in range(SWEEPS):
        for colour in range(2):
            update = (source + neighbour_sum(field_now, conduct, blanks)) / diagonal
            field_now = jnp.where(parity == colour, update, field_now)
    return field_now


def misfit(field_now, source_part, conduct, conduct_sum, borders):
    return (
        source_part
        - (reaction + conduct_sum) * field_now
        + neighbour_sum(field_now, conduct, borders)
    )


def coarse_weights(extent_x, extent_y):
    along_x = (jnp.arange(extent_x, dtype=jnp.float32) + 0.5) / extent_x
    along_y = (jnp.arange(extent_y, dtype=jnp.float32) + 0.5) / extent_y
    return (
        (1.0 - along_x)[:, None] * (1.0 - along_y)[None, :],
        along_x[:, None] * (1.0 - along_y)[None, :],
        (1.0 - along_x)[:, None] * along_y[None, :],
        along_x[:, None] * along_y[None, :],
    )


def restrict(leftover):
    column_sum = jnp.sum(leftover, axis=2)
    weights = coarse_weights(leftover.shape[0], leftover.shape[1])
    return jnp.stack([jnp.sum(weights[corner] * column_sum) for corner in range(4)])


def interpolate(corners, extent_x, extent_y):
    weights = coarse_weights(extent_x, extent_y)
    return (
        corners[0, 0] * weights[0]
        + corners[1, 0] * weights[1]
        + corners[0, 1] * weights[2]
        + corners[1, 1] * weights[3]
    )


def robin_traces(field_now, borders, conduct, inside, robin_pair):
    return (
        inside[0] * (conduct[0][0] * borders[0] + robin_pair[0] * field_now[0]),
        inside[1] * (conduct[1][-1] * borders[1] + robin_pair[0] * field_now[-1]),
        inside[2] * (conduct[2][:, 0] * borders[2] + robin_pair[1] * field_now[:, 0]),
        inside[3] * (conduct[3][:, -1] * borders[3] + robin_pair[1] * field_now[:, -1]),
    )


def combine_partials(stacked):
    from_west = jnp.pad(stacked[:-1, :, 1], ((1, 0), (0, 0)))
    from_south = jnp.pad(stacked[:, :-1, 2], ((0, 0), (1, 0)))
    from_corner = jnp.pad(stacked[:-1, :-1, 3], ((1, 0), (1, 0)))
    return stacked[:, :, 0] + from_west + from_south + from_corner


def table_lookup(keys, table):
    entries = jnp.arange(table.shape[0], dtype=jnp.int32)
    return jnp.sum(jnp.where(keys[..., None] == entries, table, 0.0), -1)


def face_rows(widened):
    return (widened[0, 1:-1], widened[-1, 1:-1], widened[1:-1, 0], widened[1:-1, -1])


def body(right_side, labels, material_table, robin_table, robin_index, coarse_rows):
    wide_at = lax.axis_index("wide")
    narrow_at = lax.axis_index("narrow")
    wide_count = lax.axis_size("wide")
    narrow_count = lax.axis_size("narrow")
    extent_x, extent_y = (right_side.shape[0], right_side.shape[1])
    label_pad = padded(labels, (("wide", 0), ("narrow", 1)), 1)
    kappa_pad = table_lookup(label_pad, material_table)
    inside = jnp.stack(
        [wide_at > 0, wide_at < wide_count - 1, narrow_at > 0, narrow_at < narrow_count - 1]
    ).astype(jnp.float32)
    robin_pair = table_lookup(robin_index[0, 0], robin_table)
    material = (
        kappa_pad[1:-1, 1:-1],
        kappa_pad[0, 1:-1],
        kappa_pad[-1, 1:-1],
        kappa_pad[1:-1, 0],
        kappa_pad[1:-1, -1],
        inside,
        robin_pair,
    )
    conduct, conduct_sum, robin_term, parity = assemble_local(material)
    diagonal = reaction + conduct_sum + robin_term
    solution_now = jnp.zeros_like(right_side)
    traces = (
        jnp.zeros_like(right_side[0]),
        jnp.zeros_like(right_side[0]),
        jnp.zeros_like(right_side[:, 0]),
        jnp.zeros_like(right_side[:, 0]),
    )
    for outer in range(ITERS):
        source = right_side + robin_source(traces, right_side.shape)
        solution_now = relax(solution_now, source, conduct, diagonal, parity)
        widened = padded(solution_now, (("wide", 0), ("narrow", 1)), 1)
        borders = face_rows(widened)
        partial_value = restrict(misfit(solution_now, right_side, conduct, conduct_sum, borders))
        every = lax.all_gather(partial_value[None], ("wide", "narrow"), axis=0, tiled=True)
        coarse_vec = combine_partials(every.reshape(wide_count, narrow_count, 4)).reshape(-1)
        coarse_own = jnp.dot(
            coarse_rows,
            coarse_vec,
            precision=lax.Precision.HIGHEST,
            preferred_element_type=jnp.float32,
        )
        east_value = shifted(coarse_own, "wide", -1)
        column_pair = jnp.stack([coarse_own[0], east_value[0]])
        north_pair = shifted(column_pair, "narrow", -1)
        corners = jnp.stack(
            [jnp.stack([column_pair[0], north_pair[0]]), jnp.stack([column_pair[1], north_pair[1]])]
        )
        solution_now = solution_now + interpolate(corners, extent_x, extent_y)[:, :, None]
        widened = padded(solution_now, (("wide", 0), ("narrow", 1)), 1)
        borders = face_rows(widened)
        if outer + 1 < ITERS:
            traces = robin_traces(solution_now, borders, conduct, inside, robin_pair)
    leftover = misfit(solution_now, right_side, conduct, conduct_sum, borders)
    return (solution_now.astype(jnp.bfloat16), leftover.astype(jnp.bfloat16))


def solution(mesh):
    placed = (
        P("wide", "narrow", None),
        P("wide", "narrow", None),
        P(),
        P(),
        P("wide", "narrow", None),
        P(("wide", "narrow"), None),
    )
    return jax.shard_map(
        body,
        mesh=mesh,
        in_specs=placed,
        out_specs=(P("wide", "narrow", None), P("wide", "narrow", None)),
        check_vma=False,
    )
```

profile of v0, /device:TPU:31, one launch (start us, length us, event | category | flops | bytes accessed | tf_op | source)
XLA Modules:
  0.0 420.9 jit_solution(12907860764941592942)
XLA Ops:
  1.4 1.3 collective-permute-start.3
  2.7 4.2 collective-permute-start
  7.6 2.9 collective-permute-start.2
  10.5 15.5 %collective-permute-start.1 = (s32[1,2,16]{2,1,0:T(2,128)S(1)}, s32[1,2,16]{2,1,0:T(2,128)S(1)}, u32[]{:S(2)}, u32[]{:S(2)}) collective-permute-start(s32[1,2,16]{2,1,0:T(2,128)S(1)} %get-tuple-element.159), channel_id=1, source_target_pairs={{0,8},{8,16},{16,24},{24,32},{32,40},{40,48},{48,56},{56,64},{64,7... | collective-permute-start | bytes 392 | tf_op jit(solution)/shard_map/ppermute | solution.py:22
  30.9 3.8 add_multiply_fusion.1
  41.7 9.0 %collective-permute-start.4 = (f32[1,16,128]{2,1,0:T(8,128)S(1)}, f32[1,16,128]{2,1,0:T(8,128)S(1)}, u32[]{:S(2)}, u32[]{:S(2)}) collective-permute-start(f32[1,16,128]{2,1,0:T(8,128)S(1)} %get-tuple-element.100), channel_id=1, source_target_pairs={{0,8},{8,16},{16,24},{24,32},{32,40},{40,48},{48,56},{56,64},{64,7... | collective-permute-start | bytes 24584 | tf_op jit(solution)/shard_map/ppermute | solution.py:22
  50.8 1.9 collective-permute-start.5
  52.7 3.5 collective-permute-start.6
  56.3 1.3 collective-permute-start.7
  57.6 11.1 %collective-permute-done.5 = f32[1,16,128]{2,1,0:T(8,128)S(1)} collective-permute-done((f32[1,16,128]{2,1,0:T(8,128)S(1)}, f32[1,16,128]{2,1,0:T(8,128)S(1)}, u32[]{:S(2)}, u32[]{:S(2)}) %collective-permute-start.5) | collective-permute-done | bytes 8224 | tf_op jit(solution)/shard_map/ppermute | solution.py:23
  69.7 2.7 maximum_dynamic-update-slice_fusion
  72.4 102.1 %all-reduce.104 = f32[2048]{0:T(1024)S(1)} all-reduce(f32[2048]{0:T(1024)S(1)} %maximum_dynamic-update-slice_fusion), channel_id=2, replica_groups=mesh['wide'=64,'narrow'=8] {'wide','narrow'}, use_global_device_ids=true, to_apply=%add.104 | all-reduce | flops 2048 | bytes 16384
  176.8 1.9 collective-permute-start.8
  178.7 16.1 %collective-permute-done.8 = f32[1]{0:T(128)} collective-permute-done((f32[1]{0:T(128)}, f32[1]{0:T(128)}, u32[]{:S(2)}, u32[]{:S(2)}) %collective-permute-start.8) | collective-permute-done | bytes 36 | tf_op jit(solution)/shard_map/ppermute | solution.py:37
  194.7 1.3 pad_maximum_fusion
  196.0 1.3 collective-permute-start.9
  197.3 3.0 collective-permute-done.9
  200.9 1.3 maximum_bitcast_fusion.1
  202.9 1.3 maximum_bitcast_fusion
  204.8 2.6 fusion.30
  207.6 2.5 collective-permute-start.12
  210.2 3.3 collective-permute-start.10
  213.5 1.3 fusion.49
  214.8 1.3 collective-permute-start.13
  216.1 1.2 fusion.48
  217.3 1.9 collective-permute-start.11
  219.3 1.4 fusion.50
  220.6 14.6 %collective-permute-done.11 = f32[1,16,128]{2,1,0:T(8,128)S(1)} collective-permute-done((f32[1,16,128]{2,1,0:T(8,128)S(1)}, f32[1,16,128]{2,1,0:T(8,128)S(1)}, u32[]{:S(2)}, u32[]{:S(2)}) %collective-permute-start.11) | collective-permute-done | bytes 8224 | tf_op jit(solution)/shard_map/ppermute | solution.py:23
  239.8 2.0 collective-permute-start.14
  241.8 2.3 collective-permute-start.15
  244.1 4.0 collective-permute-start.16
  248.1 1.3 collective-permute-start.17
  249.4 10.2 %collective-permute-done.15 = f32[1,16,128]{2,1,0:T(8,128)S(1)} collective-permute-done((f32[1,16,128]{2,1,0:T(8,128)S(1)}, f32[1,16,128]{2,1,0:T(8,128)S(1)}, u32[]{:S(2)}, u32[]{:S(2)}) %collective-permute-start.15) | collective-permute-done | bytes 8224 | tf_op jit(solution)/shard_map/ppermute | solution.py:23
  260.7 2.7 maximum_dynamic-update-slice_fusion.1
  263.4 101.7 %all-reduce.105 = f32[2048]{0:T(1024)S(1)} all-reduce(f32[2048]{0:T(1024)S(1)} %maximum_dynamic-update-slice_fusion.1), channel_id=3, replica_groups=mesh['wide'=64,'narrow'=8] {'wide','narrow'}, use_global_device_ids=true, to_apply=%add.105 | all-reduce | flops 2048 | bytes 16384
  367.4 1.9 collective-permute-start.18
  369.3 16.0 %collective-permute-done.18 = f32[1]{0:T(128)} collective-permute-done((f32[1]{0:T(128)}, f32[1]{0:T(128)}, u32[]{:S(2)}, u32[]{:S(2)}) %collective-permute-start.18) | collective-permute-done | bytes 36 | tf_op jit(solution)/shard_map/ppermute | solution.py:37
  385.3 1.4 pad_maximum_fusion.1
  386.6 1.3 collective-permute-start.19
  387.9 3.0 collective-permute-done.19
  391.6 1.3 maximum_bitcast_fusion.3
  393.5 1.4 maximum_bitcast_fusion.2
  395.5 2.6 fusion.34
  399.0 3.2 collective-permute-start.20
  402.2 1.9 collective-permute-start.21
  404.1 2.2 collective-permute-start.22
  406.3 1.3 collective-permute-start.23
  407.7 12.4 %collective-permute-done.21 = f32[1,16,128]{2,1,0:T(8,128)S(1)} collective-permute-done((f32[1,16,128]{2,1,0:T(8,128)S(1)}, f32[1,16,128]{2,1,0:T(8,128)S(1)}, u32[]{:S(2)}, u32[]{:S(2)}) %collective-permute-start.21) | collective-permute-done | bytes 8224 | tf_op jit(solution)/shard_map/ppermute | solution.py:23
  (168 shorter events, 26.8 us)
Async XLA Ops:
  1.4 33.4 %collective-permute-start.3 = (s32[2,1,16]{2,1,0:T(1,128)S(1)}, s32[2,1,16]{2,1,0:T(1,128)S(1)}, u32[]{:S(2)}, u32[]{:S(2)}) collective-permute-start(s32[2,1,16]{2,1,0:T(1,128)S(1)} %get-tuple-element.162), channel_id=1, source_target_pairs={{1,0},{2,1},{3,2},{4,3},{5,4},{6,5},{7,6},{9,8},{10,9},{11,10},{12... | collective-permute-start | bytes 392 | tf_op jit(solution)/shard_map/ppermute | solution.py:23
  2.7 32.1 %collective-permute-start = (s32[2,1,16]{2,1,0:T(1,128)S(1)}, s32[2,1,16]{2,1,0:T(1,128)S(1)}, u32[]{:S(2)}, u32[]{:S(2)}) collective-permute-start(s32[2,1,16]{2,1,0:T(1,128)S(1)} %get-tuple-element.161), channel_id=1, source_target_pairs={{0,1},{1,2},{2,3},{3,4},{4,5},{5,6},{6,7},{8,9},{9,10},{10,11},{11... | collective-permute-start | bytes 392 | tf_op jit(solution)/shard_map/ppermute | solution.py:22
  7.6 27.2 %collective-permute-start.2 = (s32[1,2,16]{2,1,0:T(2,128)S(1)}, s32[1,2,16]{2,1,0:T(2,128)S(1)}, u32[]{:S(2)}, u32[]{:S(2)}) collective-permute-start(s32[1,2,16]{2,1,0:T(2,128)S(1)} %get-tuple-element.160), channel_id=1, source_target_pairs={{8,0},{16,8},{24,16},{32,24},{40,32},{48,40},{56,48},{64,56},{72,6... | collective-permute-start | bytes 392 | tf_op jit(solution)/shard_map/ppermute | solution.py:23
  10.5 24.3 %collective-permute-start.1 = (s32[1,2,16]{2,1,0:T(2,128)S(1)}, s32[1,2,16]{2,1,0:T(2,128)S(1)}, u32[]{:S(2)}, u32[]{:S(2)}) collective-permute-start(s32[1,2,16]{2,1,0:T(2,128)S(1)} %get-tuple-element.159), channel_id=1, source_target_pairs={{0,8},{8,16},{16,24},{24,32},{32,40},{40,48},{48,56},{56,64},{64,7... | collective-permute-start | bytes 392 | tf_op jit(solution)/shard_map/ppermute | solution.py:22
  37.7 1.1 copy-start
  41.7 15.9 %collective-permute-start.4 = (f32[1,16,128]{2,1,0:T(8,128)S(1)}, f32[1,16,128]{2,1,0:T(8,128)S(1)}, u32[]{:S(2)}, u32[]{:S(2)}) collective-permute-start(f32[1,16,128]{2,1,0:T(8,128)S(1)} %get-tuple-element.100), channel_id=1, source_target_pairs={{0,8},{8,16},{16,24},{24,32},{32,40},{40,48},{48,56},{56,64},{64,7... | collective-permute-start | bytes 24584 | tf_op jit(solution)/shard_map/ppermute | solution.py:22
  50.8 17.9 %collective-permute-start.5 = (f32[1,16,128]{2,1,0:T(8,128)S(1)}, f32[1,16,128]{2,1,0:T(8,128)S(1)}, u32[]{:S(2)}, u32[]{:S(2)}) collective-permute-start(f32[1,16,128]{2,1,0:T(8,128)S(1)} %get-tuple-element.99), channel_id=1, source_target_pairs={{8,0},{16,8},{24,16},{32,24},{40,32},{48,40},{56,48},{64,56},{72,6... | collective-permute-start | bytes 24584 | tf_op jit(solution)/shard_map/ppermute | solution.py:23
  52.7 16.0 %collective-permute-start.6 = (f32[16,1,128]{2,1,0:T(1,128)S(1)}, f32[16,1,128]{2,1,0:T(1,128)S(1)}, u32[]{:S(2)}, u32[]{:S(2)}) collective-permute-start(f32[16,1,128]{2,1,0:T(1,128)S(1)} %get-tuple-element.96), channel_id=1, source_target_pairs={{0,1},{1,2},{2,3},{3,4},{4,5},{5,6},{6,7},{8,9},{9,10},{10,11},{11... | collective-permute-start | bytes 24584 | tf_op jit(solution)/shard_map/ppermute | solution.py:22
  56.3 12.4 %collective-permute-start.7 = (f32[16,1,128]{2,1,0:T(1,128)S(1)}, f32[16,1,128]{2,1,0:T(1,128)S(1)}, u32[]{:S(2)}, u32[]{:S(2)}) collective-permute-start(f32[16,1,128]{2,1,0:T(1,128)S(1)} %get-tuple-element.95), channel_id=1, source_target_pairs={{1,0},{2,1},{3,2},{4,3},{5,4},{6,5},{7,6},{9,8},{10,9},{11,10},{12... | collective-permute-start | bytes 24584 | tf_op jit(solution)/shard_map/ppermute | solution.py:23
  68.7 107.4 %copy-start.1 = (f32[1,512]{1,0:T(1,128)S(1)}, f32[1,512]{1,0:T(1,128)}, u32[]{:S(2)}) copy-start(f32[1,512]{1,0:T(1,128)} %param.11) | copy-start | bytes 6148
  176.8 18.0 %collective-permute-start.8 = (f32[1]{0:T(128)}, f32[1]{0:T(128)}, u32[]{:S(2)}, u32[]{:S(2)}) collective-permute-start(f32[1]{0:T(128)} %bitcast.26), channel_id=1, source_target_pairs={{8,0},{16,8},{24,16},{32,24},{40,32},{48,40},{56,48},{64,56},{72,6... | collective-permute-start | bytes 20 | tf_op jit(solution)/shard_map/ppermute | solution.py:37
  196.0 4.3 %collective-permute-start.9 = (f32[2]{0:T(128)S(1)}, f32[2]{0:T(128)S(1)}, u32[]{:S(2)}, u32[]{:S(2)}) collective-permute-start(f32[2]{0:T(128)S(1)} %pad_maximum_fusion), channel_id=1, source_target_pairs={{1,0},{2,1},{3,2},{4,3},{5,4},{6,5},{7,6},{9,8},{10,9},{11,10},{12... | collective-permute-start | bytes 32 | tf_op jit(solution)/shard_map/ppermute | solution.py:37
  207.6 5.9 %collective-permute-start.12 = (f32[16,1,128]{2,1,0:T(1,128)S(1)}, f32[16,1,128]{2,1,0:T(1,128)S(1)}, u32[]{:S(2)}, u32[]{:S(2)}) collective-permute-start(f32[16,1,128]{2,1,0:T(1,128)S(1)} %slice.802), channel_id=1, source_target_pairs={{0,1},{1,2},{2,3},{3,4},{4,5},{5,6},{6,7},{8,9},{9,10},{10,11},{11... | collective-permute-start | bytes 24584 | tf_op jit(solution)/shard_map/ppermute | solution.py:22
  210.2 5.9 %collective-permute-start.10 = (f32[1,16,128]{2,1,0:T(8,128)S(1)}, f32[1,16,128]{2,1,0:T(8,128)S(1)}, u32[]{:S(2)}, u32[]{:S(2)}) collective-permute-start(f32[1,16,128]{2,1,0:T(8,128)S(1)} %slice.798), channel_id=1, source_target_pairs={{0,8},{8,16},{16,24},{24,32},{32,40},{40,48},{48,56},{56,64},{64,7... | collective-permute-start | bytes 24584 | tf_op jit(solution)/shard_map/ppermute | solution.py:22
  214.8 4.5 %collective-permute-start.13 = (f32[16,1,128]{2,1,0:T(1,128)S(1)}, f32[16,1,128]{2,1,0:T(1,128)S(1)}, u32[]{:S(2)}, u32[]{:S(2)}) collective-permute-start(f32[16,1,128]{2,1,0:T(1,128)S(1)} %get-tuple-element.84), channel_id=1, source_target_pairs={{1,0},{2,1},{3,2},{4,3},{5,4},{6,5},{7,6},{9,8},{10,9},{11,10},{12... | collective-permute-start | bytes 24584 | tf_op jit(solution)/shard_map/ppermute | solution.py:23
  217.3 17.9 %collective-permute-start.11 = (f32[1,16,128]{2,1,0:T(8,128)S(1)}, f32[1,16,128]{2,1,0:T(8,128)S(1)}, u32[]{:S(2)}, u32[]{:S(2)}) collective-permute-start(f32[1,16,128]{2,1,0:T(8,128)S(1)} %get-tuple-element.82), channel_id=1, source_target_pairs={{8,0},{16,8},{24,16},{32,24},{40,32},{48,40},{56,48},{64,56},{72,6... | collective-permute-start | bytes 24584 | tf_op jit(solution)/shard_map/ppermute | solution.py:23
  239.8 9.7 %collective-permute-start.14 = (f32[1,16,128]{2,1,0:T(8,128)S(1)}, f32[1,16,128]{2,1,0:T(8,128)S(1)}, u32[]{:S(2)}, u32[]{:S(2)}) collective-permute-start(f32[1,16,128]{2,1,0:T(8,128)S(1)} %get-tuple-element.38), channel_id=1, source_target_pairs={{0,8},{8,16},{16,24},{24,32},{32,40},{40,48},{48,56},{56,64},{64,7... | collective-permute-start | bytes 24584 | tf_op jit(solution)/shard_map/ppermute | solution.py:22
  241.8 17.9 %collective-permute-start.15 = (f32[1,16,128]{2,1,0:T(8,128)S(1)}, f32[1,16,128]{2,1,0:T(8,128)S(1)}, u32[]{:S(2)}, u32[]{:S(2)}) collective-permute-start(f32[1,16,128]{2,1,0:T(8,128)S(1)} %get-tuple-element.37), channel_id=1, source_target_pairs={{8,0},{16,8},{24,16},{32,24},{40,32},{48,40},{56,48},{64,56},{72,6... | collective-permute-start | bytes 24584 | tf_op jit(solution)/shard_map/ppermute | solution.py:23
  244.1 15.5 %collective-permute-start.16 = (f32[16,1,128]{2,1,0:T(1,128)S(1)}, f32[16,1,128]{2,1,0:T(1,128)S(1)}, u32[]{:S(2)}, u32[]{:S(2)}) collective-permute-start(f32[16,1,128]{2,1,0:T(1,128)S(1)} %get-tuple-element.34), channel_id=1, source_target_pairs={{0,1},{1,2},{2,3},{3,4},{4,5},{5,6},{6,7},{8,9},{9,10},{10,11},{11... | collective-permute-start | bytes 24584 | tf_op jit(solution)/shard_map/ppermute | solution.py:22
  248.1 11.6 %collective-permute-start.17 = (f32[16,1,128]{2,1,0:T(1,128)S(1)}, f32[16,1,128]{2,1,0:T(1,128)S(1)}, u32[]{:S(2)}, u32[]{:S(2)}) collective-permute-start(f32[16,1,128]{2,1,0:T(1,128)S(1)} %get-tuple-element.33), channel_id=1, source_target_pairs={{1,0},{2,1},{3,2},{4,3},{5,4},{6,5},{7,6},{9,8},{10,9},{11,10},{12... | collective-permute-start | bytes 24584 | tf_op jit(solution)/shard_map/ppermute | solution.py:23
  367.4 17.9 %collective-permute-start.18 = (f32[1]{0:T(128)}, f32[1]{0:T(128)}, u32[]{:S(2)}, u32[]{:S(2)}) collective-permute-start(f32[1]{0:T(128)} %bitcast.45), channel_id=1, source_target_pairs={{8,0},{16,8},{24,16},{32,24},{40,32},{48,40},{56,48},{64,56},{72,6... | collective-permute-start | bytes 20 | tf_op jit(solution)/shard_map/ppermute | solution.py:37
  386.6 4.3 %collective-permute-start.19 = (f32[2]{0:T(128)S(1)}, f32[2]{0:T(128)S(1)}, u32[]{:S(2)}, u32[]{:S(2)}) collective-permute-start(f32[2]{0:T(128)S(1)} %pad_maximum_fusion.1), channel_id=1, source_target_pairs={{1,0},{2,1},{3,2},{4,3},{5,4},{6,5},{7,6},{9,8},{10,9},{11,10},{12... | collective-permute-start | bytes 32 | tf_op jit(solution)/shard_map/ppermute | solution.py:37
  399.0 8.6 %collective-permute-start.20 = (f32[1,16,128]{2,1,0:T(8,128)S(1)}, f32[1,16,128]{2,1,0:T(8,128)S(1)}, u32[]{:S(2)}, u32[]{:S(2)}) collective-permute-start(f32[1,16,128]{2,1,0:T(8,128)S(1)} %get-tuple-element.28), channel_id=1, source_target_pairs={{0,8},{8,16},{16,24},{24,32},{32,40},{40,48},{48,56},{56,64},{64,7... | collective-permute-start | bytes 24584 | tf_op jit(solution)/shard_map/ppermute | solution.py:22
  402.2 17.9 %collective-permute-start.21 = (f32[1,16,128]{2,1,0:T(8,128)S(1)}, f32[1,16,128]{2,1,0:T(8,128)S(1)}, u32[]{:S(2)}, u32[]{:S(2)}) collective-permute-start(f32[1,16,128]{2,1,0:T(8,128)S(1)} %get-tuple-element.27), channel_id=1, source_target_pairs={{8,0},{16,8},{24,16},{32,24},{40,32},{48,40},{56,48},{64,56},{72,6... | collective-permute-start | bytes 24584 | tf_op jit(solution)/shard_map/ppermute | solution.py:23
  404.1 16.0 %collective-permute-start.22 = (f32[16,1,128]{2,1,0:T(1,128)S(1)}, f32[16,1,128]{2,1,0:T(1,128)S(1)}, u32[]{:S(2)}, u32[]{:S(2)}) collective-permute-start(f32[16,1,128]{2,1,0:T(1,128)S(1)} %get-tuple-element.24), channel_id=1, source_target_pairs={{0,1},{1,2},{2,3},{3,4},{4,5},{5,6},{6,7},{8,9},{9,10},{10,11},{11... | collective-permute-start | bytes 24584 | tf_op jit(solution)/shard_map/ppermute | solution.py:22
  406.3 13.8 %collective-permute-start.23 = (f32[16,1,128]{2,1,0:T(1,128)S(1)}, f32[16,1,128]{2,1,0:T(1,128)S(1)}, u32[]{:S(2)}, u32[]{:S(2)}) collective-permute-start(f32[16,1,128]{2,1,0:T(1,128)S(1)} %get-tuple-element.23), channel_id=1, source_target_pairs={{1,0},{2,1},{3,2},{4,3},{5,4},{6,5},{7,6},{9,8},{10,9},{11,10},{12... | collective-permute-start | bytes 24584 | tf_op jit(solution)/shard_map/ppermute | solution.py:23
where the time goes:
time: 422 us; the launch traced here: 421 us
  blocking collectives  204 us (48%)
  waiting for transfers between devices  86.4 us (20%)
  starting transfers between devices  73.3 us (17%)
  other arithmetic  39 us (9%)
  local copies, waits for them, and re-layouts  14.1 us (3%)
  between operations  4.27 us (1%)
    unnamed x2, blocking collectives  204 us
    ppermute x10, starting transfers between devices, padded(): lax.ppermute(last, axis, up)  49.4 us
    ppermute x10, waiting for transfers between devices, padded(): lax.ppermute(first, axis, [(b, a) for a, b in up])  48.3 us
    ppermute x4, waiting for transfers between devices, shifted(): return lax.ppermute(array, axis, pairs)  38.1 us
    ppermute x10, starting transfers between devices, padded(): lax.ppermute(first, axis, [(b, a) for a, b in up])  17.5 us
  transfers between devices with their start and end apart: 24, of which 8 were waited for; matrix products, arithmetic and copies ran while one was open for 3% of the time, Pallas kernels for 0%

commit v1 on v0

--- a/solution.py
+++ b/solution.py
@@ -1,6 +1,7 @@
 import jax
 import jax.numpy as jnp
 from jax import lax
+from jax.sharding import Mesh
 from jax.sharding import PartitionSpec as P
 
 BLOCK = 8
@@ -9,32 +10,6 @@
 
 
 reaction = 1.0
-
-
-def padded(array, sides, width):
-    edges = {}
-    for axis, dim in sides:
-        peers, length = (lax.axis_size(axis), array.shape[dim])
-        up = [(i, (i + 1) % peers) for i in range(peers - 1)]
-        last = lax.slice_in_dim(array, length - width, length, axis=dim)
-        first = lax.slice_in_dim(array, 0, width, axis=dim)
-        edges[dim] = (
-            lax.ppermute(last, axis, up),
-            lax.ppermute(first, axis, [(b, a) for a, b in up]),
-        )
-    done = []
-    for _, dim in sides:
-        low, high = edges[dim]
-        around = [(width, width) if d in done else (0, 0) for d in range(array.ndim)]
-        array = jnp.concatenate([jnp.pad(low, around), array, jnp.pad(high, around)], axis=dim)
-        done.append(dim)
-    return array
-
-
-def shifted(array, axis, by):
-    peers = lax.axis_size(axis)
-    pairs = [(i, i + by) for i in range(peers) if 0 <= i + by < peers]
-    return lax.ppermute(array, axis, pairs)
 
 
 def spread_cells(blocks):
@@ -149,12 +124,6 @@
     )
 
 
-def restrict(leftover):
-    column_sum = jnp.sum(leftover, axis=2)
-    weights = coarse_weights(leftover.shape[0], leftover.shape[1])
-    return jnp.stack([jnp.sum(weights[corner] * column_sum) for corner in range(4)])
-
-
 def interpolate(corners, extent_x, extent_y):
     weights = coarse_weights(extent_x, extent_y)
     return (
@@ -174,94 +143,144 @@
     )
 
 
-def combine_partials(stacked):
-    from_west = jnp.pad(stacked[:-1, :, 1], ((1, 0), (0, 0)))
-    from_south = jnp.pad(stacked[:, :-1, 2], ((0, 0), (1, 0)))
-    from_corner = jnp.pad(stacked[:-1, :-1, 3], ((1, 0), (1, 0)))
-    return stacked[:, :, 0] + from_west + from_south + from_corner
-
-
 def table_lookup(keys, table):
     entries = jnp.arange(table.shape[0], dtype=jnp.int32)
     return jnp.sum(jnp.where(keys[..., None] == entries, table, 0.0), -1)
 
 
-def face_rows(widened):
-    return (widened[0, 1:-1], widened[-1, 1:-1], widened[1:-1, 0], widened[1:-1, -1])
+WIDE = ("half", "plane")
+NEAR = 1.0 / 32.0
+FAR = 31.0 / 32.0
+
+
+def neighbour_pairs(peers, by):
+    return [(i, i + by) for i in range(peers) if 0 <= i + by < peers]
+
+
+def exchange(west, east, south, north, wide_count, narrow_count):
+    return (
+        lax.ppermute(east, WIDE, neighbour_pairs(wide_count, 1)),
+        lax.ppermute(west, WIDE, neighbour_pairs(wide_count, -1)),
+        lax.ppermute(north, "narrow", neighbour_pairs(narrow_count, 1)),
+        lax.ppermute(south, "narrow", neighbour_pairs(narrow_count, -1)),
+    )
+
+
+def contributions(field_now, right_side, conduct, conduct_sum, inside):
+    blank_x = jnp.zeros_like(field_now[0])
+    blank_y = jnp.zeros_like(field_now[:, 0])
+    own = misfit(field_now, right_side, conduct, conduct_sum, (blank_x, blank_x, blank_y, blank_y))
+    ramp = (jnp.arange(16, dtype=jnp.float32) + 0.5) / 16
+    pair = jnp.stack([1.0 - ramp, ramp])
+    column_sum = jnp.sum(own, axis=2)
+    centre = jnp.sum(pair[:, None, :, None] * pair[None, :, None, :] * column_sum, axis=(2, 3))
+    west = inside[0] * jnp.sum(pair * jnp.sum(conduct[0][0] * field_now[0], -1), 1)
+    east = inside[1] * jnp.sum(pair * jnp.sum(conduct[1][-1] * field_now[-1], -1), 1)
+    south = inside[2] * jnp.sum(pair * jnp.sum(conduct[2][:, 0] * field_now[:, 0], -1), 1)
+    north = inside[3] * jnp.sum(pair * jnp.sum(conduct[3][:, -1] * field_now[:, -1], -1), 1)
+    centre = centre + FAR * (jnp.stack([west, east], 0) + jnp.stack([south, north], 1))
+    zero = jnp.zeros((1,), jnp.float32)
+    return jnp.concatenate(
+        [
+            zero, NEAR * west, zero,
+            NEAR * south[:1], centre[0], NEAR * north[:1],
+            NEAR * south[1:], centre[1], NEAR * north[1:],
+            zero, NEAR * east, zero,
+        ]
+    )
+
+
+def spread_rows(rows, wide_count, narrow_count, halves):
+    grid = jnp.pad(rows.reshape(4, wide_count, narrow_count), ((0, 0), (1, 2), (1, 2)))
+    moved = jnp.stack(
+        [grid[:, i : i + wide_count, j : j + narrow_count] for i in range(4) for j in range(4)], -1
+    )
+    moved = moved.reshape(4, halves, wide_count // halves, narrow_count, 16)
+    return moved.transpose(0, 1, 3, 2, 4).reshape(4, halves * narrow_count, -1)
+
+
+def gather_all(values, planes, columns):
+    first = lax.all_to_all(
+        jnp.broadcast_to(values[None], (planes, 16)), "plane", 0, 0, tiled=True
+    )
+    second = jnp.broadcast_to(first.reshape(1, planes * 16), (columns, planes * 16))
+    return lax.all_to_all(second, ("half", "narrow"), 0, 0, tiled=True)
 
 
 def body(right_side, labels, material_table, robin_table, robin_index, coarse_rows):
-    wide_at = lax.axis_index("wide")
+    wide_at = lax.axis_index(WIDE)
     narrow_at = lax.axis_index("narrow")
-    wide_count = lax.axis_size("wide")
+    halves = lax.axis_size("half")
+    planes = lax.axis_size("plane")
+    wide_count = halves * planes
     narrow_count = lax.axis_size("narrow")
     extent_x, extent_y = (right_side.shape[0], right_side.shape[1])
-    label_pad = padded(labels, (("wide", 0), ("narrow", 1)), 1)
-    kappa_pad = table_lookup(label_pad, material_table)
+    kappa_own = table_lookup(labels, material_table)
+    flat = lambda item: item.reshape(1, -1)
+    width = kappa_own[0].size
+    from_west = lax.ppermute(flat(kappa_own[-1]), WIDE, neighbour_pairs(wide_count, 1))
+    from_east = lax.ppermute(
+        jnp.concatenate([flat(kappa_own[0]), coarse_rows], 1), WIDE, neighbour_pairs(wide_count, -1)
+    )
+    from_south = lax.ppermute(flat(kappa_own[:, -1]), "narrow", neighbour_pairs(narrow_count, 1))
+    row_pair = jnp.concatenate([coarse_rows, from_east[:, width:]], 1)
+    from_north = lax.ppermute(
+        jnp.concatenate([flat(kappa_own[:, 0]), row_pair], 1),
+        "narrow",
+        neighbour_pairs(narrow_count, -1),
+    )
+    rows = jnp.concatenate([row_pair, from_north[:, width:]], 1)
+    spread = spread_rows(rows, wide_count, narrow_count, halves)
     inside = jnp.stack(
         [wide_at > 0, wide_at < wide_count - 1, narrow_at > 0, narrow_at < narrow_count - 1]
     ).astype(jnp.float32)
     robin_pair = table_lookup(robin_index[0, 0], robin_table)
     material = (
-        kappa_pad[1:-1, 1:-1],
-        kappa_pad[0, 1:-1],
-        kappa_pad[-1, 1:-1],
-        kappa_pad[1:-1, 0],
-        kappa_pad[1:-1, -1],
+        kappa_own,
+        from_west.reshape(kappa_own[0].shape),
+        from_east[:, :width].reshape(kappa_own[0].shape),
+        from_south.reshape(kappa_own[:, 0].shape),
+        from_north[:, :width].reshape(kappa_own[:, 0].shape),
         inside,
         robin_pair,
     )
     conduct, conduct_sum, robin_term, parity = assemble_local(material)
     diagonal = reaction + conduct_sum + robin_term
     solution_now = jnp.zeros_like(right_side)
-    traces = (
-        jnp.zeros_like(right_side[0]),
-        jnp.zeros_like(right_side[0]),
-        jnp.zeros_like(right_side[:, 0]),
-        jnp.zeros_like(right_side[:, 0]),
-    )
+    source = right_side
     for outer in range(ITERS):
-        source = right_side + robin_source(traces, right_side.shape)
         solution_now = relax(solution_now, source, conduct, diagonal, parity)
-        widened = padded(solution_now, (("wide", 0), ("narrow", 1)), 1)
-        borders = face_rows(widened)
-        partial_value = restrict(misfit(solution_now, right_side, conduct, conduct_sum, borders))
-        every = lax.all_gather(partial_value[None], ("wide", "narrow"), axis=0, tiled=True)
-        coarse_vec = combine_partials(every.reshape(wide_count, narrow_count, 4)).reshape(-1)
-        coarse_own = jnp.dot(
-            coarse_rows,
-            coarse_vec,
-            precision=lax.Precision.HIGHEST,
-            preferred_element_type=jnp.float32,
+        every = gather_all(
+            contributions(solution_now, right_side, conduct, conduct_sum, inside),
+            planes,
+            halves * narrow_count,
         )
-        east_value = shifted(coarse_own, "wide", -1)
-        column_pair = jnp.stack([coarse_own[0], east_value[0]])
-        north_pair = shifted(column_pair, "narrow", -1)
-        corners = jnp.stack(
-            [jnp.stack([column_pair[0], north_pair[0]]), jnp.stack([column_pair[1], north_pair[1]])]
+        corners = jnp.sum(spread * every, axis=(1, 2)).reshape(2, 2).T
+        solution_now = solution_now + interpolate(corners, extent_x, extent_y)[:, :, None]
+        borders = exchange(
+            solution_now[0], solution_now[-1], solution_now[:, 0], solution_now[:, -1], wide_count, narrow_count
         )
-        solution_now = solution_now + interpolate(corners, extent_x, extent_y)[:, :, None]
-        widened = padded(solution_now, (("wide", 0), ("narrow", 1)), 1)
-        borders = face_rows(widened)
         if outer + 1 < ITERS:
             traces = robin_traces(solution_now, borders, conduct, inside, robin_pair)
+            source = right_side + robin_source(traces, right_side.shape)
     leftover = misfit(solution_now, right_side, conduct, conduct_sum, borders)
     return (solution_now.astype(jnp.bfloat16), leftover.astype(jnp.bfloat16))
 
 
 def solution(mesh):
+    split = Mesh(mesh.devices.reshape(2, mesh.devices.shape[0] // 2, -1), ("half", "plane", "narrow"))
     placed = (
-        P("wide", "narrow", None),
-        P("wide", "narrow", None),
+        P(WIDE, "narrow", None),
+        P(WIDE, "narrow", None),
         P(),
         P(),
-        P("wide", "narrow", None),
-        P(("wide", "narrow"), None),
+        P(WIDE, "narrow", None),
+        P(("half", "plane", "narrow"), None),
     )
     return jax.shard_map(
         body,
-        mesh=mesh,
+        mesh=split,
         in_specs=placed,
-        out_specs=(P("wide", "narrow", None), P("wide", "narrow", None)),
+        out_specs=(P(WIDE, "narrow", None), P(WIDE, "narrow", None)),
         check_vma=False,
     )

time: 422 us -> 208 us (0.49)
  blocking collectives: 204 us -> 35.2 us
  waiting for transfers between devices: 86.4 us -> 24.7 us
  between operations: 4.27 us -> 9.69 us
  local copies, waits for them, and re-layouts: 14.1 us -> 19 us
  starting transfers between devices: 73.3 us -> 77.6 us
    unnamed x2 -> x0, blocking collectives: 204 us -> none
    ppermute x24 -> x12, waiting for transfers between devices: 86.4 us -> 14.5 us  [the longest x2 11.5 us: exchange(): lax.ppermute(west, WIDE, neighbour_pairs(wide_count, -1))]
    all_to_all x0 -> x2, blocking collectives: none -> 35.2 us  [the longest x1 25.1 us: gather_all(): return lax.all_to_all(second, ('half', 'narrow'), 0, 0, tiled=True)]
    all_to_all x0 -> x2, starting transfers between devices: none -> 17.5 us  [the longest x1 10.9 us: gather_all(): return lax.all_to_all(second, ('half', 'narrow'), 0, 0, tiled=True)]
    ppermute x24 -> x12, starting transfers between devices: 73.3 us -> 60.2 us  [the longest x2 22.7 us: exchange(): lax.ppermute(east, WIDE, neighbour_pairs(wide_count, 1))]
    all_to_all x0 -> x2, waiting for transfers between devices: none -> 10.2 us  [the longest x1 7.93 us: gather_all(): return lax.all_to_all(second, ('half', 'narrow'), 0, 0, tiled=True)]
    another operation x6 -> x0, other arithmetic: 8 us -> none  [the longest x4 5.34 us: body(): jnp.stack([jnp.stack([column_pair[0], north_pair[0]]), jnp.stack([column_...]
    mul x3 -> x16, other arithmetic: 3.78 us -> 10.3 us  [the longest x4 2.71 us: contributions(): inside[2]]
  transfers between devices with their start and end apart: 24 -> 14, of which waited for: 8 -> 4; matrix products, arithmetic and copies ran while one was open for 3% -> 9% of each run, Pallas kernels for 0% -> 0%
where the time goes in v1:
time: 208 us; the launch traced here: 206 us
  starting transfers between devices  77.6 us (37%)
  other arithmetic  40.2 us (19%)
  blocking collectives  35.2 us (17%)
  waiting for transfers between devices  24.7 us (12%)
  local copies, waits for them, and re-layouts  19 us (9%)
  between operations  9.69 us (5%)
    all_to_all x1, blocking collectives, gather_all(): return lax.all_to_all(second, ('half', 'narrow'), 0, 0, tiled=True)  25.1 us
    ppermute x2, starting transfers between devices, exchange(): lax.ppermute(east, WIDE, neighbour_pairs(wide_count, 1))  22.7 us
    ppermute x1, starting transfers between devices, body(): lax.ppermute(flat(kappa_own[-1]), WIDE, neighbour_pairs(wide_count, 1))  16.2 us
    ppermute x2, waiting for transfers between devices, exchange(): lax.ppermute(west, WIDE, neighbour_pairs(wide_count, -1))  11.5 us
    all_to_all x1, starting transfers between devices, gather_all(): return lax.all_to_all(second, ('half', 'narrow'), 0, 0, tiled=True)  10.9 us
    all_to_all x1, blocking collectives, gather_all(): lax.all_to_all(jnp.broadcast_to(values[None], (planes, 16)), 'plane', 0,...  10.1 us
    all_to_all x1, waiting for transfers between devices, gather_all(): return lax.all_to_all(second, ('half', 'narrow'), 0, 0, tiled=True)  7.93 us
    all_to_all x1, starting transfers between devices, gather_all(): lax.all_to_all(jnp.broadcast_to(values[None], (planes, 16)), 'plane', 0,...  6.59 us
  transfers between devices with their start and end apart: 14, of which 4 were waited for; matrix products, arithmetic and copies ran while one was open for 9% of the time, Pallas kernels for 0%

profile of v1, /device:TPU:31, one launch (start us, length us, event | category | flops | bytes accessed | tf_op | source)
XLA Modules:
  0.0 206.4 jit_solution(13231666077962754350)
XLA Ops:
  0.6 0.9 select_reduce_fusion
  1.6 0.8 pad_maximum_fusion.1
  2.3 2.6 %collective-permute-start.1 = (f32[1,544]{1,0:T(1,128)S(1)}, f32[1,544]{1,0:T(1,128)S(1)}, u32[]{:S(2)}, u32[]{:S(2)}) collective-permute-start(f32[1,544]{1,0:T(1,128)S(1)} %pad_maximum_fusion.1), channel_id=1, source_target_pairs={{8,0},{16,8},{24,16},{32,24},{40,32},{48,40},{56,48},{64,56},{72,6... | collective-permute-start | bytes 6536 | tf_op jit(solution)/shard_map/ppermute | solution.py:222
  5.0 3.5 %collective-permute-start.2 = (f32[1,32]{1,0:T(1,128)S(1)}, f32[1,32]{1,0:T(1,128)S(1)}, u32[]{:S(2)}, u32[]{:S(2)}) collective-permute-start(f32[1,32]{1,0:T(1,128)S(1)} %reshape_squeeze.14), channel_id=1, source_target_pairs={{0,1},{1,2},{2,3},{3,4},{4,5},{5,6},{6,7},{8,9},{9,10},{10,11},{11... | collective-permute-start | bytes 392 | tf_op jit(solution)/shard_map/ppermute | solution.py:225
  8.6 16.2 %collective-permute-start = (f32[1,32]{1,0:T(1,128)S(1)}, f32[1,32]{1,0:T(1,128)S(1)}, u32[]{:S(2)}, u32[]{:S(2)}) collective-permute-start(f32[1,32]{1,0:T(1,128)S(1)} %reshape_squeeze.12), channel_id=1, source_target_pairs={{0,8},{8,16},{16,24},{24,32},{32,40},{40,48},{48,56},{56,64},{64,7... | collective-permute-start | bytes 392 | tf_op jit(solution)/shard_map/ppermute | solution.py:221
  25.1 1.0 reshape.502
  26.9 0.7 fusion.18
  27.6 0.7 fusion.112
  29.1 3.7 %add_multiply_fusion.6 = (f32[16]{0:T(128)S(1)}, f32[16]{0:T(128)S(1)}) fusion(f32[]{:T(128)} %bitcast.10, f32[]{:T(128)} %bitcast.9, f32[]{:T(128)} %bitcast.13, f32[]{:T(128)} %bitcast.7, f32[]{:T(128)} %bitcast.4, f32[]{:T(128)} %bitcast.12), kind=kLoop, calls=%fused_computation.164 | loop fusion | flops 160 | bytes 152 | tf_op jit(solution)/shard_map/mul | solution.py:76
  38.2 1.3 collective-permute-start.3
  39.9 2.9 %collective-permute-done.3 = f32[1,1056]{1,0:T(1,128)S(1)} collective-permute-done((f32[1,1056]{1,0:T(1,128)S(1)}, f32[1,1056]{1,0:T(1,128)S(1)}, u32[]{:S(2)}, u32[]{:S(2)}) %collective-permute-start.3) | collective-permute-done | bytes 4256 | tf_op jit(solution)/shard_map/ppermute | solution.py:227
  47.5 0.6 copy-done.1
  48.6 0.7 broadcast_multiply_fusion.8
  49.3 0.7 fusion.115
  52.5 0.6 multiply_multiply_fusion.12
  53.6 0.7 fusion.109
  57.6 6.6 %all-to-all-start = ((f32[32,1,16]{2,1,0:T(1,128)}), f32[32,1,16]{2,1,0:T(1,128)S(1)}, u32[]{:S(2)}, u32[]{:S(2)}) async-start(f32[32,1,16]{2,1,0:T(1,128)} %broadcast_in_dim.67), calls=%async_computation | async-start | bytes 32768 | tf_op jit(solution)/shard_map/all_to_all | solution.py:203
  64.2 1.2 fusion.43
  65.5 2.3 %all-to-all-done = f32[32,1,16]{2,1,0:T(1,128)S(1)} async-done(((f32[32,1,16]{2,1,0:T(1,128)}), f32[32,1,16]{2,1,0:T(1,128)S(1)}, u32[]{:S(2)}, u32[]{:S(2)}) %all-to-all-start) | async-done | bytes 2080 | tf_op jit(solution)/shard_map/all_to_all | solution.py:203
  69.1 10.9 %all-to-all-start.1 = ((f32[16,1,512]{2,1,0:T(1,128)}), f32[16,1,512]{2,1,0:T(1,128)}, u32[]{:S(2)}, u32[]{:S(2)}) async-start(f32[16,1,512]{2,1,0:T(1,128)} %broadcast_in_dim.69), calls=%async_computation.1 | async-start | bytes 65536 | tf_op jit(solution)/shard_map/all_to_all | solution.py:207
  81.0 0.8 stack.104
  82.8 0.8 stack.115
  83.6 7.9 %all-to-all-done.1 = f32[16,1,512]{2,1,0:T(1,128)} async-done(((f32[16,1,512]{2,1,0:T(1,128)}), f32[16,1,512]{2,1,0:T(1,128)}, u32[]{:S(2)}, u32[]{:S(2)}) %all-to-all-start.1) | async-done | bytes 32800 | tf_op jit(solution)/shard_map/all_to_all | solution.py:207
  91.5 0.8 reduce.11
  92.9 0.7 fusion.106
  93.5 2.6 %fusion.23 = f32[16,16]{0,1:T(8,128)S(1)} fusion(f32[]{:T(128)} %bitcast.47, f32[16]{0:T(128)S(1)} %copy-done.11, f32[]{:T(128)} %bitcast.46, f32[]{:T(128)} %bitcast.45, f32[16]{0:T(128)S(1)} %copy-done.12, f32[]{:T(128)} %bitcast.44), kind=kLoop, calls=%fused_computation.101 | loop fusion | flops 2816 | bytes 1168 | tf_op jit(solution)/shard_map/add | solution.py:130
  96.5 3.9 %collective-permute-start.5 = (f32[16,128]{1,0:T(8,128)S(1)}, f32[16,128]{1,0:T(8,128)S(1)}, u32[]{:S(2)}, u32[]{:S(2)}) collective-permute-start(f32[16,128]{1,0:T(8,128)S(1)} %bitcast.196), channel_id=1, source_target_pairs={{8,0},{16,8},{24,16},{32,24},{40,32},{48,40},{56,48},{64,56},{72,6... | collective-permute-start | bytes 24584 | tf_op jit(solution)/shard_map/ppermute | solution.py:163
  100.4 2.4 %collective-permute-start.6 = (f32[16,128]{1,0:T(8,128)S(1)}, f32[16,128]{1,0:T(8,128)S(1)}, u32[]{:S(2)}, u32[]{:S(2)}) collective-permute-start(f32[16,128]{1,0:T(8,128)S(1)} %get-tuple-element.91), channel_id=1, source_target_pairs={{0,1},{1,2},{2,3},{3,4},{4,5},{5,6},{6,7},{8,9},{9,10},{10,11},{11... | collective-permute-start | bytes 24584 | tf_op jit(solution)/shard_map/ppermute | solution.py:164
  102.9 1.3 collective-permute-start.7
  104.2 15.0 %collective-permute-start.4 = (f32[16,128]{1,0:T(8,128)S(1)}, f32[16,128]{1,0:T(8,128)S(1)}, u32[]{:S(2)}, u32[]{:S(2)}) collective-permute-start(f32[16,128]{1,0:T(8,128)S(1)} %bitcast.198), channel_id=1, source_target_pairs={{0,8},{8,16},{16,24},{24,32},{32,40},{40,48},{48,56},{56,64},{64,7... | collective-permute-start | bytes 24584 | tf_op jit(solution)/shard_map/ppermute | solution.py:162
  119.2 1.2 add_multiply_fusion.2
  120.4 1.2 add_multiply_fusion.3
  121.6 2.6 %add_multiply_fusion.1 = (f32[16,128]{1,0:T(8,128)S(1)}, f32[16,128]{1,0:T(8,128)S(1)}) fusion(f32[16,128]{1,0:T(8,128)S(1)} %collective-permute-done.6, f32[16,16,128]{2,0,1:T(8,128)S(1)} %get-tuple-element.21, f32[]{:T(128)} %bitcast.13, f32[]{:T(128)} %bitcast.9, f32[16,16,128]{2,0,1:T(8,128)S(1)} %broadcast_add_fusion.1, ...), kind=kLoop, calls=%fused_computation.129 | loop fusion | flops 16384 | bytes 65548 | tf_op jit(solution)/shard_map/mul | solution.py:141
  128.9 0.8 multiply_reduce_fusion
  130.0 0.7 broadcast_multiply_fusion.7
  130.7 0.7 fusion.113
  135.4 0.6 multiply_multiply_fusion.10
  139.0 10.1 %all_to_all.24 = f32[32,1,16]{2,1,0:T(1,128)S(1)} all-to-all(f32[32,1,16]{2,1,0:T(1,128)S(1)} %broadcast_in_dim.70), channel_id=1, replica_groups=mesh['half'=2,'plane'=32,'narrow'=8] {'plane'}, dimensions={0} | all-to-all | bytes 4096 | tf_op jit(solution)/shard_map/all_to_all | solution.py:203
  149.8 25.1 %all_to_all.25 = f32[16,1,512]{2,1,0:T(1,128)S(1)} all-to-all(f32[16,1,512]{2,1,0:T(1,128)S(1)} %broadcast_in_dim.72), channel_id=1, replica_groups=mesh['half'=2,'plane'=32,'narrow'=8] {'half','narrow'}, dimensions={0} | all-to-all | bytes 65536 | tf_op jit(solution)/shard_map/all_to_all | solution.py:207
  175.5 0.7 fusion.105
  176.2 2.6 %fusion.26 = f32[16,16]{0,1:T(8,128)S(1)} fusion(f32[]{:T(128)} %bitcast.66, f32[]{:T(128)} %bitcast.65, f32[]{:T(128)} %bitcast.64, f32[]{:T(128)} %bitcast.63, f32[16]{0:T(128)S(1)} %copy-done.11, f32[16]{0:T(128)S(1)} %copy-done.12), kind=kLoop, calls=%fused_computation.104 | loop fusion | flops 2816 | bytes 1168 | tf_op jit(solution)/shard_map/add | solution.py:130
  178.8 0.7 fusion.42
  179.7 7.7 %collective-permute-start.8 = (f32[16,128]{1,0:T(8,128)S(1)}, f32[16,128]{1,0:T(8,128)S(1)}, u32[]{:S(2)}, u32[]{:S(2)}) collective-permute-start(f32[16,128]{1,0:T(8,128)S(1)} %get-tuple-element.36), channel_id=1, source_target_pairs={{0,8},{8,16},{16,24},{24,32},{32,40},{40,48},{48,56},{56,64},{64,7... | collective-permute-start | bytes 24584 | tf_op jit(solution)/shard_map/ppermute | solution.py:162
  187.4 1.9 collective-permute-start.9
  189.3 3.1 %collective-permute-start.10 = (f32[16,128]{1,0:T(8,128)S(1)}, f32[16,128]{1,0:T(8,128)S(1)}, u32[]{:S(2)}, u32[]{:S(2)}) collective-permute-start(f32[16,128]{1,0:T(8,128)S(1)} %bitcast.205), channel_id=1, source_target_pairs={{0,1},{1,2},{2,3},{3,4},{4,5},{5,6},{6,7},{8,9},{9,10},{10,11},{11... | collective-permute-start | bytes 24584 | tf_op jit(solution)/shard_map/ppermute | solution.py:164
  192.4 1.3 collective-permute-start.11
  193.9 11.5 %collective-permute-done.9 = f32[16,128]{1,0:T(8,128)S(1)} collective-permute-done((f32[16,128]{1,0:T(8,128)S(1)}, f32[16,128]{1,0:T(8,128)S(1)}, u32[]{:S(2)}, u32[]{:S(2)}) %collective-permute-start.9) | collective-permute-done | bytes 8224 | tf_op jit(solution)/shard_map/ppermute | solution.py:163
  205.5 0.9 fusion.9
  (248 shorter events, 28.7 us)
Async XLA Ops:
  2.3 35.7 %collective-permute-start.1 = (f32[1,544]{1,0:T(1,128)S(1)}, f32[1,544]{1,0:T(1,128)S(1)}, u32[]{:S(2)}, u32[]{:S(2)}) collective-permute-start(f32[1,544]{1,0:T(1,128)S(1)} %pad_maximum_fusion.1), channel_id=1, source_target_pairs={{8,0},{16,8},{24,16},{32,24},{40,32},{48,40},{56,48},{64,56},{72,6... | collective-permute-start | bytes 6536 | tf_op jit(solution)/shard_map/ppermute | solution.py:222
  5.0 30.7 %collective-permute-start.2 = (f32[1,32]{1,0:T(1,128)S(1)}, f32[1,32]{1,0:T(1,128)S(1)}, u32[]{:S(2)}, u32[]{:S(2)}) collective-permute-start(f32[1,32]{1,0:T(1,128)S(1)} %reshape_squeeze.14), channel_id=1, source_target_pairs={{0,1},{1,2},{2,3},{3,4},{4,5},{5,6},{6,7},{8,9},{9,10},{10,11},{11... | collective-permute-start | bytes 392 | tf_op jit(solution)/shard_map/ppermute | solution.py:225
  8.6 28.5 %collective-permute-start = (f32[1,32]{1,0:T(1,128)S(1)}, f32[1,32]{1,0:T(1,128)S(1)}, u32[]{:S(2)}, u32[]{:S(2)}) collective-permute-start(f32[1,32]{1,0:T(1,128)S(1)} %reshape_squeeze.12), channel_id=1, source_target_pairs={{0,8},{8,16},{16,24},{24,32},{32,40},{40,48},{48,56},{56,64},{64,7... | collective-permute-start | bytes 392 | tf_op jit(solution)/shard_map/ppermute | solution.py:221
  25.1 3.2 %copy-start.17 = (f32[8]{0:T(128)S(1)}, f32[8]{0:T(128)}, u32[]{:S(2)}) copy-start(f32[8]{0:T(128)} %param.9) | copy-start | bytes 100
  25.1 3.2 %copy-start.18 = (s32[1,1,2]{2,1,0:T(1,128)S(1)}, s32[1,1,2]{2,1,0:T(1,128)}, u32[]{:S(2)}) copy-start(s32[1,1,2]{2,1,0:T(1,128)} %param.10) | copy-start | bytes 28
  25.1 13.0 %copy-start.9 = (f32[1,512]{1,0:T(1,128)S(1)}, f32[1,512]{1,0:T(1,128)}, u32[]{:S(2)}) copy-start(f32[1,512]{1,0:T(1,128)} %param.11) | copy-start | bytes 6148
  26.3 22.1 %copy-start.13 = (f32[1,16]{1,0:T(1,128)}, f32[1,16]{1,0:T(1,128)S(1)}, u32[]{:S(2)}) copy-start(f32[1,16]{1,0:T(1,128)S(1)} %get-tuple-element.214) | copy-start | bytes 196
  26.3 22.1 %copy-start.15 = (f32[1,16]{1,0:T(1,128)}, f32[1,16]{1,0:T(1,128)S(1)}, u32[]{:S(2)}) copy-start(f32[1,16]{1,0:T(1,128)S(1)} %get-tuple-element.215) | copy-start | bytes 196
  37.1 6.4 %copy-start = (f32[16,16,128]{2,1,0:T(8,128)S(1)}, f32[16,16,128]{2,1,0:T(8,128)}, u32[]{:S(2)}) copy-start(f32[16,16,128]{2,1,0:T(8,128)} %param.6) | copy-start | bytes 393220
  38.2 4.5 %collective-permute-start.3 = (f32[1,1056]{1,0:T(1,128)S(1)}, f32[1,1056]{1,0:T(1,128)S(1)}, u32[]{:S(2)}, u32[]{:S(2)}) collective-permute-start(f32[1,1056]{1,0:T(1,128)S(1)} %concatenate.365), channel_id=1, source_target_pairs={{1,0},{2,1},{3,2},{4,3},{5,4},{6,5},{7,6},{9,8},{10,9},{11,10},{12... | collective-permute-start | bytes 12680 | tf_op jit(solution)/shard_map/ppermute | solution.py:227
  46.9 17.3 %copy-start.10 = (f32[1,512]{1,0:T(1,128)S(1)}, f32[1,512]{1,0:T(1,128)}, u32[]{:S(2)}) copy-start(f32[1,512]{1,0:T(1,128)} %param.11) | copy-start | bytes 6148
  47.1 22.0 %copy-start.2 = (f32[1,16,128]{2,0,1:T(1,128)}, f32[1,16,128]{2,0,1:T(1,128)S(1)}, u32[]{:S(2)}) copy-start(f32[1,16,128]{2,0,1:T(1,128)S(1)} %slice.792) | copy-start | bytes 24580
  47.1 22.0 %copy-start.4 = (f32[1,16,128]{2,0,1:T(1,128)}, f32[1,16,128]{2,0,1:T(1,128)S(1)}, u32[]{:S(2)}) copy-start(f32[1,16,128]{2,0,1:T(1,128)S(1)} %slice.861) | copy-start | bytes 24580
  47.5 0.6 copy-start.1
  48.6 15.5 %copy-start.7 = (f32[2,16]{1,0:T(2,128)}, f32[2,16]{1,0:T(2,128)S(1)}, u32[]{:S(2)}) copy-start(f32[2,16]{1,0:T(2,128)S(1)} %get-tuple-element.188) | copy-start | bytes 388
  57.6 10.2 %all-to-all-start = ((f32[32,1,16]{2,1,0:T(1,128)}), f32[32,1,16]{2,1,0:T(1,128)S(1)}, u32[]{:S(2)}, u32[]{:S(2)}) async-start(f32[32,1,16]{2,1,0:T(1,128)} %broadcast_in_dim.67), calls=%async_computation | async-start | bytes 32768 | tf_op jit(solution)/shard_map/all_to_all | solution.py:203
  69.1 22.4 %all-to-all-start.1 = ((f32[16,1,512]{2,1,0:T(1,128)}), f32[16,1,512]{2,1,0:T(1,128)}, u32[]{:S(2)}, u32[]{:S(2)}) async-start(f32[16,1,512]{2,1,0:T(1,128)} %broadcast_in_dim.69), calls=%async_computation.1 | async-start | bytes 65536 | tf_op jit(solution)/shard_map/all_to_all | solution.py:207
  81.9 11.7 %copy-start.11 = (f32[16]{0:T(128)S(1)}, f32[16]{0:T(128)}, u32[]{:S(2)}) copy-start(f32[16]{0:T(128)} %get-tuple-element.216) | copy-start | bytes 196
  81.9 11.7 %copy-start.12 = (f32[16]{0:T(128)S(1)}, f32[16]{0:T(128)}, u32[]{:S(2)}) copy-start(f32[16]{0:T(128)} %get-tuple-element.217) | copy-start | bytes 196
  82.8 36.4 %copy-start.5 = (f32[1,16,128]{2,0,1:T(1,128)S(1)}, f32[1,16,128]{2,0,1:T(1,128)}, u32[]{:S(2)}) copy-start(f32[1,16,128]{2,0,1:T(1,128)} %copy-done.4) | copy-start | bytes 24580
  82.8 37.6 %copy-start.3 = (f32[1,16,128]{2,0,1:T(1,128)S(1)}, f32[1,16,128]{2,0,1:T(1,128)}, u32[]{:S(2)}) copy-start(f32[1,16,128]{2,0,1:T(1,128)} %copy-done.2) | copy-start | bytes 24580
  96.5 22.7 %collective-permute-start.5 = (f32[16,128]{1,0:T(8,128)S(1)}, f32[16,128]{1,0:T(8,128)S(1)}, u32[]{:S(2)}, u32[]{:S(2)}) collective-permute-start(f32[16,128]{1,0:T(8,128)S(1)} %bitcast.196), channel_id=1, source_target_pairs={{8,0},{16,8},{24,16},{32,24},{40,32},{48,40},{56,48},{64,56},{72,6... | collective-permute-start | bytes 24584 | tf_op jit(solution)/shard_map/ppermute | solution.py:163
  100.4 21.2 %collective-permute-start.6 = (f32[16,128]{1,0:T(8,128)S(1)}, f32[16,128]{1,0:T(8,128)S(1)}, u32[]{:S(2)}, u32[]{:S(2)}) collective-permute-start(f32[16,128]{1,0:T(8,128)S(1)} %get-tuple-element.91), channel_id=1, source_target_pairs={{0,1},{1,2},{2,3},{3,4},{4,5},{5,6},{6,7},{8,9},{9,10},{10,11},{11... | collective-permute-start | bytes 24584 | tf_op jit(solution)/shard_map/ppermute | solution.py:164
  102.9 18.7 %collective-permute-start.7 = (f32[16,128]{1,0:T(8,128)S(1)}, f32[16,128]{1,0:T(8,128)S(1)}, u32[]{:S(2)}, u32[]{:S(2)}) collective-permute-start(f32[16,128]{1,0:T(8,128)S(1)} %get-tuple-element.92), channel_id=1, source_target_pairs={{1,0},{2,1},{3,2},{4,3},{5,4},{6,5},{7,6},{9,8},{10,9},{11,10},{12... | collective-permute-start | bytes 24584 | tf_op jit(solution)/shard_map/ppermute | solution.py:165
  104.2 16.2 %collective-permute-start.4 = (f32[16,128]{1,0:T(8,128)S(1)}, f32[16,128]{1,0:T(8,128)S(1)}, u32[]{:S(2)}, u32[]{:S(2)}) collective-permute-start(f32[16,128]{1,0:T(8,128)S(1)} %bitcast.198), channel_id=1, source_target_pairs={{0,8},{8,16},{16,24},{24,32},{32,40},{40,48},{48,56},{56,64},{64,7... | collective-permute-start | bytes 24584 | tf_op jit(solution)/shard_map/ppermute | solution.py:162
  127.8 0.8 copy-start.6
  127.9 1.9 copy-start.14
  128.0 1.9 copy-start.16
  128.9 6.3 %copy-start.8 = (f32[2,16]{1,0:T(2,128)S(1)}, f32[2,16]{1,0:T(2,128)}, u32[]{:S(2)}) copy-start(f32[2,16]{1,0:T(2,128)} %copy-done.7) | copy-start | bytes 388
  179.7 14.2 %collective-permute-start.8 = (f32[16,128]{1,0:T(8,128)S(1)}, f32[16,128]{1,0:T(8,128)S(1)}, u32[]{:S(2)}, u32[]{:S(2)}) collective-permute-start(f32[16,128]{1,0:T(8,128)S(1)} %get-tuple-element.36), channel_id=1, source_target_pairs={{0,8},{8,16},{16,24},{24,32},{32,40},{40,48},{48,56},{56,64},{64,7... | collective-permute-start | bytes 24584 | tf_op jit(solution)/shard_map/ppermute | solution.py:162
  187.4 18.0 %collective-permute-start.9 = (f32[16,128]{1,0:T(8,128)S(1)}, f32[16,128]{1,0:T(8,128)S(1)}, u32[]{:S(2)}, u32[]{:S(2)}) collective-permute-start(f32[16,128]{1,0:T(8,128)S(1)} %get-tuple-element.35), channel_id=1, source_target_pairs={{8,0},{16,8},{24,16},{32,24},{40,32},{48,40},{56,48},{64,56},{72,6... | collective-permute-start | bytes 24584 | tf_op jit(solution)/shard_map/ppermute | solution.py:163
  189.3 16.1 %collective-permute-start.10 = (f32[16,128]{1,0:T(8,128)S(1)}, f32[16,128]{1,0:T(8,128)S(1)}, u32[]{:S(2)}, u32[]{:S(2)}) collective-permute-start(f32[16,128]{1,0:T(8,128)S(1)} %bitcast.205), channel_id=1, source_target_pairs={{0,1},{1,2},{2,3},{3,4},{4,5},{5,6},{6,7},{8,9},{9,10},{10,11},{11... | collective-permute-start | bytes 24584 | tf_op jit(solution)/shard_map/ppermute | solution.py:164
  192.4 13.1 %collective-permute-start.11 = (f32[16,128]{1,0:T(8,128)S(1)}, f32[16,128]{1,0:T(8,128)S(1)}, u32[]{:S(2)}, u32[]{:S(2)}) collective-permute-start(f32[16,128]{1,0:T(8,128)S(1)} %bitcast.204), channel_id=1, source_target_pairs={{1,0},{2,1},{3,2},{4,3},{5,4},{6,5},{7,6},{9,8},{10,9},{11,10},{12... | collective-permute-start | bytes 24584 | tf_op jit(solution)/shard_map/ppermute | solution.py:165

commit v2 on v0

v2 whole, which is shorter than its diff:
```python
import jax
import jax.numpy as jnp
from jax import lax
from jax.experimental import pallas as pl
from jax.experimental.pallas import tpu as pltpu
from jax.sharding import PartitionSpec as P

BLOCK = 8
SWEEPS = 4
CX = 16
CY = 16
NZ = 128
MATERIALS = 16
NEAR = 0.5 / 16
FAR = 15.5 / 16
INTERPRET = False
GRANT = 8 * 1024 * 1024
EXACT = lax.Precision.HIGHEST
F32 = jnp.float32
SHIFTS = [(i, j) for i in range(4) for j in range(4) if i in (1, 2) or j in (1, 2)]

VMEM = pl.BlockSpec(memory_space=pltpu.VMEM)
SMEM = pl.BlockSpec(memory_space=pltpu.SMEM)


def row_at(i):
    return (i + 0.5) / CX


def iota(shape, axis):
    return lax.broadcasted_iota(jnp.int32, shape, axis)


def rolled(value, shift, axis):
    return pltpu.roll(value, shift % value.shape[axis], axis)


def place():
    wide, narrow = lax.axis_index("wide"), lax.axis_index("narrow")
    last_wide, last_narrow = lax.axis_size("wide") - 1, lax.axis_size("narrow") - 1
    inside = tuple(
        jnp.where(flag, F32(1.0), F32(0.0))
        for flag in (wide > 0, wide < last_wide, narrow > 0, narrow < last_narrow)
    )
    return wide % 2 == 0, narrow % 2 == 0, inside


def sided(even, first, second):
    return jnp.where(even, second, first), jnp.where(even, first, second)


def eta_pair():
    eta = (iota((CY, NZ), 0).astype(F32) + 0.5) / CY
    return 1.0 - eta, eta


def robin_of(robin_index, robin_table):
    return robin_table[robin_index[0]], robin_table[robin_index[1]]


class Coefficients:
    def __init__(self, kap):
        row = lambda r: jnp.broadcast_to(kap[r : r + 1, :], (BLOCK, NZ))
        tile = lambda low, high: jnp.concatenate([row(low), row(high)], 0)
        at_y, at_z = iota((CY, NZ), 0), iota((CY, NZ), 1)
        both = (tile(0, 1), tile(2, 3))
        self.x = (
            [0.5 * (both[0] + tile(4, 5))]
            + [both[0]] * 7
            + [0.5 * (both[0] + both[1])]
            + [both[1]] * 7
            + [0.5 * (both[1] + tile(6, 7))]
        )
        self.south, self.north, self.below, self.above = [], [], [], []
        self.rest = []
        for a in range(2):
            k = both[a]
            flipped = tile(2 * a + 1, 2 * a)
            middle = 0.5 * (k + flipped)
            south = jnp.where(at_y == 0, 0.5 * (k + tile(8 + a, 8 + a)), jnp.where(at_y == BLOCK, middle, k))
            north = jnp.where(
                at_y == CY - 1, 0.5 * (k + tile(10 + a, 10 + a)), jnp.where(at_y == BLOCK - 1, middle, k)
            )
            below = jnp.where(at_z == 0, k, 0.5 * (k + rolled(k, 1, 1)))
            above = jnp.where(at_z == NZ - 1, k, 0.5 * (k + rolled(k, -1, 1)))
            self.south.append(south)
            self.north.append(north)
            self.rest.append(south + north + below + above)
            self.below.append(jnp.where(at_z == 0, 0.0, below))
            self.above.append(jnp.where(at_z == NZ - 1, 0.0, above))
        self.south_in = [jnp.where(at_y == 0, 0.0, c) for c in self.south]
        self.north_in = [jnp.where(at_y == CY - 1, 0.0, c) for c in self.north]
        self.at_y = at_y
        self.totals = {}

    def total(self, i):
        key = i if i in (0, 7, 8, 15) else i // BLOCK + 20
        if key not in self.totals:
            self.totals[key] = 1.0 + self.x[i] + self.x[i + 1] + self.rest[i // BLOCK]
        return self.totals[key]

    def coupling(self, u, i):
        a, here = i // BLOCK, u[i]
        total = self.south_in[a] * rolled(here, 1, 0) + self.north_in[a] * rolled(here, -1, 0)
        total = total + self.below[a] * rolled(here, 1, 1) + self.above[a] * rolled(here, -1, 1)
        if i > 0:
            total = total + self.x[i] * u[i - 1]
        if i < CX - 1:
            total = total + self.x[i + 1] * u[i + 1]
        return total


def relax(coef, inside, robin, u, source, first):
    at_y = coef.at_y
    side_y = robin[1] * (
        jnp.where(at_y == 0, inside[2], 0.0) + jnp.where(at_y == CY - 1, inside[3], 0.0)
    )
    inverse = {}
    for i in range(CX):
        key = i if i in (0, 7, 8, 15) else i // BLOCK + 20
        if key not in inverse:
            diagonal = coef.total(i) + side_y
            if i == 0:
                diagonal = diagonal + robin[0] * inside[0]
            if i == CX - 1:
                diagonal = diagonal + robin[0] * inside[1]
            inverse[key] = 1.0 / diagonal
        inverse[i + 100] = inverse[key]
    odd = (iota((CY, NZ), 0) + iota((CY, NZ), 1)) % 2
    masks = (odd == 0, odd == 1)
    for half in range(2 * SWEEPS):
        for i in range(CX):
            mask = masks[(i + half) % 2]
            if first and half == 0:
                u[i] = jnp.where(mask, source[i] * inverse[i + 100], 0.0)
            else:
                update = (source[i] + coef.coupling(u, i)) * inverse[i + 100]
                u[i] = jnp.where(mask, update, u[i])


def contribute(coef, inside, u, right, sums, out):
    weights = eta_pair()
    zero = jnp.zeros((CY, NZ), F32)
    own, south, north = [zero, zero], [zero, zero], [zero, zero]
    for i in range(CX):
        a, here = i // BLOCK, u[i]
        left = right[i] - coef.total(i) * here + coef.coupling(u, i)
        low, high = coef.south[a] * here, coef.north[a] * here
        for side, weight in enumerate((1.0 - row_at(i), row_at(i))):
            own[side] = own[side] + weight * left
            south[side] = south[side] + weight * low
            north[side] = north[side] + weight * high
    across = lambda value, b: jnp.sum(value * weights[b], axis=0, keepdims=True)
    west, east = inside[0] * coef.x[0] * u[0], inside[1] * coef.x[CX] * u[CX - 1]
    west_row = [across(west, b) for b in range(2)]
    east_row = [across(east, b) for b in range(2)]
    south_row = [inside[2] * south[a][:1] for a in range(2)]
    north_row = [inside[3] * north[a][CY - 1 :] for a in range(2)]
    sums[...] = jnp.zeros_like(sums)
    for a in range(2):
        for b in range(2):
            near_x, near_y = (west_row, east_row)[a][b], (south_row, north_row)[b][a]
            at = (1 + a) * 4 + 1 + b
            sums[at : at + 1, :] = across(own[a], b) + FAR * (near_x + near_y)
    for b in range(2):
        sums[1 + b : 2 + b, :] = NEAR * west_row[b]
        sums[13 + b : 14 + b, :] = NEAR * east_row[b]
    for a in range(2):
        at = (1 + a) * 4
        sums[at : at + 1, :] = NEAR * south_row[a]
        sums[at + 3 : at + 4, :] = NEAR * north_row[a]
    column = jnp.sum(sums[...], axis=1, keepdims=True)
    spread = jnp.where(iota((16, NZ), 0) == iota((16, NZ), 1), column, 0.0)
    out[...] = jnp.broadcast_to(jnp.sum(spread, axis=0, keepdims=True), out.shape)


def pack_kernel(labels, row, pay):
    pay[...] = jnp.zeros_like(pay)
    for a in range(2):
        pay[2 * a : 2 * a + 2, 0 : labels.shape[2]] = labels[a].astype(F32)
    for c in range(row.shape[1] // NZ):
        pay[4 + c : 5 + c, :] = row[:, c * NZ : (c + 1) * NZ]


def first_kernel(right, table, robin_table, robin_index, own, y2, y1, x1, x2, u, out, kap, east, sums):
    even_x, even_y, inside = place()
    from_west, from_east = sided(even_x, x1[...], x2[...])
    from_south, from_north = sided(even_y, y1[...], y2[...])
    east[...] = from_east
    keys = jnp.concatenate([own[...], from_west, from_east, from_south, from_north], 0)
    pick = (iota((NZ, NZ), 0) == iota((NZ, NZ), 1) // BLOCK).astype(F32)
    keys = jnp.dot(keys, pick, precision=EXACT, preferred_element_type=F32)
    found = jnp.zeros_like(keys)
    for m in range(MATERIALS):
        found = jnp.where(jnp.abs(keys - m) < 0.5, table[m], found)
    kap[...] = jnp.zeros_like(kap)
    kap[0:4, :] = found[0:4]
    for b in range(2):
        own_of = lambda a, c: found[2 * a + c : 2 * a + c + 1]
        kap[4 + b : 5 + b, :] = jnp.where(inside[0] > 0, found[10 + b : 11 + b], own_of(0, b))
        kap[6 + b : 7 + b, :] = jnp.where(inside[1] > 0, found[16 + b : 17 + b], own_of(1, b))
        kap[8 + b : 9 + b, :] = jnp.where(inside[2] > 0, found[25 + 2 * b : 26 + 2 * b], own_of(b, 0))
        kap[10 + b : 11 + b, :] = jnp.where(inside[3] > 0, found[32 + 2 * b : 33 + 2 * b], own_of(b, 1))
    coef = Coefficients(kap)
    relax(coef, inside, robin_of(robin_index, robin_table), u, right, True)
    contribute(coef, inside, u, right, sums, out)


def correct(every, own, east, north, corner, u, shifted, rows, new, sends):
    even_x, even_y, _ = place()
    count = rows.shape[1]
    narrow_count = lax.axis_size("narrow")
    wide_count = count // narrow_count
    rows[...] = jnp.zeros_like(rows)
    for k, pay in enumerate((own, east, north, corner)):
        for c in range(count // NZ):
            rows[k : k + 1, c * NZ : (c + 1) * NZ] = pay[4 + c : 5 + c, :]
    at = iota((8, count), 1)
    at_x, at_y = at // narrow_count, at % narrow_count
    held = rows[...]
    for t, (i, j) in enumerate(SHIFTS):
        x, y = at_x + (i - 1), at_y + (j - 1)
        fits = (x >= 0) & (x < wide_count) & (y >= 0) & (y < narrow_count)
        moved = rolled(held, -((i - 1) * narrow_count + j - 1), 1)
        shifted[8 * t : 8 * t + 8, :] = jnp.where(fits, moved, 0.0)
    product = jnp.dot(shifted[...], every[...], precision=EXACT, preferred_element_type=F32)
    lane = iota((8, NZ), 1)
    picked = jnp.zeros((8, NZ), F32)
    for t, (i, j) in enumerate(SHIFTS):
        picked = picked + jnp.where(lane == 4 * i + j, product[8 * t : 8 * t + 8], 0.0)
    value = jnp.sum(picked, axis=1, keepdims=True)
    value = [jnp.broadcast_to(value[k : k + 1], (CY, NZ)) for k in range(4)]
    low, high = eta_pair()
    west, east_side = value[0] * low + value[2] * high, value[1] * low + value[3] * high
    sx1, sx2, sy1, sy2 = sends
    for i in range(CX):
        now = u[i] + ((1.0 - row_at(i)) * west + row_at(i) * east_side)
        new[i] = now
        south, north_row = now[:1], now[CY - 1 :]
        sy1[i : i + 1, :] = jnp.where(even_y, north_row, south)
        sy2[i : i + 1, :] = jnp.where(even_y, south, north_row)
        if i == 0:
            first = now
    sx1[...] = jnp.where(even_x, now, first)
    sx2[...] = jnp.where(even_x, first, now)


def make_correct(final):
    def kernel(every, own, east, y1, y2, corner, u, new, sx1, sx2, sy1, sy2, *more):
        if final:
            solution_out, shifted, rows, north = more
        else:
            shifted, rows, north = more
        _, even_y, _ = place()
        north[...] = sided(even_y, y1[...], y2[...])[1]
        correct(every, own, east, north, corner, u, shifted, rows, new, (sx1, sx2, sy1, sy2))
        if final:
            solution_out[...] = new[...].astype(jnp.bfloat16)

    return kernel


def second_kernel(right, robin_table, robin_index, kap, old, x2, x1, y1, y2, u, out, source, sums):
    even_x, even_y, inside = place()
    west, east = sided(even_x, x1[...], x2[...])
    south, north = sided(even_y, y1[...], y2[...])
    robin = robin_of(robin_index, robin_table)
    coef = Coefficients(kap)
    for i in range(CX):
        a, here = i // BLOCK, old[i]
        u[i] = here
        total = right[i]
        trace = inside[2] * (coef.south[a] * south[i : i + 1] + robin[1] * here)
        total = total + jnp.where(coef.at_y == 0, trace, 0.0)
        trace = inside[3] * (coef.north[a] * north[i : i + 1] + robin[1] * here)
        total = total + jnp.where(coef.at_y == CY - 1, trace, 0.0)
        if i == 0:
            total = total + inside[0] * (coef.x[0] * west + robin[0] * here)
        if i == CX - 1:
            total = total + inside[1] * (coef.x[CX] * east + robin[0] * here)
        source[i] = total
    relax(coef, inside, robin, u, source, False)
    contribute(coef, inside, u, right, sums, out)


def last_kernel(right, kap, u, x2, x1, y1, y2, out):
    even_x, even_y, inside = place()
    west, east = sided(even_x, x1[...], x2[...])
    south, north = sided(even_y, y1[...], y2[...])
    coef = Coefficients(kap)
    for i in range(CX):
        a = i // BLOCK
        left = right[i] - coef.total(i) * u[i] + coef.coupling(u, i)
        left = left + jnp.where(coef.at_y == 0, inside[2] * coef.south[a] * south[i : i + 1], 0.0)
        left = left + jnp.where(coef.at_y == CY - 1, inside[3] * coef.north[a] * north[i : i + 1], 0.0)
        if i == 0:
            left = left + inside[0] * coef.x[0] * west
        if i == CX - 1:
            left = left + inside[1] * coef.x[CX] * east
        out[i] = left.astype(jnp.bfloat16)


def call(kernel, out_shape, spaces, scratch=()):
    return pl.pallas_call(
        kernel,
        out_shape=out_shape,
        in_specs=list(spaces),
        out_specs=jax.tree.map(lambda _: VMEM, out_shape),
        scratch_shapes=list(scratch),
        interpret=INTERPRET,
        compiler_params=pltpu.CompilerParams(vmem_limit_bytes=GRANT),
    )


def swap_pairs(peers, start):
    pairs = []
    for i in range(start, peers - 1, 2):
        pairs += [(i, i + 1), (i + 1, i)]
    return pairs


def swaps(sx1, sx2, sy1, sy2):
    wide_count, narrow_count = lax.axis_size("wide"), lax.axis_size("narrow")
    x2 = lax.ppermute(sx2, "wide", swap_pairs(wide_count, 1))
    x1 = lax.ppermute(sx1, "wide", swap_pairs(wide_count, 0))
    y1 = lax.ppermute(sy1, "narrow", swap_pairs(narrow_count, 0))
    y2 = lax.ppermute(sy2, "narrow", swap_pairs(narrow_count, 1))
    return x2, x1, y1, y2


def everywhere(values):
    return lax.all_to_all(values, ("wide", "narrow"), 0, 0, tiled=True)


def body(right_side, labels, material_table, robin_table, robin_index, coarse_rows):
    count = coarse_rows.shape[1]
    shape = lambda *dims: jax.ShapeDtypeStruct(dims, F32)
    field, face, gathered = shape(CX, CY, NZ), shape(CY, NZ), shape(count, NZ)
    pay_shape = shape(8, NZ)
    index = robin_index[0, 0]
    pay = call(pack_kernel, pay_shape, [VMEM] * 2)(labels, coarse_rows)
    x2, x1, y1, y2 = swaps(pay, pay, pay, pay)
    u, sent, kap, east = call(
        first_kernel,
        (field, gathered, shape(16, NZ), pay_shape),
        [VMEM] + [SMEM] * 3 + [VMEM] * 5,
        [pltpu.VMEM((16, NZ), F32)],
    )(right_side, material_table, robin_table, index, pay, y2, y1, x1, x2)
    narrow_count = lax.axis_size("narrow")
    corner = lax.ppermute(east, "narrow", [(i + 1, i) for i in range(narrow_count - 1)])
    work = [pltpu.VMEM((8 * len(SHIFTS), count), F32), pltpu.VMEM((8, count), F32), pltpu.VMEM((8, NZ), F32)]
    u, *faces = call(make_correct(False), (field, face, face, face, face), [VMEM] * 7, work)(
        everywhere(sent), pay, east, y1, y2, corner, u
    )
    seen = swaps(*faces)
    u, sent = call(
        second_kernel,
        (field, gathered),
        [VMEM] + [SMEM] * 2 + [VMEM] * 6,
        [pltpu.VMEM((CX, CY, NZ), F32), pltpu.VMEM((16, NZ), F32)],
    )(right_side, robin_table, index, kap, u, *seen)
    half = jax.ShapeDtypeStruct((CX, CY, NZ), jnp.bfloat16)
    u, f1, f2, f3, f4, answer = call(
        make_correct(True), (field, face, face, face, face, half), [VMEM] * 7, work
    )(everywhere(sent), pay, east, y1, y2, corner, u)
    seen = swaps(f1, f2, f3, f4)
    leftover = call(last_kernel, half, [VMEM] * 7)(right_side, kap, u, *seen)
    return (answer, leftover)


def solution(mesh):
    placed = (
        P("wide", "narrow", None),
        P("wide", "narrow", None),
        P(),
        P(),
        P("wide", "narrow", None),
        P(("wide", "narrow"), None),
    )
    return jax.shard_map(
        body,
        mesh=mesh,
        in_specs=placed,
        out_specs=(P("wide", "narrow", None), P("wide", "narrow", None)),
        check_vma=False,
    )
```

time: 422 us -> 141 us (0.33)
  blocking collectives: 204 us -> 36.1 us
  waiting for transfers between devices: 86.4 us -> 31.5 us
  other arithmetic: 39 us -> 0 us
  local copies, waits for them, and re-layouts: 14.1 us -> 2.27 us
  starting transfers between devices: 73.3 us -> 63.6 us
  Pallas kernels: 0 us -> 6.59 us
    unnamed x2 -> x0, blocking collectives: 204 us -> none
    ppermute x24 -> x13, waiting for transfers between devices: 86.4 us -> 19.2 us  [the longest x3 10.9 us: swaps(): x2 = lax.ppermute(sx2, 'wide', swap_pairs(wide_count, 1))]
    all_to_all x0 -> x1, blocking collectives: none -> 36.1 us  [everywhere(): return lax.all_to_all(values, ('wide', 'narrow'), 0, 0, tiled=True)]
    ppermute x24 -> x13, starting transfers between devices: 73.3 us -> 47 us  [the longest x3 30.5 us: swaps(): x2 = lax.ppermute(sx2, 'wide', swap_pairs(wide_count, 1))]
    all_to_all x0 -> x1, starting transfers between devices: none -> 16.6 us  [everywhere(): return lax.all_to_all(values, ('wide', 'narrow'), 0, 0, tiled=True)]
    all_to_all x0 -> x1, waiting for transfers between devices: none -> 12.2 us  [everywhere(): return lax.all_to_all(values, ('wide', 'narrow'), 0, 0, tiled=True)]
    slice x92 -> x0, local copies, waits for them, and re-layouts: 11.1 us -> none  [the longest x18 1.63 us: neighbour_sum(): field_now[:, :, :-1]]
    mul x5 -> x0, other arithmetic: 8.91 us -> none  [the longest x1 3.8 us: assemble_local(): robin_pair[1] * (inside[2] * marks[2] + inside[3] * marks[3])]
  transfers between devices with their start and end apart: 24 -> 14, of which waited for: 8 -> 5; matrix products, arithmetic and copies ran while one was open for 3% -> 0% of each run, Pallas kernels for 0% -> 0%
where the time goes in v2:
time: 141 us
  starting transfers between devices  63.6 us (45%)
  blocking collectives  36.1 us (26%)
  waiting for transfers between devices  31.5 us (22%)
  Pallas kernels  6.59 us (5%)
  local copies, waits for them, and re-layouts  2.27 us (2%)
    all_to_all x1, blocking collectives, everywhere(): return lax.all_to_all(values, ('wide', 'narrow'), 0, 0, tiled=True)  36.1 us
    ppermute x3, starting transfers between devices, swaps(): x2 = lax.ppermute(sx2, 'wide', swap_pairs(wide_count, 1))  30.5 us
    all_to_all x1, starting transfers between devices, everywhere(): return lax.all_to_all(values, ('wide', 'narrow'), 0, 0, tiled=True)  16.6 us
    all_to_all x1, waiting for transfers between devices, everywhere(): return lax.all_to_all(values, ('wide', 'narrow'), 0, 0, tiled=True)  12.2 us
    ppermute x3, waiting for transfers between devices, swaps(): x2 = lax.ppermute(sx2, 'wide', swap_pairs(wide_count, 1))  10.9 us
    ppermute x3, starting transfers between devices, swaps(): y1 = lax.ppermute(sy1, 'narrow', swap_pairs(narrow_count, 0))  7.44 us
    ppermute x1, waiting for transfers between devices, body(): lax.ppermute(east, 'narrow', [(i + 1, i) for i in range(narrow_count - 1)])  7.27 us
    ppermute x3, starting transfers between devices, swaps(): x1 = lax.ppermute(sx1, 'wide', swap_pairs(wide_count, 0))  5.76 us
  transfers between devices with their start and end apart: 14, of which 5 were waited for; matrix products, arithmetic and copies ran while one was open for 0% of the time, Pallas kernels for 0%

profile of v2, /device:TPU:31, one launch (start us, length us, event | category | flops | bytes accessed | tf_op | source)
XLA Modules:
  0.0 140.9 jit_solution(10883466835345408656)
XLA Ops:
  0.6 0.0 copy-start.4
  0.6 0.7 copy-done.4
  1.3 0.0 copy-start.5
  1.3 0.7 copy-done.5
  2.0 0.0 copy-start.2
  2.0 0.0 copy-start.3
  2.0 0.0 copy-start.6
  2.0 15.7 %collective-permute-start.3 = (f32[8,128]{1,0:T(8,128)S(1)}, f32[8,128]{1,0:T(8,128)S(1)}, u32[]{:S(2)}, u32[]{:S(2)}) collective-permute-start(f32[8,128]{1,0:T(8,128)S(1)} %shard_map.77.own), channel_id=1, source_target_pairs={{8,16},{16,8},{24,32},{32,24},{40,48},{48,40},{56,64},{64,56},{72,... | collective-permute-start | bytes 12296 | tf_op jit(solution)/shard_map/ppermute | solution.py:324
  17.7 1.9 %collective-permute-start.2 = (f32[8,128]{1,0:T(8,128)S(1)}, f32[8,128]{1,0:T(8,128)S(1)}, u32[]{:S(2)}, u32[]{:S(2)}) collective-permute-start(f32[8,128]{1,0:T(8,128)S(1)} %shard_map.77.own), channel_id=1, source_target_pairs={{0,8},{8,0},{16,24},{24,16},{32,40},{40,32},{48,56},{56,48},{64,72... | collective-permute-start | bytes 12296 | tf_op jit(solution)/shard_map/ppermute | solution.py:325
  19.7 2.6 %collective-permute-start.1 = (f32[8,128]{1,0:T(8,128)S(1)}, f32[8,128]{1,0:T(8,128)S(1)}, u32[]{:S(2)}, u32[]{:S(2)}) collective-permute-start(f32[8,128]{1,0:T(8,128)S(1)} %shard_map.77.own), channel_id=1, source_target_pairs={{0,1},{1,0},{2,3},{3,2},{4,5},{5,4},{6,7},{7,6},{8,9},{9,8},{10,11... | collective-permute-start | bytes 12296 | tf_op jit(solution)/shard_map/ppermute | solution.py:326
  22.3 0.7 collective-permute-start
  23.0 0.0 collective-permute-done.3.x2
  23.0 0.0 collective-permute-done.2.x1
  23.0 1.0 collective-permute-done.1.y1
  24.0 0.0 collective-permute-done.y2
  24.0 0.0 copy-done.2
  24.0 0.0 copy-done.3
  24.0 0.0 copy-done.6
  24.0 0.0 copy-start
  24.0 0.9 copy-done
  24.9 2.6 %shard_map.78 = (f32[16,16,128]{2,1,0:T(8,128)S(1)}, f32[512,128]{1,0:T(8,128)}, f32[16,128]{1,0:T(8,128)S(1)}, f32[8,128]{1,0:T(8,128)S(1)}) custom-call(f32[16,16,128]{2,1,0:T(8,128)S(1)} %copy-done, f32[16]{0:T(128)S(1)} %copy-done.6, f32[8]{0:T(128)S(1)} %copy-done.2, s32[2]{0:T(128)S(1)} %bitcast.12, f32[8,128]{1,0:T(8,128)S(1)} %shard_map.77.own, ...), custom_call_target="tpu_custom_call" | custom-call | tf_op jit(solution)/shard_map/pallas_call | solution.py:343
  27.5 16.6 %all-to-all-start = ((f32[512,1,128]{2,1,0:T(1,128)}), f32[512,1,128]{2,1,0:T(1,128)S(1)}, u32[]{:S(2)}, u32[]{:S(2)}) async-start(f32[512,1,128]{2,1,0:T(1,128)} %bitcast.2), calls=%async_computation | async-start | bytes 524288 | tf_op jit(solution)/shard_map/all_to_all | solution.py:332
  44.1 1.3 collective-permute-start.4
  45.4 7.3 %collective-permute-done.4.corner = f32[8,128]{1,0:T(8,128)S(1)} collective-permute-done((f32[8,128]{1,0:T(8,128)S(1)}, f32[8,128]{1,0:T(8,128)S(1)}, u32[]{:S(2)}, u32[]{:S(2)}) %collective-permute-start.4) | collective-permute-done | bytes 4128 | tf_op jit(solution)/shard_map/ppermute | solution.py:350
  52.6 12.2 %all-to-all-done = f32[512,1,128]{2,1,0:T(1,128)S(1)} async-done(((f32[512,1,128]{2,1,0:T(1,128)}), f32[512,1,128]{2,1,0:T(1,128)S(1)}, u32[]{:S(2)}, u32[]{:S(2)}) %all-to-all-start) | async-done | bytes 262176 | tf_op jit(solution)/shard_map/all_to_all | solution.py:332
  64.9 0.0 copy-start.1
  64.9 0.5 shard_map.79
  65.4 7.4 %collective-permute-start.5 = (f32[16,128]{1,0:T(8,128)S(1)}, f32[16,128]{1,0:T(8,128)S(1)}, u32[]{:S(2)}, u32[]{:S(2)}) collective-permute-start(f32[16,128]{1,0:T(8,128)S(1)} %get-tuple-element.24), channel_id=1, source_target_pairs={{8,16},{16,8},{24,32},{32,24},{40,48},{48,40},{56,64},{64,56},{72,... | collective-permute-start | bytes 24584 | tf_op jit(solution)/shard_map/ppermute | solution.py:324
  72.8 1.9 %collective-permute-start.6 = (f32[16,128]{1,0:T(8,128)S(1)}, f32[16,128]{1,0:T(8,128)S(1)}, u32[]{:S(2)}, u32[]{:S(2)}) collective-permute-start(f32[16,128]{1,0:T(8,128)S(1)} %get-tuple-element.25), channel_id=1, source_target_pairs={{0,8},{8,0},{16,24},{24,16},{32,40},{40,32},{48,56},{56,48},{64,72... | collective-permute-start | bytes 24584 | tf_op jit(solution)/shard_map/ppermute | solution.py:325
  74.7 2.4 %collective-permute-start.7 = (f32[16,128]{1,0:T(8,128)S(1)}, f32[16,128]{1,0:T(8,128)S(1)}, u32[]{:S(2)}, u32[]{:S(2)}) collective-permute-start(f32[16,128]{1,0:T(8,128)S(1)} %get-tuple-element.26), channel_id=1, source_target_pairs={{0,1},{1,0},{2,3},{3,2},{4,5},{5,4},{6,7},{7,6},{8,9},{9,8},{10,11... | collective-permute-start | bytes 24584 | tf_op jit(solution)/shard_map/ppermute | solution.py:326
  77.2 0.7 collective-permute-start.8
  77.8 5.5 %collective-permute-done.5.x2 = f32[16,128]{1,0:T(8,128)S(1)} collective-permute-done((f32[16,128]{1,0:T(8,128)S(1)}, f32[16,128]{1,0:T(8,128)S(1)}, u32[]{:S(2)}, u32[]{:S(2)}) %collective-permute-start.5) | collective-permute-done | bytes 8224 | tf_op jit(solution)/shard_map/ppermute | solution.py:324
  83.3 0.0 collective-permute-done.6.x1
  83.3 0.0 collective-permute-done.7.y1
  83.3 0.0 collective-permute-done.8.y2
  83.3 0.0 copy-done.1
  83.3 1.6 %shard_map.80 = (f32[16,16,128]{2,1,0:T(8,128)S(1)}, f32[512,128]{1,0:T(8,128)S(1)}) custom-call(f32[16,16,128]{2,1,0:T(8,128)S(1)} %copy-done.1, f32[8]{0:T(128)S(1)} %copy-done.2, s32[2]{0:T(128)S(1)} %bitcast.13, f32[16,128]{1,0:T(8,128)S(1)} %get-tuple-element.19.kap, f32[16,16,128]{2,1,0:T(8,128)S(1)} %get-tuple-element.23.old, ...), custom_call_target="tpu_custom_call" | custom-call | tf_op jit(solution)/shard_map/pallas_call | solution.py:356
  84.9 36.1 %all_to_all.22 = f32[512,1,128]{2,1,0:T(1,128)S(1)} all-to-all(f32[512,1,128]{2,1,0:T(1,128)S(1)} %bitcast.11), channel_id=1, replica_groups=mesh['wide'=64,'narrow'=8] {'wide','narrow'}, dimensions={0} | all-to-all | bytes 524288 | tf_op jit(solution)/shard_map/all_to_all | solution.py:332
  121.0 1.1 shard_map.81
  122.2 7.4 %collective-permute-start.9 = (f32[16,128]{1,0:T(8,128)S(1)}, f32[16,128]{1,0:T(8,128)S(1)}, u32[]{:S(2)}, u32[]{:S(2)}) collective-permute-start(f32[16,128]{1,0:T(8,128)S(1)} %get-tuple-element.32), channel_id=1, source_target_pairs={{8,16},{16,8},{24,32},{32,24},{40,48},{48,40},{56,64},{64,56},{72,... | collective-permute-start | bytes 24584 | tf_op jit(solution)/shard_map/ppermute | solution.py:324
  129.6 1.9 %collective-permute-start.10 = (f32[16,128]{1,0:T(8,128)S(1)}, f32[16,128]{1,0:T(8,128)S(1)}, u32[]{:S(2)}, u32[]{:S(2)}) collective-permute-start(f32[16,128]{1,0:T(8,128)S(1)} %get-tuple-element.33), channel_id=1, source_target_pairs={{0,8},{8,0},{16,24},{24,16},{32,40},{40,32},{48,56},{56,48},{64,72... | collective-permute-start | bytes 24584 | tf_op jit(solution)/shard_map/ppermute | solution.py:325
  131.5 2.4 %collective-permute-start.11 = (f32[16,128]{1,0:T(8,128)S(1)}, f32[16,128]{1,0:T(8,128)S(1)}, u32[]{:S(2)}, u32[]{:S(2)}) collective-permute-start(f32[16,128]{1,0:T(8,128)S(1)} %get-tuple-element.34), channel_id=1, source_target_pairs={{0,1},{1,0},{2,3},{3,2},{4,5},{5,4},{6,7},{7,6},{8,9},{9,8},{10,11... | collective-permute-start | bytes 24584 | tf_op jit(solution)/shard_map/ppermute | solution.py:326
  133.9 0.7 collective-permute-start.12
  134.6 5.5 %collective-permute-done.9.x2 = f32[16,128]{1,0:T(8,128)S(1)} collective-permute-done((f32[16,128]{1,0:T(8,128)S(1)}, f32[16,128]{1,0:T(8,128)S(1)}, u32[]{:S(2)}, u32[]{:S(2)}) %collective-permute-start.9) | collective-permute-done | bytes 8224 | tf_op jit(solution)/shard_map/ppermute | solution.py:324
  140.1 0.0 collective-permute-done.10.x1
  140.1 0.0 collective-permute-done.11.y1
  140.1 0.0 collective-permute-done.12.y2
  140.1 0.8 shard_map.82
  (1 shorter events, 0.0 us)
Async XLA Ops:
  0.6 0.7 copy-start.4
  1.3 0.7 copy-start.5
  2.0 22.0 %copy-start.2 = (f32[8]{0:T(128)S(1)}, f32[8]{0:T(128)}, u32[]{:S(2)}) copy-start(f32[8]{0:T(128)} %robin_table.3) | copy-start | bytes 100
  2.0 22.0 %copy-start.3 = (s32[1,1,2]{2,1,0:T(1,128)S(1)}, s32[1,1,2]{2,1,0:T(1,128)}, u32[]{:S(2)}) copy-start(s32[1,1,2]{2,1,0:T(1,128)} %param.10) | copy-start | bytes 28
  2.0 22.0 %copy-start.6 = (f32[16]{0:T(128)S(1)}, f32[16]{0:T(128)}, u32[]{:S(2)}) copy-start(f32[16]{0:T(128)} %table.1) | copy-start | bytes 196
  2.0 21.0 %collective-permute-start.3 = (f32[8,128]{1,0:T(8,128)S(1)}, f32[8,128]{1,0:T(8,128)S(1)}, u32[]{:S(2)}, u32[]{:S(2)}) collective-permute-start(f32[8,128]{1,0:T(8,128)S(1)} %shard_map.77.own), channel_id=1, source_target_pairs={{8,16},{16,8},{24,32},{32,24},{40,48},{48,40},{56,64},{64,56},{72,... | collective-permute-start | bytes 12296 | tf_op jit(solution)/shard_map/ppermute | solution.py:324
  17.7 5.3 %collective-permute-start.2 = (f32[8,128]{1,0:T(8,128)S(1)}, f32[8,128]{1,0:T(8,128)S(1)}, u32[]{:S(2)}, u32[]{:S(2)}) collective-permute-start(f32[8,128]{1,0:T(8,128)S(1)} %shard_map.77.own), channel_id=1, source_target_pairs={{0,8},{8,0},{16,24},{24,16},{32,40},{40,32},{48,56},{56,48},{64,72... | collective-permute-start | bytes 12296 | tf_op jit(solution)/shard_map/ppermute | solution.py:325
  19.7 4.4 %collective-permute-start.1 = (f32[8,128]{1,0:T(8,128)S(1)}, f32[8,128]{1,0:T(8,128)S(1)}, u32[]{:S(2)}, u32[]{:S(2)}) collective-permute-start(f32[8,128]{1,0:T(8,128)S(1)} %shard_map.77.own), channel_id=1, source_target_pairs={{0,1},{1,0},{2,3},{3,2},{4,5},{5,4},{6,7},{7,6},{8,9},{9,8},{10,11... | collective-permute-start | bytes 12296 | tf_op jit(solution)/shard_map/ppermute | solution.py:326
  22.3 1.7 %collective-permute-start = (f32[8,128]{1,0:T(8,128)S(1)}, f32[8,128]{1,0:T(8,128)S(1)}, u32[]{:S(2)}, u32[]{:S(2)}) collective-permute-start(f32[8,128]{1,0:T(8,128)S(1)} %shard_map.77.own), channel_id=1, source_target_pairs={{1,2},{2,1},{3,4},{4,3},{5,6},{6,5},{9,10},{10,9},{11,12},{12,11},... | collective-permute-start | bytes 12296 | tf_op jit(solution)/shard_map/ppermute | solution.py:327
  24.0 0.9 copy-start
  27.5 37.4 %all-to-all-start = ((f32[512,1,128]{2,1,0:T(1,128)}), f32[512,1,128]{2,1,0:T(1,128)S(1)}, u32[]{:S(2)}, u32[]{:S(2)}) async-start(f32[512,1,128]{2,1,0:T(1,128)} %bitcast.2), calls=%async_computation | async-start | bytes 524288 | tf_op jit(solution)/shard_map/all_to_all | solution.py:332
  44.1 8.6 %collective-permute-start.4 = (f32[8,128]{1,0:T(8,128)S(1)}, f32[8,128]{1,0:T(8,128)S(1)}, u32[]{:S(2)}, u32[]{:S(2)}) collective-permute-start(f32[8,128]{1,0:T(8,128)S(1)} %get-tuple-element.21.east), channel_id=1, source_target_pairs={{1,0},{2,1},{3,2},{4,3},{5,4},{6,5},{7,6},{9,8},{10,9},{11,10},{12... | collective-permute-start | bytes 12296 | tf_op jit(solution)/shard_map/ppermute | solution.py:350
  64.9 18.4 %copy-start.1 = (f32[16,16,128]{2,1,0:T(8,128)S(1)}, f32[16,16,128]{2,1,0:T(8,128)}, u32[]{:S(2)}) copy-start(f32[16,16,128]{2,1,0:T(8,128)} %right.5) | copy-start | bytes 393220
  65.4 17.9 %collective-permute-start.5 = (f32[16,128]{1,0:T(8,128)S(1)}, f32[16,128]{1,0:T(8,128)S(1)}, u32[]{:S(2)}, u32[]{:S(2)}) collective-permute-start(f32[16,128]{1,0:T(8,128)S(1)} %get-tuple-element.24), channel_id=1, source_target_pairs={{8,16},{16,8},{24,32},{32,24},{40,48},{48,40},{56,64},{64,56},{72,... | collective-permute-start | bytes 24584 | tf_op jit(solution)/shard_map/ppermute | solution.py:324
  72.8 10.5 %collective-permute-start.6 = (f32[16,128]{1,0:T(8,128)S(1)}, f32[16,128]{1,0:T(8,128)S(1)}, u32[]{:S(2)}, u32[]{:S(2)}) collective-permute-start(f32[16,128]{1,0:T(8,128)S(1)} %get-tuple-element.25), channel_id=1, source_target_pairs={{0,8},{8,0},{16,24},{24,16},{32,40},{40,32},{48,56},{56,48},{64,72... | collective-permute-start | bytes 24584 | tf_op jit(solution)/shard_map/ppermute | solution.py:325
  74.7 8.6 %collective-permute-start.7 = (f32[16,128]{1,0:T(8,128)S(1)}, f32[16,128]{1,0:T(8,128)S(1)}, u32[]{:S(2)}, u32[]{:S(2)}) collective-permute-start(f32[16,128]{1,0:T(8,128)S(1)} %get-tuple-element.26), channel_id=1, source_target_pairs={{0,1},{1,0},{2,3},{3,2},{4,5},{5,4},{6,7},{7,6},{8,9},{9,8},{10,11... | collective-permute-start | bytes 24584 | tf_op jit(solution)/shard_map/ppermute | solution.py:326
  77.2 6.1 %collective-permute-start.8 = (f32[16,128]{1,0:T(8,128)S(1)}, f32[16,128]{1,0:T(8,128)S(1)}, u32[]{:S(2)}, u32[]{:S(2)}) collective-permute-start(f32[16,128]{1,0:T(8,128)S(1)} %get-tuple-element.27), channel_id=1, source_target_pairs={{1,2},{2,1},{3,4},{4,3},{5,6},{6,5},{9,10},{10,9},{11,12},{12,11},... | collective-permute-start | bytes 24584 | tf_op jit(solution)/shard_map/ppermute | solution.py:327
  122.2 17.9 %collective-permute-start.9 = (f32[16,128]{1,0:T(8,128)S(1)}, f32[16,128]{1,0:T(8,128)S(1)}, u32[]{:S(2)}, u32[]{:S(2)}) collective-permute-start(f32[16,128]{1,0:T(8,128)S(1)} %get-tuple-element.32), channel_id=1, source_target_pairs={{8,16},{16,8},{24,32},{32,24},{40,48},{48,40},{56,64},{64,56},{72,... | collective-permute-start | bytes 24584 | tf_op jit(solution)/shard_map/ppermute | solution.py:324
  129.6 10.5 %collective-permute-start.10 = (f32[16,128]{1,0:T(8,128)S(1)}, f32[16,128]{1,0:T(8,128)S(1)}, u32[]{:S(2)}, u32[]{:S(2)}) collective-permute-start(f32[16,128]{1,0:T(8,128)S(1)} %get-tuple-element.33), channel_id=1, source_target_pairs={{0,8},{8,0},{16,24},{24,16},{32,40},{40,32},{48,56},{56,48},{64,72... | collective-permute-start | bytes 24584 | tf_op jit(solution)/shard_map/ppermute | solution.py:325
  131.5 8.5 %collective-permute-start.11 = (f32[16,128]{1,0:T(8,128)S(1)}, f32[16,128]{1,0:T(8,128)S(1)}, u32[]{:S(2)}, u32[]{:S(2)}) collective-permute-start(f32[16,128]{1,0:T(8,128)S(1)} %get-tuple-element.34), channel_id=1, source_target_pairs={{0,1},{1,0},{2,3},{3,2},{4,5},{5,4},{6,7},{7,6},{8,9},{9,8},{10,11... | collective-permute-start | bytes 24584 | tf_op jit(solution)/shard_map/ppermute | solution.py:326
  133.9 6.2 %collective-permute-start.12 = (f32[16,128]{1,0:T(8,128)S(1)}, f32[16,128]{1,0:T(8,128)S(1)}, u32[]{:S(2)}, u32[]{:S(2)}) collective-permute-start(f32[16,128]{1,0:T(8,128)S(1)} %get-tuple-element.35), channel_id=1, source_target_pairs={{1,2},{2,1},{3,4},{4,3},{5,6},{6,5},{9,10},{10,9},{11,12},{12,11},... | collective-permute-start | bytes 24584 | tf_op jit(solution)/shard_map/ppermute | solution.py:327

commit v3 on v2

--- a/solution.py
+++ b/solution.py
@@ -4,6 +4,7 @@
 from jax.experimental import pallas as pl
 from jax.experimental.pallas import tpu as pltpu
 from jax.sharding import PartitionSpec as P
+
 
 BLOCK = 8
 SWEEPS = 4
@@ -182,11 +183,10 @@
         pay[4 + c : 5 + c, :] = row[:, c * NZ : (c + 1) * NZ]
 
 
-def first_kernel(right, table, robin_table, robin_index, own, y2, y1, x1, x2, u, out, kap, east, sums):
+def first_kernel(right, table, robin_table, robin_index, own, y2, y1, x1, x2, u, out, kap, fx2, fx1, fy1, fy2, sums):
     even_x, even_y, inside = place()
     from_west, from_east = sided(even_x, x1[...], x2[...])
     from_south, from_north = sided(even_y, y1[...], y2[...])
-    east[...] = from_east
     keys = jnp.concatenate([own[...], from_west, from_east, from_south, from_north], 0)
     pick = (iota((NZ, NZ), 0) == iota((NZ, NZ), 1) // BLOCK).astype(F32)
     keys = jnp.dot(keys, pick, precision=EXACT, preferred_element_type=F32)
@@ -204,71 +204,112 @@
     coef = Coefficients(kap)
     relax(coef, inside, robin_of(robin_index, robin_table), u, right, True)
     contribute(coef, inside, u, right, sums, out)
-
-
-def correct(every, own, east, north, corner, u, shifted, rows, new, sends):
+    faces(even_x, even_y, u, (fx2, fx1, fy1, fy2))
+
+
+def faces(even_x, even_y, u, sends):
+    sx2, sx1, sy1, sy2 = sends
+    for i in range(CX):
+        south, north = u[i][:1], u[i][CY - 1 :]
+        sy1[i : i + 1, :] = jnp.where(even_y, north, south)
+        sy2[i : i + 1, :] = jnp.where(even_y, south, north)
+    sx1[0:CY, :] = jnp.where(even_x, u[CX - 1], u[0])
+    sx2[0:CY, :] = jnp.where(even_x, u[0], u[CX - 1])
+
+
+def join_kernel(x1, x2, out):
+    out[0:8, :] = x1[...]
+    out[8:16, :] = x2[...]
+
+
+def ride_kernel(x2, x1, y1, y2, far, fx2, fx1, fy1, fy2, px2, px1, py1, py2):
     even_x, even_y, _ = place()
+    east = sided(even_x, x1[...], x2[...])[1][4:8]
+    north = sided(even_y, y1[...], y2[...])[1][4:8]
+    corner = sided(even_x, far[0:8], far[8:16])[1][4:8]
+    for out, face in ((px2, fx2), (px1, fx1)):
+        out[0:CY, :] = face[...]
+        out[CY : CY + 4, :] = east
+        out[CY + 4 : CY + 8, :] = corner
+    for out, face in ((py1, fy1), (py2, fy2)):
+        out[0:CX, :] = face[...]
+        out[CX : CX + 4, :] = north
+        out[CX + 4 : CX + 8, :] = corner
+        out[CX + 8 : CX + 12, :] = east
+        out[CX + 12 : CX + 16, :] = jnp.zeros((4, NZ), F32)
+
+
+def widen(even_x, even_y, pays, far, seen, rows, shifted):
+    own, x2, x1, y1, y2 = pays
     count = rows.shape[1]
     narrow_count = lax.axis_size("narrow")
     wide_count = count // narrow_count
+    west, east = (p[4:8] for p in sided(even_x, x1[...], x2[...]))
+    south, north = (p[4:8] for p in sided(even_y, y1[...], y2[...]))
+    corners = [p[4:8] for p in sided(even_x, far[0:8], far[8:16])]
+    beyond_x = sided(even_x, seen[1][...], seen[0][...])[1]
+    below, above = sided(even_y, seen[2][...], seen[3][...])
+    held = (
+        own[4:8], east, north, corners[1],
+        west, corners[0],
+        beyond_x[CY : CY + 4], beyond_x[CY + 4 : CY + 8],
+        south, below[CX + 8 : CX + 12],
+        above[CX : CX + 4], above[CX + 4 : CX + 8],
+    )
     rows[...] = jnp.zeros_like(rows)
-    for k, pay in enumerate((own, east, north, corner)):
+    for k, piece in enumerate(held):
         for c in range(count // NZ):
-            rows[k : k + 1, c * NZ : (c + 1) * NZ] = pay[4 + c : 5 + c, :]
-    at = iota((8, count), 1)
+            rows[k : k + 1, c * NZ : (c + 1) * NZ] = piece[c : c + 1]
+    at = iota((16, count), 1)
     at_x, at_y = at // narrow_count, at % narrow_count
-    held = rows[...]
+    value = rows[...]
     for t, (i, j) in enumerate(SHIFTS):
         x, y = at_x + (i - 1), at_y + (j - 1)
         fits = (x >= 0) & (x < wide_count) & (y >= 0) & (y < narrow_count)
-        moved = rolled(held, -((i - 1) * narrow_count + j - 1), 1)
-        shifted[8 * t : 8 * t + 8, :] = jnp.where(fits, moved, 0.0)
+        moved = rolled(value, -((i - 1) * narrow_count + j - 1), 1)
+        shifted[16 * t : 16 * t + 16, :] = jnp.where(fits, moved, 0.0)
+
+
+def window(every, shifted):
     product = jnp.dot(shifted[...], every[...], precision=EXACT, preferred_element_type=F32)
-    lane = iota((8, NZ), 1)
-    picked = jnp.zeros((8, NZ), F32)
+    lane = iota((16, NZ), 1)
+    picked = jnp.zeros((16, NZ), F32)
     for t, (i, j) in enumerate(SHIFTS):
-        picked = picked + jnp.where(lane == 4 * i + j, product[8 * t : 8 * t + 8], 0.0)
+        picked = picked + jnp.where(lane == 4 * i + j, product[16 * t : 16 * t + 16], 0.0)
     value = jnp.sum(picked, axis=1, keepdims=True)
-    value = [jnp.broadcast_to(value[k : k + 1], (CY, NZ)) for k in range(4)]
+    return [jnp.broadcast_to(value[k : k + 1], (CY, NZ)) for k in range(12)]
+
+
+def correct(even_x, even_y, value, old, new, seen):
     low, high = eta_pair()
-    west, east_side = value[0] * low + value[2] * high, value[1] * low + value[3] * high
-    sx1, sx2, sy1, sy2 = sends
-    for i in range(CX):
-        now = u[i] + ((1.0 - row_at(i)) * west + row_at(i) * east_side)
-        new[i] = now
-        south, north_row = now[:1], now[CY - 1 :]
-        sy1[i : i + 1, :] = jnp.where(even_y, north_row, south)
-        sy2[i : i + 1, :] = jnp.where(even_y, south, north_row)
-        if i == 0:
-            first = now
-    sx1[...] = jnp.where(even_x, now, first)
-    sx2[...] = jnp.where(even_x, first, now)
-
-
-def make_correct(final):
-    def kernel(every, own, east, y1, y2, corner, u, new, sx1, sx2, sy1, sy2, *more):
-        if final:
-            solution_out, shifted, rows, north = more
-        else:
-            shifted, rows, north = more
-        _, even_y, _ = place()
-        north[...] = sided(even_y, y1[...], y2[...])[1]
-        correct(every, own, east, north, corner, u, shifted, rows, new, (sx1, sx2, sy1, sy2))
-        if final:
-            solution_out[...] = new[...].astype(jnp.bfloat16)
-
-    return kernel
-
-
-def second_kernel(right, robin_table, robin_index, kap, old, x2, x1, y1, y2, u, out, source, sums):
+    v00, v10, v01, v11, w0, w1, e0, e1, s0, s1, n0, n1 = value
+    ramp = lambda first, second: first * low + second * high
+    west, east, south, north = ramp(v00, v01), ramp(v10, v11), ramp(v00, v10), ramp(v01, v11)
+    for i in range(CX):
+        new[i] = old[i] + ((1.0 - row_at(i)) * west + row_at(i) * east)
+    seen_x = sided(even_x, seen[1][0:CY], seen[0][0:CY])
+    seen_y = sided(even_y, seen[2][0:CX], seen[3][0:CX])
+    return (
+        seen_x[0] + (NEAR * ramp(w0, w1) + FAR * west),
+        seen_x[1] + (FAR * east + NEAR * ramp(e0, e1)),
+        seen_y[0] + (NEAR * ramp(s0, s1) + FAR * south),
+        seen_y[1] + (FAR * north + NEAR * ramp(n0, n1)),
+    )
+
+
+def second_kernel(
+    right, robin_table, robin_index, kap, old, every, own, x2, x1, y1, y2, far, q2, q1, r1, r2,
+    u, out, shifted, fx2, fx1, fy1, fy2, rows, source, sums,
+):
     even_x, even_y, inside = place()
-    west, east = sided(even_x, x1[...], x2[...])
-    south, north = sided(even_y, y1[...], y2[...])
+    seen = (q2, q1, r1, r2)
+    widen(even_x, even_y, (own, x2, x1, y1, y2), far, seen, rows, shifted)
+    value = window(every, shifted)
+    west, east, south, north = correct(even_x, even_y, value, old, u, seen)
     robin = robin_of(robin_index, robin_table)
     coef = Coefficients(kap)
     for i in range(CX):
-        a, here = i // BLOCK, old[i]
-        u[i] = here
+        a, here = i // BLOCK, u[i]
         total = right[i]
         trace = inside[2] * (coef.south[a] * south[i : i + 1] + robin[1] * here)
         total = total + jnp.where(coef.at_y == 0, trace, 0.0)
@@ -281,12 +322,13 @@
         source[i] = total
     relax(coef, inside, robin, u, source, False)
     contribute(coef, inside, u, right, sums, out)
-
-
-def last_kernel(right, kap, u, x2, x1, y1, y2, out):
+    faces(even_x, even_y, u, (fx2, fx1, fy1, fy2))
+
+
+def last_kernel(right, kap, old, every, shifted, q2, q1, r1, r2, answer, out, u):
     even_x, even_y, inside = place()
-    west, east = sided(even_x, x1[...], x2[...])
-    south, north = sided(even_y, y1[...], y2[...])
+    value = window(every, shifted)
+    west, east, south, north = correct(even_x, even_y, value, old, u, (q2, q1, r1, r2))
     coef = Coefficients(kap)
     for i in range(CX):
         a = i // BLOCK
@@ -298,6 +340,7 @@
         if i == CX - 1:
             left = left + inside[1] * coef.x[CX] * east
         out[i] = left.astype(jnp.bfloat16)
+        answer[i] = u[i].astype(jnp.bfloat16)
 
 
 def call(kernel, out_shape, spaces, scratch=()):
@@ -319,7 +362,7 @@
     return pairs
 
 
-def swaps(sx1, sx2, sy1, sy2):
+def swaps(sx2, sx1, sy1, sy2):
     wide_count, narrow_count = lax.axis_size("wide"), lax.axis_size("narrow")
     x2 = lax.ppermute(sx2, "wide", swap_pairs(wide_count, 1))
     x1 = lax.ppermute(sx1, "wide", swap_pairs(wide_count, 0))
@@ -334,38 +377,38 @@
 
 def body(right_side, labels, material_table, robin_table, robin_index, coarse_rows):
     count = coarse_rows.shape[1]
+    narrow_count = lax.axis_size("narrow")
     shape = lambda *dims: jax.ShapeDtypeStruct(dims, F32)
+    scratch = lambda *dims: pltpu.VMEM(dims, F32)
     field, face, gathered = shape(CX, CY, NZ), shape(CY, NZ), shape(count, NZ)
-    pay_shape = shape(8, NZ)
     index = robin_index[0, 0]
-    pay = call(pack_kernel, pay_shape, [VMEM] * 2)(labels, coarse_rows)
+    pay = call(pack_kernel, shape(8, NZ), [VMEM] * 2)(labels, coarse_rows)
     x2, x1, y1, y2 = swaps(pay, pay, pay, pay)
-    u, sent, kap, east = call(
+    both = call(join_kernel, shape(16, NZ), [VMEM] * 2)(x1, x2)
+    far = lax.ppermute(both, "narrow", [(i + 1, i) for i in range(narrow_count - 1)])
+    u, sent, kap, *edges = call(
         first_kernel,
-        (field, gathered, shape(16, NZ), pay_shape),
+        (field, gathered, shape(16, NZ), face, face, face, face),
         [VMEM] + [SMEM] * 3 + [VMEM] * 5,
-        [pltpu.VMEM((16, NZ), F32)],
+        [scratch(16, NZ)],
     )(right_side, material_table, robin_table, index, pay, y2, y1, x1, x2)
-    narrow_count = lax.axis_size("narrow")
-    corner = lax.ppermute(east, "narrow", [(i + 1, i) for i in range(narrow_count - 1)])
-    work = [pltpu.VMEM((8 * len(SHIFTS), count), F32), pltpu.VMEM((8, count), F32), pltpu.VMEM((8, NZ), F32)]
-    u, *faces = call(make_correct(False), (field, face, face, face, face), [VMEM] * 7, work)(
-        everywhere(sent), pay, east, y1, y2, corner, u
-    )
-    seen = swaps(*faces)
-    u, sent = call(
+    every = everywhere(sent)
+    edges = call(
+        ride_kernel, (shape(CY + 8, NZ),) * 2 + (shape(CX + 16, NZ),) * 2, [VMEM] * 9
+    )(x2, x1, y1, y2, far, *edges)
+    seen = swaps(*edges)
+    u, sent, shifted, *edges = call(
         second_kernel,
-        (field, gathered),
-        [VMEM] + [SMEM] * 2 + [VMEM] * 6,
-        [pltpu.VMEM((CX, CY, NZ), F32), pltpu.VMEM((16, NZ), F32)],
-    )(right_side, robin_table, index, kap, u, *seen)
+        (field, gathered, shape(16 * len(SHIFTS), count), face, face, face, face),
+        [VMEM] + [SMEM] * 2 + [VMEM] * 13,
+        [scratch(16, count), scratch(CX, CY, NZ), scratch(16, NZ)],
+    )(right_side, robin_table, index, kap, u, every, pay, x2, x1, y1, y2, far, *seen)
+    every = everywhere(sent)
+    seen = swaps(*edges)
     half = jax.ShapeDtypeStruct((CX, CY, NZ), jnp.bfloat16)
-    u, f1, f2, f3, f4, answer = call(
-        make_correct(True), (field, face, face, face, face, half), [VMEM] * 7, work
-    )(everywhere(sent), pay, east, y1, y2, corner, u)
-    seen = swaps(f1, f2, f3, f4)
-    leftover = call(last_kernel, half, [VMEM] * 7)(right_side, kap, u, *seen)
-    return (answer, leftover)
+    return call(last_kernel, (half, half), [VMEM] * 9, [scratch(CX, CY, NZ)])(
+        right_side, kap, u, every, shifted, *seen
+    )
 
 
 def solution(mesh):

time: 141 us -> 124 us (0.88)
  the two profiles are of different devices: /device:TPU:31 before, /device:TPU:1 now
where the time goes in v3:
time: 124 us; the launch traced here: 123 us
  starting transfers between devices  81.9 us (66%)
  waiting for transfers between devices  31.4 us (25%)
  Pallas kernels  6.9 us (6%)
  local copies, waits for them, and re-layouts  2.27 us (2%)
    all_to_all x2, starting transfers between devices, everywhere(): return lax.all_to_all(values, ('wide', 'narrow'), 0, 0, tiled=True)  50.5 us
    all_to_all x2, waiting for transfers between devices, everywhere(): return lax.all_to_all(values, ('wide', 'narrow'), 0, 0, tiled=True)  18.9 us
    ppermute x3, starting transfers between devices, swaps(): x2 = lax.ppermute(sx2, 'wide', swap_pairs(wide_count, 1))  12.2 us
    ppermute x3, starting transfers between devices, swaps(): x1 = lax.ppermute(sx1, 'wide', swap_pairs(wide_count, 0))  10.2 us
    ppermute x1, waiting for transfers between devices, body(): lax.ppermute(both, 'narrow', [(i + 1, i) for i in range(narrow_count - 1)])  7.42 us
    ppermute x3, starting transfers between devices, swaps(): y1 = lax.ppermute(sy1, 'narrow', swap_pairs(narrow_count, 0))  5.76 us
    ppermute x3, waiting for transfers between devices, swaps(): y1 = lax.ppermute(sy1, 'narrow', swap_pairs(narrow_count, 0))  3.88 us
    pallas_call x1, Pallas kernels, body(): call(second_kernel, (field, gathered, shape(16 * len(SHIFTS), count), fac...  2.96 us
  transfers between devices with their start and end apart: 15, of which 6 were waited for; matrix products, arithmetic and copies ran while one was open for 0% of the time, Pallas kernels for 0%

profile of v3, /device:TPU:1, one launch (start us, length us, event | category | flops | bytes accessed | tf_op | source)
XLA Modules:
  0.0 123.3 jit_solution(13531225664238972739)
XLA Ops:
  0.6 0.0 copy-start.4
  0.6 0.7 copy-done.4
  1.3 0.0 copy-start.5
  1.3 0.7 copy-done.5
  2.0 0.0 copy-start.2
  2.0 0.0 copy-start.3
  2.0 0.0 copy-start.6
  2.0 4.6 %collective-permute-start.3 = (f32[8,128]{1,0:T(8,128)S(1)}, f32[8,128]{1,0:T(8,128)S(1)}, u32[]{:S(2)}, u32[]{:S(2)}) collective-permute-start(f32[8,128]{1,0:T(8,128)S(1)} %shard_map.77.own), channel_id=1, source_target_pairs={{8,16},{16,8},{24,32},{32,24},{40,48},{48,40},{56,64},{64,56},{72,... | collective-permute-start | bytes 12296 | tf_op jit(solution)/shard_map/ppermute | solution.py:367
  6.6 4.9 %collective-permute-start.2 = (f32[8,128]{1,0:T(8,128)S(1)}, f32[8,128]{1,0:T(8,128)S(1)}, u32[]{:S(2)}, u32[]{:S(2)}) collective-permute-start(f32[8,128]{1,0:T(8,128)S(1)} %shard_map.77.own), channel_id=1, source_target_pairs={{0,8},{8,0},{16,24},{24,16},{32,40},{40,32},{48,56},{56,48},{64,72... | collective-permute-start | bytes 12296 | tf_op jit(solution)/shard_map/ppermute | solution.py:368
  11.6 1.9 %collective-permute-start.1 = (f32[8,128]{1,0:T(8,128)S(1)}, f32[8,128]{1,0:T(8,128)S(1)}, u32[]{:S(2)}, u32[]{:S(2)}) collective-permute-start(f32[8,128]{1,0:T(8,128)S(1)} %shard_map.77.own), channel_id=1, source_target_pairs={{0,1},{1,0},{2,3},{3,2},{4,5},{5,4},{6,7},{7,6},{8,9},{9,8},{10,11... | collective-permute-start | bytes 12296 | tf_op jit(solution)/shard_map/ppermute | solution.py:369
  13.5 0.7 collective-permute-start
  14.2 0.0 collective-permute-done.3.x2
  14.2 0.0 collective-permute-done.2.x1
  14.2 1.7 %collective-permute-done.1.y1 = f32[8,128]{1,0:T(8,128)S(1)} collective-permute-done((f32[8,128]{1,0:T(8,128)S(1)}, f32[8,128]{1,0:T(8,128)S(1)}, u32[]{:S(2)}, u32[]{:S(2)}) %collective-permute-start.1) | collective-permute-done | bytes 4128 | tf_op jit(solution)/shard_map/ppermute | solution.py:369
  15.9 0.0 collective-permute-done.y2
  15.9 0.0 copy-done.2
  15.9 0.0 copy-done.3
  15.9 0.0 copy-done.6
  15.9 0.0 copy-start
  16.0 0.9 copy-done
  16.8 2.6 %shard_map.78 = (f32[16,16,128]{2,1,0:T(8,128)S(1)}, f32[512,128]{1,0:T(8,128)}, f32[16,128]{1,0:T(8,128)S(1)}, f32[16,128]{1,0:T(8,128)S(1)}, f32[16,128]{1,0:T...) custom-call(f32[16,16,128]{2,1,0:T(8,128)S(1)} %copy-done, f32[16]{0:T(128)S(1)} %copy-done.6, f32[8]{0:T(128)S(1)} %copy-done.2, ...), custom_call_target="tpu_custom_call" | custom-call | tf_op jit(solution)/shard_map/pallas_call | solution.py:389
  19.4 0.0 copy-start.1
  19.4 25.6 %all-to-all-start = ((f32[512,1,128]{2,1,0:T(1,128)}), f32[512,1,128]{2,1,0:T(1,128)S(1)}, u32[]{:S(2)}, u32[]{:S(2)}) async-start(f32[512,1,128]{2,1,0:T(1,128)} %bitcast.2), calls=%async_computation | async-start | bytes 524288 | tf_op jit(solution)/shard_map/all_to_all | solution.py:375
  45.0 1.3 %collective-permute-start.4 = (f32[16,128]{1,0:T(8,128)S(1)}, f32[16,128]{1,0:T(8,128)S(1)}, u32[]{:S(2)}, u32[]{:S(2)}) collective-permute-start(f32[16,128]{1,0:T(8,128)S(1)} %shard_map.79), channel_id=1, source_target_pairs={{1,0},{2,1},{3,2},{4,3},{5,4},{6,5},{7,6},{9,8},{10,9},{11,10},{12... | collective-permute-start | bytes 24584 | tf_op jit(solution)/shard_map/ppermute | solution.py:388
  46.3 7.4 %collective-permute-done.4.far = f32[16,128]{1,0:T(8,128)S(1)} collective-permute-done((f32[16,128]{1,0:T(8,128)S(1)}, f32[16,128]{1,0:T(8,128)S(1)}, u32[]{:S(2)}, u32[]{:S(2)}) %collective-permute-start.4) | collective-permute-done | bytes 8224 | tf_op jit(solution)/shard_map/ppermute | solution.py:388
  53.8 1.9 %collective-permute-start.7 = (f32[32,128]{1,0:T(8,128)S(1)}, f32[32,128]{1,0:T(8,128)S(1)}, u32[]{:S(2)}, u32[]{:S(2)}) collective-permute-start(f32[32,128]{1,0:T(8,128)S(1)} %get-tuple-element.29), channel_id=1, source_target_pairs={{0,1},{1,0},{2,3},{3,2},{4,5},{5,4},{6,7},{7,6},{8,9},{9,8},{10,11... | collective-permute-start | bytes 49160 | tf_op jit(solution)/shard_map/ppermute | solution.py:369
  55.7 0.7 collective-permute-start.8
  56.4 4.1 %collective-permute-start.5 = (f32[24,128]{1,0:T(8,128)S(1)}, f32[24,128]{1,0:T(8,128)S(1)}, u32[]{:S(2)}, u32[]{:S(2)}) collective-permute-start(f32[24,128]{1,0:T(8,128)S(1)} %get-tuple-element.27), channel_id=1, source_target_pairs={{8,16},{16,8},{24,32},{32,24},{40,48},{48,40},{56,64},{64,56},{72,... | collective-permute-start | bytes 36872 | tf_op jit(solution)/shard_map/ppermute | solution.py:367
  60.4 1.9 %collective-permute-start.6 = (f32[24,128]{1,0:T(8,128)S(1)}, f32[24,128]{1,0:T(8,128)S(1)}, u32[]{:S(2)}, u32[]{:S(2)}) collective-permute-start(f32[24,128]{1,0:T(8,128)S(1)} %get-tuple-element.28), channel_id=1, source_target_pairs={{0,8},{8,0},{16,24},{24,16},{32,40},{40,32},{48,56},{56,48},{64,72... | collective-permute-start | bytes 36872 | tf_op jit(solution)/shard_map/ppermute | solution.py:368
  62.4 0.0 collective-permute-done.5.q2
  62.4 1.1 collective-permute-done.6.q1
  63.5 0.0 collective-permute-done.7.r1
  63.5 0.0 collective-permute-done.8.r2
  63.5 6.0 %all-to-all-done = f32[512,1,128]{2,1,0:T(1,128)S(1)} async-done(((f32[512,1,128]{2,1,0:T(1,128)}), f32[512,1,128]{2,1,0:T(1,128)S(1)}, u32[]{:S(2)}, u32[]{:S(2)}) %all-to-all-start) | async-done | bytes 262176 | tf_op jit(solution)/shard_map/all_to_all | solution.py:375
  69.5 0.0 copy-done.1
  69.5 3.0 %shard_map.81 = (f32[16,16,128]{2,1,0:T(8,128)S(1)}, f32[512,128]{1,0:T(8,128)}, f32[192,512]{1,0:T(8,128)S(1)}, f32[16,128]{1,0:T(8,128)S(1)}, f32[16,128]{1,0:...) custom-call(f32[16,16,128]{2,1,0:T(8,128)S(1)} %copy-done.1, f32[8]{0:T(128)S(1)} %copy-done.2, ...), custom_call_target="tpu_custom_call" | custom-call | tf_op jit(solution)/shard_map/pallas_call | solution.py:400
  72.5 24.8 %all-to-all-start.1 = ((f32[512,1,128]{2,1,0:T(1,128)}), f32[512,1,128]{2,1,0:T(1,128)S(1)}, u32[]{:S(2)}, u32[]{:S(2)}) async-start(f32[512,1,128]{2,1,0:T(1,128)} %bitcast.5), calls=%async_computation.1 | async-start | bytes 524288 | tf_op jit(solution)/shard_map/all_to_all | solution.py:375
  97.3 3.5 %collective-permute-start.9 = (f32[16,128]{1,0:T(8,128)S(1)}, f32[16,128]{1,0:T(8,128)S(1)}, u32[]{:S(2)}, u32[]{:S(2)}) collective-permute-start(f32[16,128]{1,0:T(8,128)S(1)} %get-tuple-element.34), channel_id=1, source_target_pairs={{8,16},{16,8},{24,32},{32,24},{40,48},{48,40},{56,64},{64,56},{72,... | collective-permute-start | bytes 24584 | tf_op jit(solution)/shard_map/ppermute | solution.py:367
  100.9 3.3 %collective-permute-start.10 = (f32[16,128]{1,0:T(8,128)S(1)}, f32[16,128]{1,0:T(8,128)S(1)}, u32[]{:S(2)}, u32[]{:S(2)}) collective-permute-start(f32[16,128]{1,0:T(8,128)S(1)} %get-tuple-element.35), channel_id=1, source_target_pairs={{0,8},{8,0},{16,24},{24,16},{32,40},{40,32},{48,56},{56,48},{64,72... | collective-permute-start | bytes 24584 | tf_op jit(solution)/shard_map/ppermute | solution.py:368
  104.2 1.9 %collective-permute-start.11 = (f32[16,128]{1,0:T(8,128)S(1)}, f32[16,128]{1,0:T(8,128)S(1)}, u32[]{:S(2)}, u32[]{:S(2)}) collective-permute-start(f32[16,128]{1,0:T(8,128)S(1)} %get-tuple-element.36), channel_id=1, source_target_pairs={{0,1},{1,0},{2,3},{3,2},{4,5},{5,4},{6,7},{7,6},{8,9},{9,8},{10,11... | collective-permute-start | bytes 24584 | tf_op jit(solution)/shard_map/ppermute | solution.py:369
  106.2 0.7 collective-permute-start.12
  106.8 0.0 collective-permute-done.9.q2
  106.8 0.0 collective-permute-done.10.q1
  106.9 2.1 %collective-permute-done.11.r1 = f32[16,128]{1,0:T(8,128)S(1)} collective-permute-done((f32[16,128]{1,0:T(8,128)S(1)}, f32[16,128]{1,0:T(8,128)S(1)}, u32[]{:S(2)}, u32[]{:S(2)}) %collective-permute-start.11) | collective-permute-done | bytes 8224 | tf_op jit(solution)/shard_map/ppermute | solution.py:369
  109.0 0.0 collective-permute-done.12.r2
  109.0 12.9 %all-to-all-done.1 = f32[512,1,128]{2,1,0:T(1,128)S(1)} async-done(((f32[512,1,128]{2,1,0:T(1,128)}), f32[512,1,128]{2,1,0:T(1,128)S(1)}, u32[]{:S(2)}, u32[]{:S(2)}) %all-to-all-start.1) | async-done | bytes 262176 | tf_op jit(solution)/shard_map/all_to_all | solution.py:375
  121.9 1.4 %shard_map.82 = (bf16[16,16,128]{2,1,0:T(8,128)(2,1)}, bf16[16,16,128]{2,1,0:T(8,128)(2,1)}) custom-call(f32[16,16,128]{2,1,0:T(8,128)S(1)} %copy-done.1, f32[16,128]{1,0:T(8,128)S(1)} %get-tuple-element.20.kap, f32[16,16,128]{2,1,0:T(8,128)S(1)} %get-tuple-element.31.old, f32[512,128]{1,0:T(8,128)S(1)} %bitcast.10, ...), custom_call_target="tpu_custom_call" | custom-call | tf_op jit(solution)/shard_map/pallas_call | solution.py:409
  (3 shorter events, 0.0 us)
Async XLA Ops:
  0.6 0.7 copy-start.4
  1.3 0.7 copy-start.5
  2.0 13.9 %copy-start.2 = (f32[8]{0:T(128)S(1)}, f32[8]{0:T(128)}, u32[]{:S(2)}) copy-start(f32[8]{0:T(128)} %robin_table.3) | copy-start | bytes 100
  2.0 13.9 %copy-start.3 = (s32[1,1,2]{2,1,0:T(1,128)S(1)}, s32[1,1,2]{2,1,0:T(1,128)}, u32[]{:S(2)}) copy-start(s32[1,1,2]{2,1,0:T(1,128)} %param.10) | copy-start | bytes 28
  2.0 13.9 %copy-start.6 = (f32[16]{0:T(128)S(1)}, f32[16]{0:T(128)}, u32[]{:S(2)}) copy-start(f32[16]{0:T(128)} %table.1) | copy-start | bytes 196
  2.0 12.2 %collective-permute-start.3 = (f32[8,128]{1,0:T(8,128)S(1)}, f32[8,128]{1,0:T(8,128)S(1)}, u32[]{:S(2)}, u32[]{:S(2)}) collective-permute-start(f32[8,128]{1,0:T(8,128)S(1)} %shard_map.77.own), channel_id=1, source_target_pairs={{8,16},{16,8},{24,32},{32,24},{40,48},{48,40},{56,64},{64,56},{72,... | collective-permute-start | bytes 12296 | tf_op jit(solution)/shard_map/ppermute | solution.py:367
  6.6 7.5 %collective-permute-start.2 = (f32[8,128]{1,0:T(8,128)S(1)}, f32[8,128]{1,0:T(8,128)S(1)}, u32[]{:S(2)}, u32[]{:S(2)}) collective-permute-start(f32[8,128]{1,0:T(8,128)S(1)} %shard_map.77.own), channel_id=1, source_target_pairs={{0,8},{8,0},{16,24},{24,16},{32,40},{40,32},{48,56},{56,48},{64,72... | collective-permute-start | bytes 12296 | tf_op jit(solution)/shard_map/ppermute | solution.py:368
  11.6 4.4 %collective-permute-start.1 = (f32[8,128]{1,0:T(8,128)S(1)}, f32[8,128]{1,0:T(8,128)S(1)}, u32[]{:S(2)}, u32[]{:S(2)}) collective-permute-start(f32[8,128]{1,0:T(8,128)S(1)} %shard_map.77.own), channel_id=1, source_target_pairs={{0,1},{1,0},{2,3},{3,2},{4,5},{5,4},{6,7},{7,6},{8,9},{9,8},{10,11... | collective-permute-start | bytes 12296 | tf_op jit(solution)/shard_map/ppermute | solution.py:369
  13.5 2.4 %collective-permute-start = (f32[8,128]{1,0:T(8,128)S(1)}, f32[8,128]{1,0:T(8,128)S(1)}, u32[]{:S(2)}, u32[]{:S(2)}) collective-permute-start(f32[8,128]{1,0:T(8,128)S(1)} %shard_map.77.own), channel_id=1, source_target_pairs={{1,2},{2,1},{3,4},{4,3},{5,6},{6,5},{9,10},{10,9},{11,12},{12,11},... | collective-permute-start | bytes 12296 | tf_op jit(solution)/shard_map/ppermute | solution.py:370
  15.9 0.9 copy-start
  19.4 50.1 %copy-start.1 = (f32[16,16,128]{2,1,0:T(8,128)S(1)}, f32[16,16,128]{2,1,0:T(8,128)}, u32[]{:S(2)}) copy-start(f32[16,16,128]{2,1,0:T(8,128)} %right.5) | copy-start | bytes 393220
  19.4 50.1 %all-to-all-start = ((f32[512,1,128]{2,1,0:T(1,128)}), f32[512,1,128]{2,1,0:T(1,128)S(1)}, u32[]{:S(2)}, u32[]{:S(2)}) async-start(f32[512,1,128]{2,1,0:T(1,128)} %bitcast.2), calls=%async_computation | async-start | bytes 524288 | tf_op jit(solution)/shard_map/all_to_all | solution.py:375
  45.0 8.7 %collective-permute-start.4 = (f32[16,128]{1,0:T(8,128)S(1)}, f32[16,128]{1,0:T(8,128)S(1)}, u32[]{:S(2)}, u32[]{:S(2)}) collective-permute-start(f32[16,128]{1,0:T(8,128)S(1)} %shard_map.79), channel_id=1, source_target_pairs={{1,0},{2,1},{3,2},{4,3},{5,4},{6,5},{7,6},{9,8},{10,9},{11,10},{12... | collective-permute-start | bytes 24584 | tf_op jit(solution)/shard_map/ppermute | solution.py:388
  53.8 9.8 %collective-permute-start.7 = (f32[32,128]{1,0:T(8,128)S(1)}, f32[32,128]{1,0:T(8,128)S(1)}, u32[]{:S(2)}, u32[]{:S(2)}) collective-permute-start(f32[32,128]{1,0:T(8,128)S(1)} %get-tuple-element.29), channel_id=1, source_target_pairs={{0,1},{1,0},{2,3},{3,2},{4,5},{5,4},{6,7},{7,6},{8,9},{9,8},{10,11... | collective-permute-start | bytes 49160 | tf_op jit(solution)/shard_map/ppermute | solution.py:369
  55.7 7.8 %collective-permute-start.8 = (f32[32,128]{1,0:T(8,128)S(1)}, f32[32,128]{1,0:T(8,128)S(1)}, u32[]{:S(2)}, u32[]{:S(2)}) collective-permute-start(f32[32,128]{1,0:T(8,128)S(1)} %get-tuple-element.30), channel_id=1, source_target_pairs={{1,2},{2,1},{3,4},{4,3},{5,6},{6,5},{9,10},{10,9},{11,12},{12,11},... | collective-permute-start | bytes 49160 | tf_op jit(solution)/shard_map/ppermute | solution.py:370
  56.4 6.0 %collective-permute-start.5 = (f32[24,128]{1,0:T(8,128)S(1)}, f32[24,128]{1,0:T(8,128)S(1)}, u32[]{:S(2)}, u32[]{:S(2)}) collective-permute-start(f32[24,128]{1,0:T(8,128)S(1)} %get-tuple-element.27), channel_id=1, source_target_pairs={{8,16},{16,8},{24,32},{32,24},{40,48},{48,40},{56,64},{64,56},{72,... | collective-permute-start | bytes 36872 | tf_op jit(solution)/shard_map/ppermute | solution.py:367
  60.4 3.1 %collective-permute-start.6 = (f32[24,128]{1,0:T(8,128)S(1)}, f32[24,128]{1,0:T(8,128)S(1)}, u32[]{:S(2)}, u32[]{:S(2)}) collective-permute-start(f32[24,128]{1,0:T(8,128)S(1)} %get-tuple-element.28), channel_id=1, source_target_pairs={{0,8},{8,0},{16,24},{24,16},{32,40},{40,32},{48,56},{56,48},{64,72... | collective-permute-start | bytes 36872 | tf_op jit(solution)/shard_map/ppermute | solution.py:368
  72.5 49.4 %all-to-all-start.1 = ((f32[512,1,128]{2,1,0:T(1,128)}), f32[512,1,128]{2,1,0:T(1,128)S(1)}, u32[]{:S(2)}, u32[]{:S(2)}) async-start(f32[512,1,128]{2,1,0:T(1,128)} %bitcast.5), calls=%async_computation.1 | async-start | bytes 524288 | tf_op jit(solution)/shard_map/all_to_all | solution.py:375
  97.3 9.5 %collective-permute-start.9 = (f32[16,128]{1,0:T(8,128)S(1)}, f32[16,128]{1,0:T(8,128)S(1)}, u32[]{:S(2)}, u32[]{:S(2)}) collective-permute-start(f32[16,128]{1,0:T(8,128)S(1)} %get-tuple-element.34), channel_id=1, source_target_pairs={{8,16},{16,8},{24,32},{32,24},{40,48},{48,40},{56,64},{64,56},{72,... | collective-permute-start | bytes 24584 | tf_op jit(solution)/shard_map/ppermute | solution.py:367
  100.9 6.0 %collective-permute-start.10 = (f32[16,128]{1,0:T(8,128)S(1)}, f32[16,128]{1,0:T(8,128)S(1)}, u32[]{:S(2)}, u32[]{:S(2)}) collective-permute-start(f32[16,128]{1,0:T(8,128)S(1)} %get-tuple-element.35), channel_id=1, source_target_pairs={{0,8},{8,0},{16,24},{24,16},{32,40},{40,32},{48,56},{56,48},{64,72... | collective-permute-start | bytes 24584 | tf_op jit(solution)/shard_map/ppermute | solution.py:368
  104.2 4.8 %collective-permute-start.11 = (f32[16,128]{1,0:T(8,128)S(1)}, f32[16,128]{1,0:T(8,128)S(1)}, u32[]{:S(2)}, u32[]{:S(2)}) collective-permute-start(f32[16,128]{1,0:T(8,128)S(1)} %get-tuple-element.36), channel_id=1, source_target_pairs={{0,1},{1,0},{2,3},{3,2},{4,5},{5,4},{6,7},{7,6},{8,9},{9,8},{10,11... | collective-permute-start | bytes 24584 | tf_op jit(solution)/shard_map/ppermute | solution.py:369
  106.2 2.8 %collective-permute-start.12 = (f32[16,128]{1,0:T(8,128)S(1)}, f32[16,128]{1,0:T(8,128)S(1)}, u32[]{:S(2)}, u32[]{:S(2)}) collective-permute-start(f32[16,128]{1,0:T(8,128)S(1)} %get-tuple-element.37), channel_id=1, source_target_pairs={{1,2},{2,1},{3,4},{4,3},{5,6},{6,5},{9,10},{10,9},{11,12},{12,11},... | collective-permute-start | bytes 24584 | tf_op jit(solution)/shard_map/ppermute | solution.py:370

commit v4 on v3

--- a/solution.py
+++ b/solution.py
@@ -183,7 +183,10 @@
         pay[4 + c : 5 + c, :] = row[:, c * NZ : (c + 1) * NZ]
 
 
-def first_kernel(right, table, robin_table, robin_index, own, y2, y1, x1, x2, u, out, kap, fx2, fx1, fy1, fy2, sums):
+def first_kernel(
+    right, table, robin_table, robin_index, own, y2, y1, x1, x2,
+    u, out, kap, fx2, fx1, fy1, fy2, sums,
+):
     even_x, even_y, inside = place()
     from_west, from_east = sided(even_x, x1[...], x2[...])
     from_south, from_north = sided(even_y, y1[...], y2[...])
@@ -217,44 +220,43 @@
     sx2[0:CY, :] = jnp.where(even_x, u[0], u[CX - 1])
 
 
-def join_kernel(x1, x2, out):
-    out[0:8, :] = x1[...]
-    out[8:16, :] = x2[...]
-
-
-def ride_kernel(x2, x1, y1, y2, far, fx2, fx1, fy1, fy2, px2, px1, py1, py2):
+def ride_y_kernel(x2, x1, y1, y2, fy1, fy2, py1, py2):
+    even_x, even_y, _ = place()
+    west, east = (p[4:8] for p in sided(even_x, x1[...], x2[...]))
+    north = sided(even_y, y1[...], y2[...])[1][4:8]
+    for out, face in ((py1, fy1), (py2, fy2)):
+        out[0:CX, :] = face[...]
+        for k, piece in enumerate((north, east, west, jnp.zeros((4, NZ), F32))):
+            out[CX + 4 * k : CX + 4 * k + 4, :] = piece
+
+
+def ride_x_kernel(x2, x1, r1, r2, fx2, fx1, px2, px1):
     even_x, even_y, _ = place()
     east = sided(even_x, x1[...], x2[...])[1][4:8]
-    north = sided(even_y, y1[...], y2[...])[1][4:8]
-    corner = sided(even_x, far[0:8], far[8:16])[1][4:8]
+    above = sided(even_y, r1[...], r2[...])[1]
     for out, face in ((px2, fx2), (px1, fx1)):
         out[0:CY, :] = face[...]
-        out[CY : CY + 4, :] = east
-        out[CY + 4 : CY + 8, :] = corner
-    for out, face in ((py1, fy1), (py2, fy2)):
-        out[0:CX, :] = face[...]
-        out[CX : CX + 4, :] = north
-        out[CX + 4 : CX + 8, :] = corner
-        out[CX + 8 : CX + 12, :] = east
-        out[CX + 12 : CX + 16, :] = jnp.zeros((4, NZ), F32)
-
-
-def widen(even_x, even_y, pays, far, seen, rows, shifted):
-    own, x2, x1, y1, y2 = pays
+        pieces = (east, above[CX + 4 : CX + 8], above[CX : CX + 4], jnp.zeros((4, NZ), F32))
+        for k, piece in enumerate(pieces):
+            out[CY + 4 * k : CY + 4 * k + 4, :] = piece
+
+
+def widen_kernel(own, x2, x1, y1, y2, q2, q1, r1, r2, shifted, rows):
+    even_x, even_y, _ = place()
     count = rows.shape[1]
     narrow_count = lax.axis_size("narrow")
     wide_count = count // narrow_count
     west, east = (p[4:8] for p in sided(even_x, x1[...], x2[...]))
     south, north = (p[4:8] for p in sided(even_y, y1[...], y2[...]))
-    corners = [p[4:8] for p in sided(even_x, far[0:8], far[8:16])]
-    beyond_x = sided(even_x, seen[1][...], seen[0][...])[1]
-    below, above = sided(even_y, seen[2][...], seen[3][...])
+    beyond = sided(even_x, q1[...], q2[...])[1]
+    below, above = sided(even_y, r1[...], r2[...])
+    taken = lambda value, k: value[CX + 4 * k : CX + 4 * k + 4]
     held = (
-        own[4:8], east, north, corners[1],
-        west, corners[0],
-        beyond_x[CY : CY + 4], beyond_x[CY + 4 : CY + 8],
-        south, below[CX + 8 : CX + 12],
-        above[CX : CX + 4], above[CX + 4 : CX + 8],
+        own[4:8], east, north, taken(above, 1),
+        west, taken(above, 2),
+        taken(beyond, 0), taken(beyond, 1),
+        south, taken(below, 1),
+        taken(above, 0), taken(beyond, 2),
     )
     rows[...] = jnp.zeros_like(rows)
     for k, piece in enumerate(held):
@@ -298,12 +300,11 @@
 
 
 def second_kernel(
-    right, robin_table, robin_index, kap, old, every, own, x2, x1, y1, y2, far, q2, q1, r1, r2,
-    u, out, shifted, fx2, fx1, fy1, fy2, rows, source, sums,
+    right, robin_table, robin_index, kap, old, every, shifted, q2, q1, r1, r2,
+    u, out, fx2, fx1, fy1, fy2, source, sums,
 ):
     even_x, even_y, inside = place()
     seen = (q2, q1, r1, r2)
-    widen(even_x, even_y, (own, x2, x1, y1, y2), far, seen, rows, shifted)
     value = window(every, shifted)
     west, east, south, north = correct(even_x, even_y, value, old, u, seen)
     robin = robin_of(robin_index, robin_table)
@@ -362,12 +363,15 @@
     return pairs
 
 
+def swap(array, axis, start):
+    return lax.ppermute(array, axis, swap_pairs(lax.axis_size(axis), start))
+
+
 def swaps(sx2, sx1, sy1, sy2):
-    wide_count, narrow_count = lax.axis_size("wide"), lax.axis_size("narrow")
-    x2 = lax.ppermute(sx2, "wide", swap_pairs(wide_count, 1))
-    x1 = lax.ppermute(sx1, "wide", swap_pairs(wide_count, 0))
-    y1 = lax.ppermute(sy1, "narrow", swap_pairs(narrow_count, 0))
-    y2 = lax.ppermute(sy2, "narrow", swap_pairs(narrow_count, 1))
+    x2 = swap(sx2, "wide", 1)
+    x1 = swap(sx1, "wide", 0)
+    y1 = swap(sy1, "narrow", 0)
+    y2 = swap(sy2, "narrow", 1)
     return x2, x1, y1, y2
 
 
@@ -377,32 +381,34 @@
 
 def body(right_side, labels, material_table, robin_table, robin_index, coarse_rows):
     count = coarse_rows.shape[1]
-    narrow_count = lax.axis_size("narrow")
     shape = lambda *dims: jax.ShapeDtypeStruct(dims, F32)
     scratch = lambda *dims: pltpu.VMEM(dims, F32)
     field, face, gathered = shape(CX, CY, NZ), shape(CY, NZ), shape(count, NZ)
     index = robin_index[0, 0]
     pay = call(pack_kernel, shape(8, NZ), [VMEM] * 2)(labels, coarse_rows)
     x2, x1, y1, y2 = swaps(pay, pay, pay, pay)
-    both = call(join_kernel, shape(16, NZ), [VMEM] * 2)(x1, x2)
-    far = lax.ppermute(both, "narrow", [(i + 1, i) for i in range(narrow_count - 1)])
-    u, sent, kap, *edges = call(
+    u, sent, kap, fx2, fx1, fy1, fy2 = call(
         first_kernel,
         (field, gathered, shape(16, NZ), face, face, face, face),
         [VMEM] + [SMEM] * 3 + [VMEM] * 5,
         [scratch(16, NZ)],
     )(right_side, material_table, robin_table, index, pay, y2, y1, x1, x2)
     every = everywhere(sent)
-    edges = call(
-        ride_kernel, (shape(CY + 8, NZ),) * 2 + (shape(CX + 16, NZ),) * 2, [VMEM] * 9
-    )(x2, x1, y1, y2, far, *edges)
-    seen = swaps(*edges)
-    u, sent, shifted, *edges = call(
+    ridden = (shape(CY + 16, NZ),) * 2
+    py1, py2 = call(ride_y_kernel, ridden, [VMEM] * 6)(x2, x1, y1, y2, fy1, fy2)
+    r1 = swap(py1, "narrow", 0)
+    r2 = swap(py2, "narrow", 1)
+    px2, px1 = call(ride_x_kernel, ridden, [VMEM] * 6)(x2, x1, r1, r2, fx2, fx1)
+    seen = (swap(px2, "wide", 1), swap(px1, "wide", 0), r1, r2)
+    shifted = call(
+        widen_kernel, shape(16 * len(SHIFTS), count), [VMEM] * 9, [scratch(16, count)]
+    )(pay, x2, x1, y1, y2, *seen)
+    u, sent, *edges = call(
         second_kernel,
-        (field, gathered, shape(16 * len(SHIFTS), count), face, face, face, face),
-        [VMEM] + [SMEM] * 2 + [VMEM] * 13,
-        [scratch(16, count), scratch(CX, CY, NZ), scratch(16, NZ)],
-    )(right_side, robin_table, index, kap, u, every, pay, x2, x1, y1, y2, far, *seen)
+        (field, gathered, face, face, face, face),
+        [VMEM] + [SMEM] * 2 + [VMEM] * 8,
+        [scratch(CX, CY, NZ), scratch(16, NZ)],
+    )(right_side, robin_table, index, kap, u, every, shifted, *seen)
     every = everywhere(sent)
     seen = swaps(*edges)
     half = jax.ShapeDtypeStruct((CX, CY, NZ), jnp.bfloat16)

time: 124 us -> 119 us (0.960)
  starting transfers between devices: 81.9 us -> 77.4 us
    all_to_all x2, starting transfers between devices: 50.5 us -> 46 us  [everywhere(): return lax.all_to_all(values, ('wide', 'narrow'), 0, 0, tiled=True)]
    ppermute x13 -> x12, waiting for transfers between devices: 12.5 us -> 9.99 us  [swap(): return lax.ppermute(array, axis, swap_pairs(lax.axis_size(axis), start))]
    all_to_all x2, waiting for transfers between devices: 18.9 us -> 21.3 us  [everywhere(): return lax.all_to_all(values, ('wide', 'narrow'), 0, 0, tiled=True)]
    pallas_call x3 -> x4, Pallas kernels: 2.98 us -> 3.07 us  [the longest x1 2.87 us: body(): call(second_kernel, (field, gathered, face, face, face, face), [VMEM] + [...]
    ppermute x13 -> x12, starting transfers between devices: 31.4 us -> 31.5 us  [swap(): return lax.ppermute(array, axis, swap_pairs(lax.axis_size(axis), start))]
  transfers between devices with their start and end apart: 15 -> 14, of which waited for: 6 -> 6; matrix products, arithmetic and copies ran while one was open for 0% -> 0% of each run, Pallas kernels for 0% -> 0%
where the time goes in v4:
time: 119 us
  starting transfers between devices  77.4 us (65%)
  waiting for transfers between devices  31.3 us (26%)
  Pallas kernels  6.99 us (6%)
  local copies, waits for them, and re-layouts  2.27 us (2%)
    all_to_all x2, starting transfers between devices, everywhere(): return lax.all_to_all(values, ('wide', 'narrow'), 0, 0, tiled=True)  46 us
    ppermute x12, starting transfers between devices, swap(): return lax.ppermute(array, axis, swap_pairs(lax.axis_size(axis), start))  31.5 us
    all_to_all x2, waiting for transfers between devices, everywhere(): return lax.all_to_all(values, ('wide', 'narrow'), 0, 0, tiled=True)  21.3 us
    ppermute x12, waiting for transfers between devices, swap(): return lax.ppermute(array, axis, swap_pairs(lax.axis_size(axis), start))  9.99 us
    pallas_call x1, Pallas kernels, body(): call(second_kernel, (field, gathered, face, face, face, face), [VMEM] + [...  2.87 us
    pallas_call x1, Pallas kernels, body(): call(first_kernel, (field, gathered, shape(16, NZ), face, face, face, fac...  2.55 us
  transfers between devices with their start and end apart: 14, of which 6 were waited for; matrix products, arithmetic and copies ran while one was open for 0% of the time, Pallas kernels for 0%

profile of v4, /device:TPU:1, one launch (start us, length us, event | category | flops | bytes accessed | tf_op | source)
XLA Modules:
  0.0 118.8 jit_solution(6522646272281375638)
XLA Ops:
  0.6 0.0 copy-start.4
  0.6 0.7 copy-done.4
  1.3 0.0 copy-start.5
  1.3 0.7 copy-done.5
  2.0 0.0 copy-start.2
  2.0 0.0 copy-start.3
  2.0 0.0 copy-start.6
  2.0 4.6 %collective-permute-start.3 = (f32[8,128]{1,0:T(8,128)S(1)}, f32[8,128]{1,0:T(8,128)S(1)}, u32[]{:S(2)}, u32[]{:S(2)}) collective-permute-start(f32[8,128]{1,0:T(8,128)S(1)} %shard_map.77.own), channel_id=1, source_target_pairs={{8,16},{16,8},{24,32},{32,24},{40,48},{48,40},{56,64},{64,56},{72,... | collective-permute-start | bytes 12296 | tf_op jit(solution)/shard_map/ppermute | solution.py:367
  6.6 4.9 %collective-permute-start.2 = (f32[8,128]{1,0:T(8,128)S(1)}, f32[8,128]{1,0:T(8,128)S(1)}, u32[]{:S(2)}, u32[]{:S(2)}) collective-permute-start(f32[8,128]{1,0:T(8,128)S(1)} %shard_map.77.own), channel_id=1, source_target_pairs={{0,8},{8,0},{16,24},{24,16},{32,40},{40,32},{48,56},{56,48},{64,72... | collective-permute-start | bytes 12296 | tf_op jit(solution)/shard_map/ppermute | solution.py:367
  11.6 1.9 %collective-permute-start.1 = (f32[8,128]{1,0:T(8,128)S(1)}, f32[8,128]{1,0:T(8,128)S(1)}, u32[]{:S(2)}, u32[]{:S(2)}) collective-permute-start(f32[8,128]{1,0:T(8,128)S(1)} %shard_map.77.own), channel_id=1, source_target_pairs={{0,1},{1,0},{2,3},{3,2},{4,5},{5,4},{6,7},{7,6},{8,9},{9,8},{10,11... | collective-permute-start | bytes 12296 | tf_op jit(solution)/shard_map/ppermute | solution.py:367
  13.5 0.7 collective-permute-start
  14.2 0.0 collective-permute-done.3.x2
  14.2 0.0 collective-permute-done.2.x1
  14.2 1.7 %collective-permute-done.1.y1 = f32[8,128]{1,0:T(8,128)S(1)} collective-permute-done((f32[8,128]{1,0:T(8,128)S(1)}, f32[8,128]{1,0:T(8,128)S(1)}, u32[]{:S(2)}, u32[]{:S(2)}) %collective-permute-start.1) | collective-permute-done | bytes 4128 | tf_op jit(solution)/shard_map/ppermute | solution.py:367
  15.9 0.0 collective-permute-done.y2
  15.9 0.0 copy-done.2
  15.9 0.0 copy-done.3
  15.9 0.0 copy-done.6
  15.9 0.0 copy-start
  16.0 0.9 copy-done
  16.8 2.6 %shard_map.78 = (f32[16,16,128]{2,1,0:T(8,128)S(1)}, f32[512,128]{1,0:T(8,128)}, f32[16,128]{1,0:T(8,128)S(1)}, f32[16,128]{1,0:T(8,128)S(1)}, f32[16,128]{1,0:T...) custom-call(f32[16,16,128]{2,1,0:T(8,128)S(1)} %copy-done, f32[16]{0:T(128)S(1)} %copy-done.6, f32[8]{0:T(128)S(1)} %copy-done.2, ...), custom_call_target="tpu_custom_call" | custom-call | tf_op jit(solution)/shard_map/pallas_call | solution.py:390
  19.4 25.6 %all-to-all-start = ((f32[512,1,128]{2,1,0:T(1,128)}), f32[512,1,128]{2,1,0:T(1,128)S(1)}, u32[]{:S(2)}, u32[]{:S(2)}) async-start(f32[512,1,128]{2,1,0:T(1,128)} %bitcast.2), calls=%async_computation | async-start | bytes 524288 | tf_op jit(solution)/shard_map/all_to_all | solution.py:379
  45.0 3.4 %collective-permute-start.4 = (f32[32,128]{1,0:T(8,128)S(1)}, f32[32,128]{1,0:T(8,128)S(1)}, u32[]{:S(2)}, u32[]{:S(2)}) collective-permute-start(f32[32,128]{1,0:T(8,128)S(1)} %get-tuple-element.24), channel_id=1, source_target_pairs={{0,1},{1,0},{2,3},{3,2},{4,5},{5,4},{6,7},{7,6},{8,9},{9,8},{10,11... | collective-permute-start | bytes 49160 | tf_op jit(solution)/shard_map/ppermute | solution.py:367
  48.4 0.7 collective-permute-start.5
  49.1 4.9 %collective-permute-done.4.r1 = f32[32,128]{1,0:T(8,128)S(1)} collective-permute-done((f32[32,128]{1,0:T(8,128)S(1)}, f32[32,128]{1,0:T(8,128)S(1)}, u32[]{:S(2)}, u32[]{:S(2)}) %collective-permute-start.4) | collective-permute-done | bytes 16416 | tf_op jit(solution)/shard_map/ppermute | solution.py:367
  54.1 0.0 collective-permute-done.5.r2
  54.1 3.8 %collective-permute-start.6 = (f32[32,128]{1,0:T(8,128)S(1)}, f32[32,128]{1,0:T(8,128)S(1)}, u32[]{:S(2)}, u32[]{:S(2)}) collective-permute-start(f32[32,128]{1,0:T(8,128)S(1)} %get-tuple-element.28), channel_id=1, source_target_pairs={{8,16},{16,8},{24,32},{32,24},{40,48},{48,40},{56,64},{64,56},{72,... | collective-permute-start | bytes 49160 | tf_op jit(solution)/shard_map/ppermute | solution.py:367
  57.9 0.0 copy-start.1
  57.9 2.1 %collective-permute-start.7 = (f32[32,128]{1,0:T(8,128)S(1)}, f32[32,128]{1,0:T(8,128)S(1)}, u32[]{:S(2)}, u32[]{:S(2)}) collective-permute-start(f32[32,128]{1,0:T(8,128)S(1)} %get-tuple-element.29), channel_id=1, source_target_pairs={{0,8},{8,0},{16,24},{24,16},{32,40},{40,32},{48,56},{56,48},{64,72... | collective-permute-start | bytes 49160 | tf_op jit(solution)/shard_map/ppermute | solution.py:367
  59.9 0.0 collective-permute-done.6.q2
  59.9 1.1 collective-permute-done.7.q1
  61.1 0.2 shard_map.81.shifted
  61.3 8.4 %all-to-all-done = f32[512,1,128]{2,1,0:T(1,128)S(1)} async-done(((f32[512,1,128]{2,1,0:T(1,128)}), f32[512,1,128]{2,1,0:T(1,128)S(1)}, u32[]{:S(2)}, u32[]{:S(2)}) %all-to-all-start) | async-done | bytes 262176 | tf_op jit(solution)/shard_map/all_to_all | solution.py:379
  69.6 0.0 copy-done.1
  69.6 2.9 %shard_map.82 = (f32[16,16,128]{2,1,0:T(8,128)S(1)}, f32[512,128]{1,0:T(8,128)}, f32[16,128]{1,0:T(8,128)S(1)}, f32[16,128]{1,0:T(8,128)S(1)}, f32[16,128]{1,0:T(8,128)S(1)}, /*index=5*/f32[16,128]{1,0:T(8,128)S(1)}) custom-call(f32[16,16,128]{2,1,0:T(8,128)S(1)} %copy-done.1, f32[8]{0:T(128)S(1)} %copy-done.2, s32[2]{0:T(128)S(1)} %bitcast.12, ...), custom_call_target="tpu_custom_call" | custom-call | tf_op jit(solution)/shard_map/pallas_call | solution.py:406
  72.5 20.4 %all-to-all-start.1 = ((f32[512,1,128]{2,1,0:T(1,128)}), f32[512,1,128]{2,1,0:T(1,128)S(1)}, u32[]{:S(2)}, u32[]{:S(2)}) async-start(f32[512,1,128]{2,1,0:T(1,128)} %bitcast.5), calls=%async_computation.1 | async-start | bytes 524288 | tf_op jit(solution)/shard_map/all_to_all | solution.py:379
  92.9 3.5 %collective-permute-start.8 = (f32[16,128]{1,0:T(8,128)S(1)}, f32[16,128]{1,0:T(8,128)S(1)}, u32[]{:S(2)}, u32[]{:S(2)}) collective-permute-start(f32[16,128]{1,0:T(8,128)S(1)} %get-tuple-element.32), channel_id=1, source_target_pairs={{8,16},{16,8},{24,32},{32,24},{40,48},{48,40},{56,64},{64,56},{72,... | collective-permute-start | bytes 24584 | tf_op jit(solution)/shard_map/ppermute | solution.py:367
  96.4 3.3 %collective-permute-start.9 = (f32[16,128]{1,0:T(8,128)S(1)}, f32[16,128]{1,0:T(8,128)S(1)}, u32[]{:S(2)}, u32[]{:S(2)}) collective-permute-start(f32[16,128]{1,0:T(8,128)S(1)} %get-tuple-element.33), channel_id=1, source_target_pairs={{0,8},{8,0},{16,24},{24,16},{32,40},{40,32},{48,56},{56,48},{64,72... | collective-permute-start | bytes 24584 | tf_op jit(solution)/shard_map/ppermute | solution.py:367
  99.8 1.9 %collective-permute-start.10 = (f32[16,128]{1,0:T(8,128)S(1)}, f32[16,128]{1,0:T(8,128)S(1)}, u32[]{:S(2)}, u32[]{:S(2)}) collective-permute-start(f32[16,128]{1,0:T(8,128)S(1)} %get-tuple-element.34), channel_id=1, source_target_pairs={{0,1},{1,0},{2,3},{3,2},{4,5},{5,4},{6,7},{7,6},{8,9},{9,8},{10,11... | collective-permute-start | bytes 24584 | tf_op jit(solution)/shard_map/ppermute | solution.py:367
  101.7 0.7 collective-permute-start.11
  102.4 0.0 collective-permute-done.8.q2
  102.4 0.0 collective-permute-done.9.q1
  102.4 2.1 %collective-permute-done.10.r1 = f32[16,128]{1,0:T(8,128)S(1)} collective-permute-done((f32[16,128]{1,0:T(8,128)S(1)}, f32[16,128]{1,0:T(8,128)S(1)}, u32[]{:S(2)}, u32[]{:S(2)}) %collective-permute-start.10) | collective-permute-done | bytes 8224 | tf_op jit(solution)/shard_map/ppermute | solution.py:367
  104.5 0.0 collective-permute-done.11.r2
  104.5 12.9 %all-to-all-done.1 = f32[512,1,128]{2,1,0:T(1,128)S(1)} async-done(((f32[512,1,128]{2,1,0:T(1,128)}), f32[512,1,128]{2,1,0:T(1,128)S(1)}, u32[]{:S(2)}, u32[]{:S(2)}) %all-to-all-start.1) | async-done | bytes 262176 | tf_op jit(solution)/shard_map/all_to_all | solution.py:379
  117.5 1.4 %shard_map.83 = (bf16[16,16,128]{2,1,0:T(8,128)(2,1)}, bf16[16,16,128]{2,1,0:T(8,128)(2,1)}) custom-call(f32[16,16,128]{2,1,0:T(8,128)S(1)} %copy-done.1, f32[16,128]{1,0:T(8,128)S(1)} %get-tuple-element.19.kap, f32[16,16,128]{2,1,0:T(8,128)S(1)} %get-tuple-element.30.old, f32[512,128]{1,0:T(8,128)S(1)} %bitcast.10, f32[192,512]{1,0:T(8,128)S(1)} %shard_map.81.shifted, ...), custom_call_target="tpu_custom_call" | custom-call | tf_op jit(solution)/shard_map/pallas_call | solution.py:415
  (3 shorter events, 0.0 us)
Async XLA Ops:
  0.6 0.7 copy-start.4
  1.3 0.7 copy-start.5
  2.0 13.9 %copy-start.2 = (f32[8]{0:T(128)S(1)}, f32[8]{0:T(128)}, u32[]{:S(2)}) copy-start(f32[8]{0:T(128)} %robin_table.3) | copy-start | bytes 100
  2.0 13.9 %copy-start.3 = (s32[1,1,2]{2,1,0:T(1,128)S(1)}, s32[1,1,2]{2,1,0:T(1,128)}, u32[]{:S(2)}) copy-start(s32[1,1,2]{2,1,0:T(1,128)} %param.10) | copy-start | bytes 28
  2.0 13.9 %copy-start.6 = (f32[16]{0:T(128)S(1)}, f32[16]{0:T(128)}, u32[]{:S(2)}) copy-start(f32[16]{0:T(128)} %table.1) | copy-start | bytes 196
  2.0 12.2 %collective-permute-start.3 = (f32[8,128]{1,0:T(8,128)S(1)}, f32[8,128]{1,0:T(8,128)S(1)}, u32[]{:S(2)}, u32[]{:S(2)}) collective-permute-start(f32[8,128]{1,0:T(8,128)S(1)} %shard_map.77.own), channel_id=1, source_target_pairs={{8,16},{16,8},{24,32},{32,24},{40,48},{48,40},{56,64},{64,56},{72,... | collective-permute-start | bytes 12296 | tf_op jit(solution)/shard_map/ppermute | solution.py:367
  6.6 7.5 %collective-permute-start.2 = (f32[8,128]{1,0:T(8,128)S(1)}, f32[8,128]{1,0:T(8,128)S(1)}, u32[]{:S(2)}, u32[]{:S(2)}) collective-permute-start(f32[8,128]{1,0:T(8,128)S(1)} %shard_map.77.own), channel_id=1, source_target_pairs={{0,8},{8,0},{16,24},{24,16},{32,40},{40,32},{48,56},{56,48},{64,72... | collective-permute-start | bytes 12296 | tf_op jit(solution)/shard_map/ppermute | solution.py:367
  11.6 4.4 %collective-permute-start.1 = (f32[8,128]{1,0:T(8,128)S(1)}, f32[8,128]{1,0:T(8,128)S(1)}, u32[]{:S(2)}, u32[]{:S(2)}) collective-permute-start(f32[8,128]{1,0:T(8,128)S(1)} %shard_map.77.own), channel_id=1, source_target_pairs={{0,1},{1,0},{2,3},{3,2},{4,5},{5,4},{6,7},{7,6},{8,9},{9,8},{10,11... | collective-permute-start | bytes 12296 | tf_op jit(solution)/shard_map/ppermute | solution.py:367
  13.5 2.4 %collective-permute-start = (f32[8,128]{1,0:T(8,128)S(1)}, f32[8,128]{1,0:T(8,128)S(1)}, u32[]{:S(2)}, u32[]{:S(2)}) collective-permute-start(f32[8,128]{1,0:T(8,128)S(1)} %shard_map.77.own), channel_id=1, source_target_pairs={{1,2},{2,1},{3,4},{4,3},{5,6},{6,5},{9,10},{10,9},{11,12},{12,11},... | collective-permute-start | bytes 12296 | tf_op jit(solution)/shard_map/ppermute | solution.py:367
  15.9 0.9 copy-start
  19.4 50.2 %all-to-all-start = ((f32[512,1,128]{2,1,0:T(1,128)}), f32[512,1,128]{2,1,0:T(1,128)S(1)}, u32[]{:S(2)}, u32[]{:S(2)}) async-start(f32[512,1,128]{2,1,0:T(1,128)} %bitcast.2), calls=%async_computation | async-start | bytes 524288 | tf_op jit(solution)/shard_map/all_to_all | solution.py:379
  45.0 9.0 %collective-permute-start.4 = (f32[32,128]{1,0:T(8,128)S(1)}, f32[32,128]{1,0:T(8,128)S(1)}, u32[]{:S(2)}, u32[]{:S(2)}) collective-permute-start(f32[32,128]{1,0:T(8,128)S(1)} %get-tuple-element.24), channel_id=1, source_target_pairs={{0,1},{1,0},{2,3},{3,2},{4,5},{5,4},{6,7},{7,6},{8,9},{9,8},{10,11... | collective-permute-start | bytes 49160 | tf_op jit(solution)/shard_map/ppermute | solution.py:367
  48.4 5.6 %collective-permute-start.5 = (f32[32,128]{1,0:T(8,128)S(1)}, f32[32,128]{1,0:T(8,128)S(1)}, u32[]{:S(2)}, u32[]{:S(2)}) collective-permute-start(f32[32,128]{1,0:T(8,128)S(1)} %get-tuple-element.25), channel_id=1, source_target_pairs={{1,2},{2,1},{3,4},{4,3},{5,6},{6,5},{9,10},{10,9},{11,12},{12,11},... | collective-permute-start | bytes 49160 | tf_op jit(solution)/shard_map/ppermute | solution.py:367
  54.1 5.9 %collective-permute-start.6 = (f32[32,128]{1,0:T(8,128)S(1)}, f32[32,128]{1,0:T(8,128)S(1)}, u32[]{:S(2)}, u32[]{:S(2)}) collective-permute-start(f32[32,128]{1,0:T(8,128)S(1)} %get-tuple-element.28), channel_id=1, source_target_pairs={{8,16},{16,8},{24,32},{32,24},{40,48},{48,40},{56,64},{64,56},{72,... | collective-permute-start | bytes 49160 | tf_op jit(solution)/shard_map/ppermute | solution.py:367
  57.9 11.8 %copy-start.1 = (f32[16,16,128]{2,1,0:T(8,128)S(1)}, f32[16,16,128]{2,1,0:T(8,128)}, u32[]{:S(2)}) copy-start(f32[16,16,128]{2,1,0:T(8,128)} %right.5) | copy-start | bytes 393220
  57.9 3.2 %collective-permute-start.7 = (f32[32,128]{1,0:T(8,128)S(1)}, f32[32,128]{1,0:T(8,128)S(1)}, u32[]{:S(2)}, u32[]{:S(2)}) collective-permute-start(f32[32,128]{1,0:T(8,128)S(1)} %get-tuple-element.29), channel_id=1, source_target_pairs={{0,8},{8,0},{16,24},{24,16},{32,40},{40,32},{48,56},{56,48},{64,72... | collective-permute-start | bytes 49160 | tf_op jit(solution)/shard_map/ppermute | solution.py:367
  72.5 45.0 %all-to-all-start.1 = ((f32[512,1,128]{2,1,0:T(1,128)}), f32[512,1,128]{2,1,0:T(1,128)S(1)}, u32[]{:S(2)}, u32[]{:S(2)}) async-start(f32[512,1,128]{2,1,0:T(1,128)} %bitcast.5), calls=%async_computation.1 | async-start | bytes 524288 | tf_op jit(solution)/shard_map/all_to_all | solution.py:379
  92.9 9.5 %collective-permute-start.8 = (f32[16,128]{1,0:T(8,128)S(1)}, f32[16,128]{1,0:T(8,128)S(1)}, u32[]{:S(2)}, u32[]{:S(2)}) collective-permute-start(f32[16,128]{1,0:T(8,128)S(1)} %get-tuple-element.32), channel_id=1, source_target_pairs={{8,16},{16,8},{24,32},{32,24},{40,48},{48,40},{56,64},{64,56},{72,... | collective-permute-start | bytes 24584 | tf_op jit(solution)/shard_map/ppermute | solution.py:367
  96.4 6.0 %collective-permute-start.9 = (f32[16,128]{1,0:T(8,128)S(1)}, f32[16,128]{1,0:T(8,128)S(1)}, u32[]{:S(2)}, u32[]{:S(2)}) collective-permute-start(f32[16,128]{1,0:T(8,128)S(1)} %get-tuple-element.33), channel_id=1, source_target_pairs={{0,8},{8,0},{16,24},{24,16},{32,40},{40,32},{48,56},{56,48},{64,72... | collective-permute-start | bytes 24584 | tf_op jit(solution)/shard_map/ppermute | solution.py:367
  99.8 4.8 %collective-permute-start.10 = (f32[16,128]{1,0:T(8,128)S(1)}, f32[16,128]{1,0:T(8,128)S(1)}, u32[]{:S(2)}, u32[]{:S(2)}) collective-permute-start(f32[16,128]{1,0:T(8,128)S(1)} %get-tuple-element.34), channel_id=1, source_target_pairs={{0,1},{1,0},{2,3},{3,2},{4,5},{5,4},{6,7},{7,6},{8,9},{9,8},{10,11... | collective-permute-start | bytes 24584 | tf_op jit(solution)/shard_map/ppermute | solution.py:367
  101.7 2.8 %collective-permute-start.11 = (f32[16,128]{1,0:T(8,128)S(1)}, f32[16,128]{1,0:T(8,128)S(1)}, u32[]{:S(2)}, u32[]{:S(2)}) collective-permute-start(f32[16,128]{1,0:T(8,128)S(1)} %get-tuple-element.35), channel_id=1, source_target_pairs={{1,2},{2,1},{3,4},{4,3},{5,6},{6,5},{9,10},{10,9},{11,12},{12,11},... | collective-permute-start | bytes 24584 | tf_op jit(solution)/shard_map/ppermute | solution.py:367

commit v5 on v3

--- a/solution.py
+++ b/solution.py
@@ -3,6 +3,7 @@
 from jax import lax
 from jax.experimental import pallas as pl
 from jax.experimental.pallas import tpu as pltpu
+from jax.sharding import Mesh
 from jax.sharding import PartitionSpec as P
 
 
@@ -18,6 +19,7 @@
 GRANT = 8 * 1024 * 1024
 EXACT = lax.Precision.HIGHEST
 F32 = jnp.float32
+WIDE = ("half", "plane")
 SHIFTS = [(i, j) for i in range(4) for j in range(4) if i in (1, 2) or j in (1, 2)]
 
 VMEM = pl.BlockSpec(memory_space=pltpu.VMEM)
@@ -37,8 +39,9 @@
 
 
 def place():
-    wide, narrow = lax.axis_index("wide"), lax.axis_index("narrow")
-    last_wide, last_narrow = lax.axis_size("wide") - 1, lax.axis_size("narrow") - 1
+    planes, narrow = lax.axis_size("plane"), lax.axis_index("narrow")
+    wide = lax.axis_index("half") * planes + lax.axis_index("plane")
+    last_wide, last_narrow = lax.axis_size("half") * planes - 1, lax.axis_size("narrow") - 1
     inside = tuple(
         jnp.where(flag, F32(1.0), F32(0.0))
         for flag in (wide > 0, wide < last_wide, narrow > 0, narrow < last_narrow)
@@ -171,7 +174,7 @@
         sums[at : at + 1, :] = NEAR * south_row[a]
         sums[at + 3 : at + 4, :] = NEAR * north_row[a]
     column = jnp.sum(sums[...], axis=1, keepdims=True)
-    spread = jnp.where(iota((16, NZ), 0) == iota((16, NZ), 1), column, 0.0)
+    spread = jnp.where(iota((16, NZ), 0) == iota((16, NZ), 1) % 16, column, 0.0)
     out[...] = jnp.broadcast_to(jnp.sum(spread, axis=0, keepdims=True), out.shape)
 
 
@@ -239,8 +242,9 @@
         out[CX + 12 : CX + 16, :] = jnp.zeros((4, NZ), F32)
 
 
-def widen(even_x, even_y, pays, far, seen, rows, shifted):
-    own, x2, x1, y1, y2 = pays
+def widen_kernel(own, x2, x1, y1, y2, far, q2, q1, r1, r2, shifted, rows, moves):
+    even_x, even_y, _ = place()
+    seen = (q2, q1, r1, r2)
     count = rows.shape[1]
     narrow_count = lax.axis_size("narrow")
     wide_count = count // narrow_count
@@ -267,12 +271,32 @@
         x, y = at_x + (i - 1), at_y + (j - 1)
         fits = (x >= 0) & (x < wide_count) & (y >= 0) & (y < narrow_count)
         moved = rolled(value, -((i - 1) * narrow_count + j - 1), 1)
-        shifted[16 * t : 16 * t + 16, :] = jnp.where(fits, moved, 0.0)
-
-
-def window(every, shifted):
-    product = jnp.dot(shifted[...], every[...], precision=EXACT, preferred_element_type=F32)
-    lane = iota((16, NZ), 1)
+        moves[16 * t : 16 * t + 16, :] = jnp.where(fits, moved, 0.0)
+    planes = lax.axis_size("plane")
+    source, target = iota((count, count), 0), iota((count, count), 1)
+    half, plane = target // (narrow_count * planes), target % planes
+    wanted = (half * planes + plane) * narrow_count + target // planes % narrow_count
+    order = (source == wanted).astype(F32)
+    shifted[...] = jnp.dot(moves[...], order, precision=EXACT, preferred_element_type=F32)
+
+
+def turn_kernel(arrived, out):
+    groups = arrived.shape[0] // 8
+    mine = iota((8, NZ), 1) // 16 == iota((8, NZ), 0)
+    for q in range(groups):
+        kept = jnp.where(mine, arrived[8 * q : 8 * q + 8, :], 0.0)
+        row = jnp.sum(kept, axis=0, keepdims=True)
+        for b in range(out.shape[0] // groups):
+            out[b * groups + q : b * groups + q + 1, :] = row
+
+
+def window(every, shifted, opened):
+    mine = iota((8, NZ), 1) // 16 == iota((8, NZ), 0)
+    for d in range(every.shape[0]):
+        row = jnp.broadcast_to(every[d : d + 1, :], (8, NZ))
+        opened[8 * d : 8 * d + 8, :] = jnp.where(mine, row, 0.0)
+    product = jnp.dot(shifted[...], opened[...], precision=EXACT, preferred_element_type=F32)
+    lane = iota((16, NZ), 1) % 16
     picked = jnp.zeros((16, NZ), F32)
     for t, (i, j) in enumerate(SHIFTS):
         picked = picked + jnp.where(lane == 4 * i + j, product[16 * t : 16 * t + 16], 0.0)
@@ -298,13 +322,12 @@
 
 
 def second_kernel(
-    right, robin_table, robin_index, kap, old, every, own, x2, x1, y1, y2, far, q2, q1, r1, r2,
-    u, out, shifted, fx2, fx1, fy1, fy2, rows, source, sums,
+    right, robin_table, robin_index, kap, old, every, shifted, q2, q1, r1, r2,
+    u, out, fx2, fx1, fy1, fy2, source, sums, opened,
 ):
     even_x, even_y, inside = place()
     seen = (q2, q1, r1, r2)
-    widen(even_x, even_y, (own, x2, x1, y1, y2), far, seen, rows, shifted)
-    value = window(every, shifted)
+    value = window(every, shifted, opened)
     west, east, south, north = correct(even_x, even_y, value, old, u, seen)
     robin = robin_of(robin_index, robin_table)
     coef = Coefficients(kap)
@@ -325,9 +348,9 @@
     faces(even_x, even_y, u, (fx2, fx1, fy1, fy2))
 
 
-def last_kernel(right, kap, old, every, shifted, q2, q1, r1, r2, answer, out, u):
+def last_kernel(right, kap, old, every, shifted, q2, q1, r1, r2, answer, out, u, opened):
     even_x, even_y, inside = place()
-    value = window(every, shifted)
+    value = window(every, shifted, opened)
     west, east, south, north = correct(even_x, even_y, value, old, u, (q2, q1, r1, r2))
     coef = Coefficients(kap)
     for i in range(CX):
@@ -362,17 +385,22 @@
     return pairs
 
 
+def swap(array, axis, start):
+    return lax.ppermute(array, axis, swap_pairs(lax.axis_size(axis), start))
+
+
 def swaps(sx2, sx1, sy1, sy2):
-    wide_count, narrow_count = lax.axis_size("wide"), lax.axis_size("narrow")
-    x2 = lax.ppermute(sx2, "wide", swap_pairs(wide_count, 1))
-    x1 = lax.ppermute(sx1, "wide", swap_pairs(wide_count, 0))
-    y1 = lax.ppermute(sy1, "narrow", swap_pairs(narrow_count, 0))
-    y2 = lax.ppermute(sy2, "narrow", swap_pairs(narrow_count, 1))
+    x2 = swap(sx2, WIDE, 1)
+    x1 = swap(sx1, WIDE, 0)
+    y1 = swap(sy1, "narrow", 0)
+    y2 = swap(sy2, "narrow", 1)
     return x2, x1, y1, y2
 
 
-def everywhere(values):
-    return lax.all_to_all(values, ("wide", "narrow"), 0, 0, tiled=True)
+def everywhere(values, count):
+    near = lax.all_to_all(values, "plane", 0, 0, tiled=True)
+    turned = call(turn_kernel, jax.ShapeDtypeStruct((count // 8, NZ), F32), [VMEM])(near)
+    return lax.all_to_all(turned, ("half", "narrow"), 0, 0, tiled=True)
 
 
 def body(right_side, labels, material_table, robin_table, robin_index, coarse_rows):
@@ -380,7 +408,7 @@
     narrow_count = lax.axis_size("narrow")
     shape = lambda *dims: jax.ShapeDtypeStruct(dims, F32)
     scratch = lambda *dims: pltpu.VMEM(dims, F32)
-    field, face, gathered = shape(CX, CY, NZ), shape(CY, NZ), shape(count, NZ)
+    field, face, mine = shape(CX, CY, NZ), shape(CY, NZ), shape(lax.axis_size("plane"), NZ)
     index = robin_index[0, 0]
     pay = call(pack_kernel, shape(8, NZ), [VMEM] * 2)(labels, coarse_rows)
     x2, x1, y1, y2 = swaps(pay, pay, pay, pay)
@@ -388,42 +416,48 @@
     far = lax.ppermute(both, "narrow", [(i + 1, i) for i in range(narrow_count - 1)])
     u, sent, kap, *edges = call(
         first_kernel,
-        (field, gathered, shape(16, NZ), face, face, face, face),
+        (field, mine, shape(16, NZ), face, face, face, face),
         [VMEM] + [SMEM] * 3 + [VMEM] * 5,
         [scratch(16, NZ)],
     )(right_side, material_table, robin_table, index, pay, y2, y1, x1, x2)
-    every = everywhere(sent)
+    every = everywhere(sent, count)
     edges = call(
         ride_kernel, (shape(CY + 8, NZ),) * 2 + (shape(CX + 16, NZ),) * 2, [VMEM] * 9
     )(x2, x1, y1, y2, far, *edges)
     seen = swaps(*edges)
-    u, sent, shifted, *edges = call(
+    lines = 16 * len(SHIFTS)
+    shifted = call(
+        widen_kernel, shape(lines, count), [VMEM] * 10, [scratch(16, count), scratch(lines, count)]
+    )(pay, x2, x1, y1, y2, far, *seen)
+    u, sent, *edges = call(
         second_kernel,
-        (field, gathered, shape(16 * len(SHIFTS), count), face, face, face, face),
-        [VMEM] + [SMEM] * 2 + [VMEM] * 13,
-        [scratch(16, count), scratch(CX, CY, NZ), scratch(16, NZ)],
-    )(right_side, robin_table, index, kap, u, every, pay, x2, x1, y1, y2, far, *seen)
-    every = everywhere(sent)
+        (field, mine, face, face, face, face),
+        [VMEM] + [SMEM] * 2 + [VMEM] * 8,
+        [scratch(CX, CY, NZ), scratch(16, NZ), scratch(count, NZ)],
+    )(right_side, robin_table, index, kap, u, every, shifted, *seen)
+    every = everywhere(sent, count)
     seen = swaps(*edges)
     half = jax.ShapeDtypeStruct((CX, CY, NZ), jnp.bfloat16)
-    return call(last_kernel, (half, half), [VMEM] * 9, [scratch(CX, CY, NZ)])(
+    return call(last_kernel, (half, half), [VMEM] * 9, [scratch(CX, CY, NZ), scratch(count, NZ)])(
         right_side, kap, u, every, shifted, *seen
     )
 
 
 def solution(mesh):
+    devices = mesh.devices
+    split = Mesh(devices.reshape(2, devices.shape[0] // 2, -1), (*WIDE, "narrow"))
     placed = (
-        P("wide", "narrow", None),
-        P("wide", "narrow", None),
+        P(WIDE, "narrow", None),
+        P(WIDE, "narrow", None),
         P(),
         P(),
-        P("wide", "narrow", None),
-        P(("wide", "narrow"), None),
+        P(WIDE, "narrow", None),
+        P((*WIDE, "narrow"), None),
     )
     return jax.shard_map(
         body,
-        mesh=mesh,
+        mesh=split,
         in_specs=placed,
-        out_specs=(P("wide", "narrow", None), P("wide", "narrow", None)),
+        out_specs=(P(WIDE, "narrow", None), P(WIDE, "narrow", None)),
         check_vma=False,
     )

time: 124 us -> 129 us (1.040)
  the two profiles are of different devices: /device:TPU:1 before, /device:TPU:62 now
where the time goes in v5:
time: 129 us; the launch traced here: 128 us
  starting transfers between devices  85.9 us (67%)
  blocking collectives  21.3 us (17%)
  waiting for transfers between devices  10.5 us (8%)
  Pallas kernels  7.67 us (6%)
  local copies, waits for them, and re-layouts  2.27 us (2%)
    ppermute x12, starting transfers between devices, swap(): return lax.ppermute(array, axis, swap_pairs(lax.axis_size(axis), start))  66.5 us
    all_to_all x2, blocking collectives, everywhere(): near = lax.all_to_all(values, 'plane', 0, 0, tiled=True)  21.3 us
    all_to_all x2, starting transfers between devices, everywhere(): return lax.all_to_all(turned, ('half', 'narrow'), 0, 0, tiled=True)  17.4 us
    ppermute x12, waiting for transfers between devices, swap(): return lax.ppermute(array, axis, swap_pairs(lax.axis_size(axis), start))  6.94 us
    ppermute x1, waiting for transfers between devices, body(): lax.ppermute(both, 'narrow', [(i + 1, i) for i in range(narrow_count - 1)])  3.52 us
  transfers between devices with their start and end apart: 15, of which 5 were waited for; matrix products, arithmetic and copies ran while one was open for 0% of the time, Pallas kernels for 1%

profile of v5, /device:TPU:62, one launch (start us, length us, event | category | flops | bytes accessed | tf_op | source)
XLA Modules:
  0.0 128.4 jit_solution(16889708941245316064)
XLA Ops:
  0.6 0.0 copy-start.2
  0.6 0.7 copy-done.2
  1.3 0.7 copy-done.3
  2.0 2.3 %collective-permute-start.3 = (f32[8,128]{1,0:T(8,128)S(1)}, f32[8,128]{1,0:T(8,128)S(1)}, u32[]{:S(2)}, u32[]{:S(2)}) collective-permute-start(f32[8,128]{1,0:T(8,128)S(1)} %shard_map.77.own), channel_id=1, source_target_pairs={{8,16},{16,8},{24,32},{32,24},{40,48},{48,40},{56,64},{64,56},{72,... | collective-permute-start | bytes 12296 | tf_op jit(solution)/shard_map/ppermute | solution.py:389
  4.3 14.2 %collective-permute-start.2 = (f32[8,128]{1,0:T(8,128)S(1)}, f32[8,128]{1,0:T(8,128)S(1)}, u32[]{:S(2)}, u32[]{:S(2)}) collective-permute-start(f32[8,128]{1,0:T(8,128)S(1)} %shard_map.77.own), channel_id=1, source_target_pairs={{0,8},{8,0},{16,24},{24,16},{32,40},{40,32},{48,56},{56,48},{64,72... | collective-permute-start | bytes 12296 | tf_op jit(solution)/shard_map/ppermute | solution.py:389
  18.6 2.9 %collective-permute-start.1 = (f32[8,128]{1,0:T(8,128)S(1)}, f32[8,128]{1,0:T(8,128)S(1)}, u32[]{:S(2)}, u32[]{:S(2)}) collective-permute-start(f32[8,128]{1,0:T(8,128)S(1)} %shard_map.77.own), channel_id=1, source_target_pairs={{0,1},{1,0},{2,3},{3,2},{4,5},{5,4},{6,7},{7,6},{8,9},{9,8},{10,11... | collective-permute-start | bytes 12296 | tf_op jit(solution)/shard_map/ppermute | solution.py:389
  21.5 2.9 %collective-permute-start = (f32[8,128]{1,0:T(8,128)S(1)}, f32[8,128]{1,0:T(8,128)S(1)}, u32[]{:S(2)}, u32[]{:S(2)}) collective-permute-start(f32[8,128]{1,0:T(8,128)S(1)} %shard_map.77.own), channel_id=1, source_target_pairs={{1,2},{2,1},{3,4},{4,3},{5,6},{6,5},{9,10},{10,9},{11,12},{12,11},... | collective-permute-start | bytes 12296 | tf_op jit(solution)/shard_map/ppermute | solution.py:389
  24.4 0.0 collective-permute-done.3.x2
  24.5 0.0 collective-permute-done.2.x1
  24.5 0.0 collective-permute-done.1.y1
  24.5 2.5 %collective-permute-done.y2 = f32[8,128]{1,0:T(8,128)S(1)} collective-permute-done((f32[8,128]{1,0:T(8,128)S(1)}, f32[8,128]{1,0:T(8,128)S(1)}, u32[]{:S(2)}, u32[]{:S(2)}) %collective-permute-start) | collective-permute-done | bytes 4128 | tf_op jit(solution)/shard_map/ppermute | solution.py:389
  27.0 0.0 copy-done.4
  27.0 0.0 copy-done.5
  27.0 0.0 copy-done.6
  27.0 0.0 copy-start
  27.0 0.9 copy-done
  27.9 1.8 %shard_map.78 = (f32[16,16,128]{2,1,0:T(8,128)S(1)}, f32[32,128]{1,0:T(8,128)S(1)}, f32[16,128]{1,0:T(8,128)S(1)}, f32[16,128]{1,0:T(8,128)S(1)}, f32[16,128]{1,...) custom-call(f32[16,16,128]{2,1,0:T(8,128)S(1)} %copy-done, f32[16]{0:T(128)S(1)} %copy-done.6, ...), custom_call_target="tpu_custom_call" | custom-call | tf_op jit(solution)/shard_map/pallas_call | solution.py:417
  29.8 10.6 %all_to_all.44 = f32[32,1,128]{2,1,0:T(1,128)S(1)} all-to-all(f32[32,1,128]{2,1,0:T(1,128)S(1)} %bitcast.18), channel_id=1, replica_groups=mesh['half'=2,'plane'=32,'narrow'=8] {'plane'}, dimensions={0} | all-to-all | bytes 32768 | tf_op jit(solution)/shard_map/all_to_all | solution.py:401
  40.4 0.6 shard_map.79
  41.0 5.9 %all-to-all-start.1 = ((f32[16,4,128]{2,1,0:T(4,128)}), f32[16,4,128]{2,1,0:T(4,128)S(1)}, u32[]{:S(2)}, u32[]{:S(2)}) async-start(f32[16,4,128]{2,1,0:T(4,128)} %bitcast.4), calls=%async_computation.1 | async-start | bytes 65536 | tf_op jit(solution)/shard_map/all_to_all | solution.py:403
  46.9 2.0 %collective-permute-start.4 = (f32[16,128]{1,0:T(8,128)S(1)}, f32[16,128]{1,0:T(8,128)S(1)}, u32[]{:S(2)}, u32[]{:S(2)}) collective-permute-start(f32[16,128]{1,0:T(8,128)S(1)} %shard_map.80), channel_id=1, source_target_pairs={{1,0},{2,1},{3,2},{4,3},{5,4},{6,5},{7,6},{9,8},{10,9},{11,10},{12... | collective-permute-start | bytes 24584 | tf_op jit(solution)/shard_map/ppermute | solution.py:416
  48.9 3.5 %collective-permute-done.4.far = f32[16,128]{1,0:T(8,128)S(1)} collective-permute-done((f32[16,128]{1,0:T(8,128)S(1)}, f32[16,128]{1,0:T(8,128)S(1)}, u32[]{:S(2)}, u32[]{:S(2)}) %collective-permute-start.4) | collective-permute-done | bytes 8224 | tf_op jit(solution)/shard_map/ppermute | solution.py:416
  52.5 2.1 %collective-permute-start.7 = (f32[32,128]{1,0:T(8,128)S(1)}, f32[32,128]{1,0:T(8,128)S(1)}, u32[]{:S(2)}, u32[]{:S(2)}) collective-permute-start(f32[32,128]{1,0:T(8,128)S(1)} %get-tuple-element.28), channel_id=1, source_target_pairs={{0,1},{1,0},{2,3},{3,2},{4,5},{5,4},{6,7},{7,6},{8,9},{9,8},{10,11... | collective-permute-start | bytes 49160 | tf_op jit(solution)/shard_map/ppermute | solution.py:389
  54.6 5.8 %collective-permute-start.8 = (f32[32,128]{1,0:T(8,128)S(1)}, f32[32,128]{1,0:T(8,128)S(1)}, u32[]{:S(2)}, u32[]{:S(2)}) collective-permute-start(f32[32,128]{1,0:T(8,128)S(1)} %get-tuple-element.29), channel_id=1, source_target_pairs={{1,2},{2,1},{3,4},{4,3},{5,6},{6,5},{9,10},{10,9},{11,12},{12,11},... | collective-permute-start | bytes 49160 | tf_op jit(solution)/shard_map/ppermute | solution.py:389
  60.4 1.9 %collective-permute-start.5 = (f32[24,128]{1,0:T(8,128)S(1)}, f32[24,128]{1,0:T(8,128)S(1)}, u32[]{:S(2)}, u32[]{:S(2)}) collective-permute-start(f32[24,128]{1,0:T(8,128)S(1)} %get-tuple-element.26), channel_id=1, source_target_pairs={{8,16},{16,8},{24,32},{32,24},{40,48},{48,40},{56,64},{64,56},{72,... | collective-permute-start | bytes 36872 | tf_op jit(solution)/shard_map/ppermute | solution.py:389
  62.4 0.0 copy-start.1
  62.4 12.6 %collective-permute-start.6 = (f32[24,128]{1,0:T(8,128)S(1)}, f32[24,128]{1,0:T(8,128)S(1)}, u32[]{:S(2)}, u32[]{:S(2)}) collective-permute-start(f32[24,128]{1,0:T(8,128)S(1)} %get-tuple-element.27), channel_id=1, source_target_pairs={{0,8},{8,0},{16,24},{24,16},{32,40},{40,32},{48,56},{56,48},{64,72... | collective-permute-start | bytes 36872 | tf_op jit(solution)/shard_map/ppermute | solution.py:389
  75.0 0.0 collective-permute-done.5.q2
  75.0 0.8 collective-permute-done.6.q1
  75.8 0.0 collective-permute-done.7.r1
  75.8 0.0 collective-permute-done.8.r2
  75.8 1.0 shard_map.82.shifted
  76.8 0.0 all-to-all-done.1
  76.9 0.0 copy-done.1
  76.9 2.2 %shard_map.83 = (f32[16,16,128]{2,1,0:T(8,128)S(1)}, f32[32,128]{1,0:T(8,128)S(1)}, f32[16,128]{1,0:T(8,128)S(1)}, f32[16,128]{1,0:T(8,128)S(1)}, f32[16,128]{1,0:T(8,128)S(1)}, /*index=5*/f32[16,128]{1,0:T(8,128)S(1)}) custom-call(f32[16,16,128]{2,1,0:T(8,128)S(1)} %copy-done.1, f32[8]{0:T(128)S(1)} %copy-done.4, s32[2]{0:T(128)S(1)} %bitcast.20, ...), custom_call_target="tpu_custom_call" | custom-call | tf_op jit(solution)/shard_map/pallas_call | solution.py:432
  79.0 10.7 %all_to_all.45 = f32[32,1,128]{2,1,0:T(1,128)S(1)} all-to-all(f32[32,1,128]{2,1,0:T(1,128)S(1)} %bitcast.17), channel_id=1, replica_groups=mesh['half'=2,'plane'=32,'narrow'=8] {'plane'}, dimensions={0} | all-to-all | bytes 32768 | tf_op jit(solution)/shard_map/all_to_all | solution.py:401
  89.7 0.6 shard_map.84
  90.4 11.5 %all-to-all-start.3 = ((f32[16,4,128]{2,1,0:T(4,128)}), f32[16,4,128]{2,1,0:T(4,128)S(1)}, u32[]{:S(2)}, u32[]{:S(2)}) async-start(f32[16,4,128]{2,1,0:T(4,128)} %bitcast.9), calls=%async_computation.3 | async-start | bytes 65536 | tf_op jit(solution)/shard_map/all_to_all | solution.py:403
  101.9 1.9 %collective-permute-start.9 = (f32[16,128]{1,0:T(8,128)S(1)}, f32[16,128]{1,0:T(8,128)S(1)}, u32[]{:S(2)}, u32[]{:S(2)}) collective-permute-start(f32[16,128]{1,0:T(8,128)S(1)} %get-tuple-element.32), channel_id=1, source_target_pairs={{8,16},{16,8},{24,32},{32,24},{40,48},{48,40},{56,64},{64,56},{72,... | collective-permute-start | bytes 24584 | tf_op jit(solution)/shard_map/ppermute | solution.py:389
  103.8 14.4 %collective-permute-start.10 = (f32[16,128]{1,0:T(8,128)S(1)}, f32[16,128]{1,0:T(8,128)S(1)}, u32[]{:S(2)}, u32[]{:S(2)}) collective-permute-start(f32[16,128]{1,0:T(8,128)S(1)} %get-tuple-element.33), channel_id=1, source_target_pairs={{0,8},{8,0},{16,24},{24,16},{32,40},{40,32},{48,56},{56,48},{64,72... | collective-permute-start | bytes 24584 | tf_op jit(solution)/shard_map/ppermute | solution.py:389
  118.1 3.4 %collective-permute-start.11 = (f32[16,128]{1,0:T(8,128)S(1)}, f32[16,128]{1,0:T(8,128)S(1)}, u32[]{:S(2)}, u32[]{:S(2)}) collective-permute-start(f32[16,128]{1,0:T(8,128)S(1)} %get-tuple-element.34), channel_id=1, source_target_pairs={{0,1},{1,0},{2,3},{3,2},{4,5},{5,4},{6,7},{7,6},{8,9},{9,8},{10,11... | collective-permute-start | bytes 24584 | tf_op jit(solution)/shard_map/ppermute | solution.py:389
  121.5 1.9 %collective-permute-start.12 = (f32[16,128]{1,0:T(8,128)S(1)}, f32[16,128]{1,0:T(8,128)S(1)}, u32[]{:S(2)}, u32[]{:S(2)}) collective-permute-start(f32[16,128]{1,0:T(8,128)S(1)} %get-tuple-element.35), channel_id=1, source_target_pairs={{1,2},{2,1},{3,4},{4,3},{5,6},{6,5},{9,10},{10,9},{11,12},{12,11},... | collective-permute-start | bytes 24584 | tf_op jit(solution)/shard_map/ppermute | solution.py:389
  123.4 0.0 collective-permute-done.9.q2
  123.5 0.0 collective-permute-done.10.q1
  123.5 0.2 collective-permute-done.11.r1
  123.7 3.4 %collective-permute-done.12.r2 = f32[16,128]{1,0:T(8,128)S(1)} collective-permute-done((f32[16,128]{1,0:T(8,128)S(1)}, f32[16,128]{1,0:T(8,128)S(1)}, u32[]{:S(2)}, u32[]{:S(2)}) %collective-permute-start.12) | collective-permute-done | bytes 8224 | tf_op jit(solution)/shard_map/ppermute | solution.py:389
  127.1 0.0 all-to-all-done.3
  127.1 1.4 %shard_map.85 = (bf16[16,16,128]{2,1,0:T(8,128)(2,1)}, bf16[16,16,128]{2,1,0:T(8,128)(2,1)}) custom-call(f32[16,16,128]{2,1,0:T(8,128)S(1)} %copy-done.1, f32[16,128]{1,0:T(8,128)S(1)} %get-tuple-element.19.kap, f32[16,16,128]{2,1,0:T(8,128)S(1)} %get-tuple-element.30.old, f32[64,128]{1,0:T(8,128)S(1)} %bitcast.14, f32[192,512]{1,0:T(8,128)S(1)} %shard_map.82.shifted, ...), custom_call_target="tpu_custom_call" | custom-call | tf_op jit(solution)/shard_map/pallas_call | solution.py:441
  (7 shorter events, 0.0 us)
Async XLA Ops:
  0.6 0.7 copy-start.2
  1.3 0.7 copy-start.3
  2.0 25.0 %copy-start.4 = (f32[8]{0:T(128)S(1)}, f32[8]{0:T(128)}, u32[]{:S(2)}) copy-start(f32[8]{0:T(128)} %robin_table.3) | copy-start | bytes 100
  2.0 25.0 %copy-start.5 = (s32[1,1,2]{2,1,0:T(1,128)S(1)}, s32[1,1,2]{2,1,0:T(1,128)}, u32[]{:S(2)}) copy-start(s32[1,1,2]{2,1,0:T(1,128)} %param.10) | copy-start | bytes 28
  2.0 25.0 %copy-start.6 = (f32[16]{0:T(128)S(1)}, f32[16]{0:T(128)}, u32[]{:S(2)}) copy-start(f32[16]{0:T(128)} %table.1) | copy-start | bytes 196
  2.0 22.4 %collective-permute-start.3 = (f32[8,128]{1,0:T(8,128)S(1)}, f32[8,128]{1,0:T(8,128)S(1)}, u32[]{:S(2)}, u32[]{:S(2)}) collective-permute-start(f32[8,128]{1,0:T(8,128)S(1)} %shard_map.77.own), channel_id=1, source_target_pairs={{8,16},{16,8},{24,32},{32,24},{40,48},{48,40},{56,64},{64,56},{72,... | collective-permute-start | bytes 12296 | tf_op jit(solution)/shard_map/ppermute | solution.py:389
  4.3 20.1 %collective-permute-start.2 = (f32[8,128]{1,0:T(8,128)S(1)}, f32[8,128]{1,0:T(8,128)S(1)}, u32[]{:S(2)}, u32[]{:S(2)}) collective-permute-start(f32[8,128]{1,0:T(8,128)S(1)} %shard_map.77.own), channel_id=1, source_target_pairs={{0,8},{8,0},{16,24},{24,16},{32,40},{40,32},{48,56},{56,48},{64,72... | collective-permute-start | bytes 12296 | tf_op jit(solution)/shard_map/ppermute | solution.py:389
  18.6 5.9 %collective-permute-start.1 = (f32[8,128]{1,0:T(8,128)S(1)}, f32[8,128]{1,0:T(8,128)S(1)}, u32[]{:S(2)}, u32[]{:S(2)}) collective-permute-start(f32[8,128]{1,0:T(8,128)S(1)} %shard_map.77.own), channel_id=1, source_target_pairs={{0,1},{1,0},{2,3},{3,2},{4,5},{5,4},{6,7},{7,6},{8,9},{9,8},{10,11... | collective-permute-start | bytes 12296 | tf_op jit(solution)/shard_map/ppermute | solution.py:389
  21.5 5.5 %collective-permute-start = (f32[8,128]{1,0:T(8,128)S(1)}, f32[8,128]{1,0:T(8,128)S(1)}, u32[]{:S(2)}, u32[]{:S(2)}) collective-permute-start(f32[8,128]{1,0:T(8,128)S(1)} %shard_map.77.own), channel_id=1, source_target_pairs={{1,2},{2,1},{3,4},{4,3},{5,6},{6,5},{9,10},{10,9},{11,12},{12,11},... | collective-permute-start | bytes 12296 | tf_op jit(solution)/shard_map/ppermute | solution.py:389
  27.0 0.9 copy-start
  41.0 35.8 %all-to-all-start.1 = ((f32[16,4,128]{2,1,0:T(4,128)}), f32[16,4,128]{2,1,0:T(4,128)S(1)}, u32[]{:S(2)}, u32[]{:S(2)}) async-start(f32[16,4,128]{2,1,0:T(4,128)} %bitcast.4), calls=%async_computation.1 | async-start | bytes 65536 | tf_op jit(solution)/shard_map/all_to_all | solution.py:403
  46.9 5.5 %collective-permute-start.4 = (f32[16,128]{1,0:T(8,128)S(1)}, f32[16,128]{1,0:T(8,128)S(1)}, u32[]{:S(2)}, u32[]{:S(2)}) collective-permute-start(f32[16,128]{1,0:T(8,128)S(1)} %shard_map.80), channel_id=1, source_target_pairs={{1,0},{2,1},{3,2},{4,3},{5,4},{6,5},{7,6},{9,8},{10,9},{11,10},{12... | collective-permute-start | bytes 24584 | tf_op jit(solution)/shard_map/ppermute | solution.py:416
  52.5 23.4 %collective-permute-start.7 = (f32[32,128]{1,0:T(8,128)S(1)}, f32[32,128]{1,0:T(8,128)S(1)}, u32[]{:S(2)}, u32[]{:S(2)}) collective-permute-start(f32[32,128]{1,0:T(8,128)S(1)} %get-tuple-element.28), channel_id=1, source_target_pairs={{0,1},{1,0},{2,3},{3,2},{4,5},{5,4},{6,7},{7,6},{8,9},{9,8},{10,11... | collective-permute-start | bytes 49160 | tf_op jit(solution)/shard_map/ppermute | solution.py:389
  54.6 21.2 %collective-permute-start.8 = (f32[32,128]{1,0:T(8,128)S(1)}, f32[32,128]{1,0:T(8,128)S(1)}, u32[]{:S(2)}, u32[]{:S(2)}) collective-permute-start(f32[32,128]{1,0:T(8,128)S(1)} %get-tuple-element.29), channel_id=1, source_target_pairs={{1,2},{2,1},{3,4},{4,3},{5,6},{6,5},{9,10},{10,9},{11,12},{12,11},... | collective-permute-start | bytes 49160 | tf_op jit(solution)/shard_map/ppermute | solution.py:389
  60.4 14.6 %collective-permute-start.5 = (f32[24,128]{1,0:T(8,128)S(1)}, f32[24,128]{1,0:T(8,128)S(1)}, u32[]{:S(2)}, u32[]{:S(2)}) collective-permute-start(f32[24,128]{1,0:T(8,128)S(1)} %get-tuple-element.26), channel_id=1, source_target_pairs={{8,16},{16,8},{24,32},{32,24},{40,48},{48,40},{56,64},{64,56},{72,... | collective-permute-start | bytes 36872 | tf_op jit(solution)/shard_map/ppermute | solution.py:389
  62.4 14.5 %copy-start.1 = (f32[16,16,128]{2,1,0:T(8,128)S(1)}, f32[16,16,128]{2,1,0:T(8,128)}, u32[]{:S(2)}) copy-start(f32[16,16,128]{2,1,0:T(8,128)} %right.5) | copy-start | bytes 393220
  62.4 13.5 %collective-permute-start.6 = (f32[24,128]{1,0:T(8,128)S(1)}, f32[24,128]{1,0:T(8,128)S(1)}, u32[]{:S(2)}, u32[]{:S(2)}) collective-permute-start(f32[24,128]{1,0:T(8,128)S(1)} %get-tuple-element.27), channel_id=1, source_target_pairs={{0,8},{8,0},{16,24},{24,16},{32,40},{40,32},{48,56},{56,48},{64,72... | collective-permute-start | bytes 36872 | tf_op jit(solution)/shard_map/ppermute | solution.py:389
  90.4 36.7 %all-to-all-start.3 = ((f32[16,4,128]{2,1,0:T(4,128)}), f32[16,4,128]{2,1,0:T(4,128)S(1)}, u32[]{:S(2)}, u32[]{:S(2)}) async-start(f32[16,4,128]{2,1,0:T(4,128)} %bitcast.9), calls=%async_computation.3 | async-start | bytes 65536 | tf_op jit(solution)/shard_map/all_to_all | solution.py:403
  101.9 21.6 %collective-permute-start.9 = (f32[16,128]{1,0:T(8,128)S(1)}, f32[16,128]{1,0:T(8,128)S(1)}, u32[]{:S(2)}, u32[]{:S(2)}) collective-permute-start(f32[16,128]{1,0:T(8,128)S(1)} %get-tuple-element.32), channel_id=1, source_target_pairs={{8,16},{16,8},{24,32},{32,24},{40,48},{48,40},{56,64},{64,56},{72,... | collective-permute-start | bytes 24584 | tf_op jit(solution)/shard_map/ppermute | solution.py:389
  103.8 19.7 %collective-permute-start.10 = (f32[16,128]{1,0:T(8,128)S(1)}, f32[16,128]{1,0:T(8,128)S(1)}, u32[]{:S(2)}, u32[]{:S(2)}) collective-permute-start(f32[16,128]{1,0:T(8,128)S(1)} %get-tuple-element.33), channel_id=1, source_target_pairs={{0,8},{8,0},{16,24},{24,16},{32,40},{40,32},{48,56},{56,48},{64,72... | collective-permute-start | bytes 24584 | tf_op jit(solution)/shard_map/ppermute | solution.py:389
  118.1 5.5 %collective-permute-start.11 = (f32[16,128]{1,0:T(8,128)S(1)}, f32[16,128]{1,0:T(8,128)S(1)}, u32[]{:S(2)}, u32[]{:S(2)}) collective-permute-start(f32[16,128]{1,0:T(8,128)S(1)} %get-tuple-element.34), channel_id=1, source_target_pairs={{0,1},{1,0},{2,3},{3,2},{4,5},{5,4},{6,7},{7,6},{8,9},{9,8},{10,11... | collective-permute-start | bytes 24584 | tf_op jit(solution)/shard_map/ppermute | solution.py:389
  121.5 5.5 %collective-permute-start.12 = (f32[16,128]{1,0:T(8,128)S(1)}, f32[16,128]{1,0:T(8,128)S(1)}, u32[]{:S(2)}, u32[]{:S(2)}) collective-permute-start(f32[16,128]{1,0:T(8,128)S(1)} %get-tuple-element.35), channel_id=1, source_target_pairs={{1,2},{2,1},{3,4},{4,3},{5,6},{6,5},{9,10},{10,9},{11,12},{12,11},... | collective-permute-start | bytes 24584 | tf_op jit(solution)/shard_map/ppermute | solution.py:389

commit v6 on v5

--- a/solution.py
+++ b/solution.py
@@ -192,7 +192,7 @@
     from_south, from_north = sided(even_y, y1[...], y2[...])
     keys = jnp.concatenate([own[...], from_west, from_east, from_south, from_north], 0)
     pick = (iota((NZ, NZ), 0) == iota((NZ, NZ), 1) // BLOCK).astype(F32)
-    keys = jnp.dot(keys, pick, precision=EXACT, preferred_element_type=F32)
+    keys = jnp.dot(keys, pick, preferred_element_type=F32)
     found = jnp.zeros_like(keys)
     for m in range(MATERIALS):
         found = jnp.where(jnp.abs(keys - m) < 0.5, table[m], found)
@@ -220,45 +220,47 @@
     sx2[0:CY, :] = jnp.where(even_x, u[0], u[CX - 1])
 
 
-def join_kernel(x1, x2, out):
-    out[0:8, :] = x1[...]
-    out[8:16, :] = x2[...]
-
-
-def ride_kernel(x2, x1, y1, y2, far, fx2, fx1, fy1, fy2, px2, px1, py1, py2):
+def put_rows(out, face, pieces):
+    out[0:CX, :] = face[...]
+    for k, piece in enumerate((*pieces, jnp.zeros((4, NZ), F32))):
+        out[CX + 4 * k : CX + 4 * k + 4, :] = piece
+
+
+def taken(value, k):
+    return value[CX + 4 * k : CX + 4 * k + 4]
+
+
+def ride_x_kernel(x2, x1, y1, y2, fx2, fx1, px2, px1):
     even_x, even_y, _ = place()
     east = sided(even_x, x1[...], x2[...])[1][4:8]
+    south, north = (p[4:8] for p in sided(even_y, y1[...], y2[...]))
+    for out, face in ((px2, fx2), (px1, fx1)):
+        put_rows(out, face, (east, north, south))
+
+
+def ride_y_kernel(y1, y2, q2, q1, fy1, fy2, py1, py2):
+    even_x, even_y, _ = place()
     north = sided(even_y, y1[...], y2[...])[1][4:8]
-    corner = sided(even_x, far[0:8], far[8:16])[1][4:8]
-    for out, face in ((px2, fx2), (px1, fx1)):
-        out[0:CY, :] = face[...]
-        out[CY : CY + 4, :] = east
-        out[CY + 4 : CY + 8, :] = corner
+    beyond = sided(even_x, q1[...], q2[...])[1]
     for out, face in ((py1, fy1), (py2, fy2)):
-        out[0:CX, :] = face[...]
-        out[CX : CX + 4, :] = north
-        out[CX + 4 : CX + 8, :] = corner
-        out[CX + 8 : CX + 12, :] = east
-        out[CX + 12 : CX + 16, :] = jnp.zeros((4, NZ), F32)
-
-
-def widen_kernel(own, x2, x1, y1, y2, far, q2, q1, r1, r2, shifted, rows, moves):
+        put_rows(out, face, (north, taken(beyond, 0), taken(beyond, 1)))
+
+
+def widen_kernel(own, x2, x1, y1, y2, q2, q1, r1, r2, shifted, rows, moves):
     even_x, even_y, _ = place()
-    seen = (q2, q1, r1, r2)
     count = rows.shape[1]
     narrow_count = lax.axis_size("narrow")
     wide_count = count // narrow_count
     west, east = (p[4:8] for p in sided(even_x, x1[...], x2[...]))
     south, north = (p[4:8] for p in sided(even_y, y1[...], y2[...]))
-    corners = [p[4:8] for p in sided(even_x, far[0:8], far[8:16])]
-    beyond_x = sided(even_x, seen[1][...], seen[0][...])[1]
-    below, above = sided(even_y, seen[2][...], seen[3][...])
+    before, beyond = sided(even_x, q1[...], q2[...])
+    above = sided(even_y, r1[...], r2[...])[1]
     held = (
-        own[4:8], east, north, corners[1],
-        west, corners[0],
-        beyond_x[CY : CY + 4], beyond_x[CY + 4 : CY + 8],
-        south, below[CX + 8 : CX + 12],
-        above[CX : CX + 4], above[CX + 4 : CX + 8],
+        own[4:8], east, north, taken(beyond, 1),
+        west, taken(before, 1),
+        taken(beyond, 0), taken(above, 1),
+        south, taken(beyond, 2),
+        taken(above, 0), taken(above, 2),
     )
     rows[...] = jnp.zeros_like(rows)
     for k, piece in enumerate(held):
@@ -283,11 +285,13 @@
 def turn_kernel(arrived, out):
     groups = arrived.shape[0] // 8
     mine = iota((8, NZ), 1) // 16 == iota((8, NZ), 0)
+    rows = []
     for q in range(groups):
         kept = jnp.where(mine, arrived[8 * q : 8 * q + 8, :], 0.0)
-        row = jnp.sum(kept, axis=0, keepdims=True)
-        for b in range(out.shape[0] // groups):
-            out[b * groups + q : b * groups + q + 1, :] = row
+        rows.append(jnp.sum(kept, axis=0, keepdims=True))
+    tile = jnp.concatenate(rows * (8 // groups), 0)
+    for b in range(out.shape[0] // 8):
+        out[8 * b : 8 * b + 8, :] = tile
 
 
 def window(every, shifted, opened):
@@ -397,45 +401,47 @@
     return x2, x1, y1, y2
 
 
-def everywhere(values, count):
-    near = lax.all_to_all(values, "plane", 0, 0, tiled=True)
+def gather_plane(values):
+    return lax.all_to_all(values, "plane", 0, 0, tiled=True)
+
+
+def gather_line(near, count):
     turned = call(turn_kernel, jax.ShapeDtypeStruct((count // 8, NZ), F32), [VMEM])(near)
     return lax.all_to_all(turned, ("half", "narrow"), 0, 0, tiled=True)
 
 
 def body(right_side, labels, material_table, robin_table, robin_index, coarse_rows):
     count = coarse_rows.shape[1]
-    narrow_count = lax.axis_size("narrow")
     shape = lambda *dims: jax.ShapeDtypeStruct(dims, F32)
     scratch = lambda *dims: pltpu.VMEM(dims, F32)
     field, face, mine = shape(CX, CY, NZ), shape(CY, NZ), shape(lax.axis_size("plane"), NZ)
     index = robin_index[0, 0]
     pay = call(pack_kernel, shape(8, NZ), [VMEM] * 2)(labels, coarse_rows)
     x2, x1, y1, y2 = swaps(pay, pay, pay, pay)
-    both = call(join_kernel, shape(16, NZ), [VMEM] * 2)(x1, x2)
-    far = lax.ppermute(both, "narrow", [(i + 1, i) for i in range(narrow_count - 1)])
-    u, sent, kap, *edges = call(
+    u, sent, kap, fx2, fx1, fy1, fy2 = call(
         first_kernel,
         (field, mine, shape(16, NZ), face, face, face, face),
         [VMEM] + [SMEM] * 3 + [VMEM] * 5,
         [scratch(16, NZ)],
     )(right_side, material_table, robin_table, index, pay, y2, y1, x1, x2)
-    every = everywhere(sent, count)
-    edges = call(
-        ride_kernel, (shape(CY + 8, NZ),) * 2 + (shape(CX + 16, NZ),) * 2, [VMEM] * 9
-    )(x2, x1, y1, y2, far, *edges)
-    seen = swaps(*edges)
-    lines = 16 * len(SHIFTS)
+    near = gather_plane(sent)
+    ridden, lines = (shape(CX + 16, NZ),) * 2, 16 * len(SHIFTS)
+    px2, px1 = call(ride_x_kernel, ridden, [VMEM] * 6)(x2, x1, y1, y2, fx2, fx1)
+    q2, q1 = swap(px2, WIDE, 1), swap(px1, WIDE, 0)
+    every = gather_line(near, count)
+    py1, py2 = call(ride_y_kernel, ridden, [VMEM] * 6)(y1, y2, q2, q1, fy1, fy2)
+    seen = (q2, q1, swap(py1, "narrow", 0), swap(py2, "narrow", 1))
     shifted = call(
-        widen_kernel, shape(lines, count), [VMEM] * 10, [scratch(16, count), scratch(lines, count)]
-    )(pay, x2, x1, y1, y2, far, *seen)
+        widen_kernel, shape(lines, count), [VMEM] * 9, [scratch(16, count), scratch(lines, count)]
+    )(pay, x2, x1, y1, y2, *seen)
     u, sent, *edges = call(
         second_kernel,
         (field, mine, face, face, face, face),
         [VMEM] + [SMEM] * 2 + [VMEM] * 8,
         [scratch(CX, CY, NZ), scratch(16, NZ), scratch(count, NZ)],
     )(right_side, robin_table, index, kap, u, every, shifted, *seen)
-    every = everywhere(sent, count)
+    near = gather_plane(sent)
+    every = gather_line(near, count)
     seen = swaps(*edges)
     half = jax.ShapeDtypeStruct((CX, CY, NZ), jnp.bfloat16)
     return call(last_kernel, (half, half), [VMEM] * 9, [scratch(CX, CY, NZ), scratch(count, NZ)])(

time: 129 us -> 127 us (0.984)
  starting transfers between devices: 85.9 us -> 83.2 us
    ppermute x12, waiting for transfers between devices: 6.94 us -> 10.6 us  [swap(): return lax.ppermute(array, axis, swap_pairs(lax.axis_size(axis), start))]
    ppermute x1 -> x0, waiting for transfers between devices: 3.52 us -> none  [body(): lax.ppermute(both, 'narrow', [(i + 1, i) for i in range(narrow_count - 1)])]
    ppermute x1 -> x0, starting transfers between devices: 2.01 us -> none  [body(): lax.ppermute(both, 'narrow', [(i + 1, i) for i in range(narrow_count - 1)])]
  transfers between devices with their start and end apart: 15 -> 14, of which waited for: 5 -> 6; matrix products, arithmetic and copies ran while one was open for 0% -> 0% of each run, Pallas kernels for 1% -> 1%
where the time goes in v6:
time: 127 us; the launch traced here: 126 us
  starting transfers between devices  83.2 us (66%)
  blocking collectives  21.2 us (17%)
  waiting for transfers between devices  10.6 us (8%)
  Pallas kernels  7.62 us (6%)
  local copies, waits for them, and re-layouts  2.27 us (2%)
    ppermute x12, starting transfers between devices, swap(): return lax.ppermute(array, axis, swap_pairs(lax.axis_size(axis), start))  65.6 us
    all_to_all x2, blocking collectives, gather_plane(): return lax.all_to_all(values, 'plane', 0, 0, tiled=True)  21.2 us
    all_to_all x2, starting transfers between devices, gather_line(): return lax.all_to_all(turned, ('half', 'narrow'), 0, 0, tiled=True)  17.7 us
    ppermute x12, waiting for transfers between devices, swap(): return lax.ppermute(array, axis, swap_pairs(lax.axis_size(axis), start))  10.6 us
  transfers between devices with their start and end apart: 14, of which 6 were waited for; matrix products, arithmetic and copies ran while one was open for 0% of the time, Pallas kernels for 1%

profile of v6, /device:TPU:62, one launch (start us, length us, event | category | flops | bytes accessed | tf_op | source)
XLA Modules:
  0.0 125.9 jit_solution(13943965000477286389)
XLA Ops:
  0.6 0.0 copy-start.4
  0.6 0.7 copy-done.4
  1.3 0.0 copy-start.5
  1.3 0.7 copy-done.5
  2.0 0.0 copy-start.2
  2.0 2.3 %collective-permute-start.3 = (f32[8,128]{1,0:T(8,128)S(1)}, f32[8,128]{1,0:T(8,128)S(1)}, u32[]{:S(2)}, u32[]{:S(2)}) collective-permute-start(f32[8,128]{1,0:T(8,128)S(1)} %shard_map.77.own), channel_id=1, source_target_pairs={{8,16},{16,8},{24,32},{32,24},{40,48},{48,40},{56,64},{64,56},{72,... | collective-permute-start | bytes 12296 | tf_op jit(solution)/shard_map/ppermute | solution.py:393
  4.3 14.2 %collective-permute-start.2 = (f32[8,128]{1,0:T(8,128)S(1)}, f32[8,128]{1,0:T(8,128)S(1)}, u32[]{:S(2)}, u32[]{:S(2)}) collective-permute-start(f32[8,128]{1,0:T(8,128)S(1)} %shard_map.77.own), channel_id=1, source_target_pairs={{0,8},{8,0},{16,24},{24,16},{32,40},{40,32},{48,56},{56,48},{64,72... | collective-permute-start | bytes 12296 | tf_op jit(solution)/shard_map/ppermute | solution.py:393
  18.6 2.9 %collective-permute-start.1 = (f32[8,128]{1,0:T(8,128)S(1)}, f32[8,128]{1,0:T(8,128)S(1)}, u32[]{:S(2)}, u32[]{:S(2)}) collective-permute-start(f32[8,128]{1,0:T(8,128)S(1)} %shard_map.77.own), channel_id=1, source_target_pairs={{0,1},{1,0},{2,3},{3,2},{4,5},{5,4},{6,7},{7,6},{8,9},{9,8},{10,11... | collective-permute-start | bytes 12296 | tf_op jit(solution)/shard_map/ppermute | solution.py:393
  21.5 2.9 %collective-permute-start = (f32[8,128]{1,0:T(8,128)S(1)}, f32[8,128]{1,0:T(8,128)S(1)}, u32[]{:S(2)}, u32[]{:S(2)}) collective-permute-start(f32[8,128]{1,0:T(8,128)S(1)} %shard_map.77.own), channel_id=1, source_target_pairs={{1,2},{2,1},{3,4},{4,3},{5,6},{6,5},{9,10},{10,9},{11,12},{12,11},... | collective-permute-start | bytes 12296 | tf_op jit(solution)/shard_map/ppermute | solution.py:393
  24.4 0.0 collective-permute-done.3.x2
  24.5 0.0 collective-permute-done.2.x1
  24.5 0.0 collective-permute-done.1.y1
  24.5 2.5 %collective-permute-done.y2 = f32[8,128]{1,0:T(8,128)S(1)} collective-permute-done((f32[8,128]{1,0:T(8,128)S(1)}, f32[8,128]{1,0:T(8,128)S(1)}, u32[]{:S(2)}, u32[]{:S(2)}) %collective-permute-start) | collective-permute-done | bytes 4128 | tf_op jit(solution)/shard_map/ppermute | solution.py:393
  27.0 0.0 copy-done.2
  27.0 0.0 copy-done.3
  27.0 0.0 copy-done.6
  27.0 0.0 copy-start
  27.0 0.9 copy-done
  27.9 1.8 %shard_map.78 = (f32[16,16,128]{2,1,0:T(8,128)S(1)}, f32[32,128]{1,0:T(8,128)S(1)}, f32[16,128]{1,0:T(8,128)S(1)}, f32[16,128]{1,0:T(8,128)S(1)}, f32[16,128]{1,...) custom-call(f32[16,16,128]{2,1,0:T(8,128)S(1)} %copy-done, f32[16]{0:T(128)S(1)} %copy-done.6, ...), custom_call_target="tpu_custom_call" | custom-call | tf_op jit(solution)/shard_map/pallas_call | solution.py:421
  29.7 10.6 %all_to_all.44 = f32[32,1,128]{2,1,0:T(1,128)S(1)} all-to-all(f32[32,1,128]{2,1,0:T(1,128)S(1)} %bitcast.18), channel_id=1, replica_groups=mesh['half'=2,'plane'=32,'narrow'=8] {'plane'}, dimensions={0} | all-to-all | bytes 32768 | tf_op jit(solution)/shard_map/all_to_all | solution.py:405
  40.3 0.6 shard_map.79
  41.0 5.9 %all-to-all-start.1 = ((f32[16,4,128]{2,1,0:T(4,128)}), f32[16,4,128]{2,1,0:T(4,128)S(1)}, u32[]{:S(2)}, u32[]{:S(2)}) async-start(f32[16,4,128]{2,1,0:T(4,128)} %bitcast.4), calls=%async_computation.1 | async-start | bytes 65536 | tf_op jit(solution)/shard_map/all_to_all | solution.py:410
  46.9 1.9 %collective-permute-start.4 = (f32[32,128]{1,0:T(8,128)S(1)}, f32[32,128]{1,0:T(8,128)S(1)}, u32[]{:S(2)}, u32[]{:S(2)}) collective-permute-start(f32[32,128]{1,0:T(8,128)S(1)} %get-tuple-element.24), channel_id=1, source_target_pairs={{8,16},{16,8},{24,32},{32,24},{40,48},{48,40},{56,64},{64,56},{72,... | collective-permute-start | bytes 49160 | tf_op jit(solution)/shard_map/ppermute | solution.py:393
  48.8 14.3 %collective-permute-start.5 = (f32[32,128]{1,0:T(8,128)S(1)}, f32[32,128]{1,0:T(8,128)S(1)}, u32[]{:S(2)}, u32[]{:S(2)}) collective-permute-start(f32[32,128]{1,0:T(8,128)S(1)} %get-tuple-element.25), channel_id=1, source_target_pairs={{0,8},{8,0},{16,24},{24,16},{32,40},{40,32},{48,56},{56,48},{64,72... | collective-permute-start | bytes 49160 | tf_op jit(solution)/shard_map/ppermute | solution.py:393
  63.1 0.0 collective-permute-done.4.q2
  63.1 0.8 collective-permute-done.5.q1
  63.9 3.4 %collective-permute-start.6 = (f32[32,128]{1,0:T(8,128)S(1)}, f32[32,128]{1,0:T(8,128)S(1)}, u32[]{:S(2)}, u32[]{:S(2)}) collective-permute-start(f32[32,128]{1,0:T(8,128)S(1)} %get-tuple-element.28), channel_id=1, source_target_pairs={{0,1},{1,0},{2,3},{3,2},{4,5},{5,4},{6,7},{7,6},{8,9},{9,8},{10,11... | collective-permute-start | bytes 49160 | tf_op jit(solution)/shard_map/ppermute | solution.py:393
  67.3 0.0 copy-start.1
  67.3 2.1 %collective-permute-start.7 = (f32[32,128]{1,0:T(8,128)S(1)}, f32[32,128]{1,0:T(8,128)S(1)}, u32[]{:S(2)}, u32[]{:S(2)}) collective-permute-start(f32[32,128]{1,0:T(8,128)S(1)} %get-tuple-element.29), channel_id=1, source_target_pairs={{1,2},{2,1},{3,4},{4,3},{5,6},{6,5},{9,10},{10,9},{11,12},{12,11},... | collective-permute-start | bytes 49160 | tf_op jit(solution)/shard_map/ppermute | solution.py:393
  69.4 0.2 collective-permute-done.6.r1
  69.6 3.5 %collective-permute-done.7.r2 = f32[32,128]{1,0:T(8,128)S(1)} collective-permute-done((f32[32,128]{1,0:T(8,128)S(1)}, f32[32,128]{1,0:T(8,128)S(1)}, u32[]{:S(2)}, u32[]{:S(2)}) %collective-permute-start.7) | collective-permute-done | bytes 16416 | tf_op jit(solution)/shard_map/ppermute | solution.py:393
  73.1 1.0 shard_map.82.shifted
  74.1 0.0 all-to-all-done.1
  74.1 0.0 copy-done.1
  74.1 2.2 %shard_map.83 = (f32[16,16,128]{2,1,0:T(8,128)S(1)}, f32[32,128]{1,0:T(8,128)S(1)}, f32[16,128]{1,0:T(8,128)S(1)}, f32[16,128]{1,0:T(8,128)S(1)}, f32[16,128]{1,0:T(8,128)S(1)}, /*index=5*/f32[16,128]{1,0:T(8,128)S(1)}) custom-call(f32[16,16,128]{2,1,0:T(8,128)S(1)} %copy-done.1, f32[8]{0:T(128)S(1)} %copy-done.2, s32[2]{0:T(128)S(1)} %bitcast.20, ...), custom_call_target="tpu_custom_call" | custom-call | tf_op jit(solution)/shard_map/pallas_call | solution.py:437
  76.3 10.6 %all_to_all.45 = f32[32,1,128]{2,1,0:T(1,128)S(1)} all-to-all(f32[32,1,128]{2,1,0:T(1,128)S(1)} %bitcast.17), channel_id=1, replica_groups=mesh['half'=2,'plane'=32,'narrow'=8] {'plane'}, dimensions={0} | all-to-all | bytes 32768 | tf_op jit(solution)/shard_map/all_to_all | solution.py:405
  86.9 0.6 shard_map.84
  87.5 11.8 %all-to-all-start.3 = ((f32[16,4,128]{2,1,0:T(4,128)}), f32[16,4,128]{2,1,0:T(4,128)S(1)}, u32[]{:S(2)}, u32[]{:S(2)}) async-start(f32[16,4,128]{2,1,0:T(4,128)} %bitcast.9), calls=%async_computation.3 | async-start | bytes 65536 | tf_op jit(solution)/shard_map/all_to_all | solution.py:410
  99.3 1.9 %collective-permute-start.8 = (f32[16,128]{1,0:T(8,128)S(1)}, f32[16,128]{1,0:T(8,128)S(1)}, u32[]{:S(2)}, u32[]{:S(2)}) collective-permute-start(f32[16,128]{1,0:T(8,128)S(1)} %get-tuple-element.32), channel_id=1, source_target_pairs={{8,16},{16,8},{24,32},{32,24},{40,48},{48,40},{56,64},{64,56},{72,... | collective-permute-start | bytes 24584 | tf_op jit(solution)/shard_map/ppermute | solution.py:393
  101.2 14.4 %collective-permute-start.9 = (f32[16,128]{1,0:T(8,128)S(1)}, f32[16,128]{1,0:T(8,128)S(1)}, u32[]{:S(2)}, u32[]{:S(2)}) collective-permute-start(f32[16,128]{1,0:T(8,128)S(1)} %get-tuple-element.33), channel_id=1, source_target_pairs={{0,8},{8,0},{16,24},{24,16},{32,40},{40,32},{48,56},{56,48},{64,72... | collective-permute-start | bytes 24584 | tf_op jit(solution)/shard_map/ppermute | solution.py:393
  115.6 3.4 %collective-permute-start.10 = (f32[16,128]{1,0:T(8,128)S(1)}, f32[16,128]{1,0:T(8,128)S(1)}, u32[]{:S(2)}, u32[]{:S(2)}) collective-permute-start(f32[16,128]{1,0:T(8,128)S(1)} %get-tuple-element.34), channel_id=1, source_target_pairs={{0,1},{1,0},{2,3},{3,2},{4,5},{5,4},{6,7},{7,6},{8,9},{9,8},{10,11... | collective-permute-start | bytes 24584 | tf_op jit(solution)/shard_map/ppermute | solution.py:393
  119.0 1.9 %collective-permute-start.11 = (f32[16,128]{1,0:T(8,128)S(1)}, f32[16,128]{1,0:T(8,128)S(1)}, u32[]{:S(2)}, u32[]{:S(2)}) collective-permute-start(f32[16,128]{1,0:T(8,128)S(1)} %get-tuple-element.35), channel_id=1, source_target_pairs={{1,2},{2,1},{3,4},{4,3},{5,6},{6,5},{9,10},{10,9},{11,12},{12,11},... | collective-permute-start | bytes 24584 | tf_op jit(solution)/shard_map/ppermute | solution.py:393
  120.9 0.0 collective-permute-done.8.q2
  120.9 0.0 collective-permute-done.9.q1
  120.9 0.2 collective-permute-done.10.r1
  121.1 3.4 %collective-permute-done.11.r2 = f32[16,128]{1,0:T(8,128)S(1)} collective-permute-done((f32[16,128]{1,0:T(8,128)S(1)}, f32[16,128]{1,0:T(8,128)S(1)}, u32[]{:S(2)}, u32[]{:S(2)}) %collective-permute-start.11) | collective-permute-done | bytes 8224 | tf_op jit(solution)/shard_map/ppermute | solution.py:393
  124.5 0.0 all-to-all-done.3
  124.5 1.4 %shard_map.85 = (bf16[16,16,128]{2,1,0:T(8,128)(2,1)}, bf16[16,16,128]{2,1,0:T(8,128)(2,1)}) custom-call(f32[16,16,128]{2,1,0:T(8,128)S(1)} %copy-done.1, f32[16,128]{1,0:T(8,128)S(1)} %get-tuple-element.19.kap, f32[16,16,128]{2,1,0:T(8,128)S(1)} %get-tuple-element.30.old, f32[64,128]{1,0:T(8,128)S(1)} %bitcast.14, f32[192,512]{1,0:T(8,128)S(1)} %shard_map.82.shifted, ...), custom_call_target="tpu_custom_call" | custom-call | tf_op jit(solution)/shard_map/pallas_call | solution.py:447
  (5 shorter events, 0.0 us)
Async XLA Ops:
  0.6 0.7 copy-start.4
  1.3 0.7 copy-start.5
  2.0 25.0 %copy-start.2 = (f32[8]{0:T(128)S(1)}, f32[8]{0:T(128)}, u32[]{:S(2)}) copy-start(f32[8]{0:T(128)} %robin_table.3) | copy-start | bytes 100
  2.0 25.0 %copy-start.3 = (s32[1,1,2]{2,1,0:T(1,128)S(1)}, s32[1,1,2]{2,1,0:T(1,128)}, u32[]{:S(2)}) copy-start(s32[1,1,2]{2,1,0:T(1,128)} %param.10) | copy-start | bytes 28
  2.0 25.0 %copy-start.6 = (f32[16]{0:T(128)S(1)}, f32[16]{0:T(128)}, u32[]{:S(2)}) copy-start(f32[16]{0:T(128)} %table.1) | copy-start | bytes 196
  2.0 22.4 %collective-permute-start.3 = (f32[8,128]{1,0:T(8,128)S(1)}, f32[8,128]{1,0:T(8,128)S(1)}, u32[]{:S(2)}, u32[]{:S(2)}) collective-permute-start(f32[8,128]{1,0:T(8,128)S(1)} %shard_map.77.own), channel_id=1, source_target_pairs={{8,16},{16,8},{24,32},{32,24},{40,48},{48,40},{56,64},{64,56},{72,... | collective-permute-start | bytes 12296 | tf_op jit(solution)/shard_map/ppermute | solution.py:393
  4.3 20.1 %collective-permute-start.2 = (f32[8,128]{1,0:T(8,128)S(1)}, f32[8,128]{1,0:T(8,128)S(1)}, u32[]{:S(2)}, u32[]{:S(2)}) collective-permute-start(f32[8,128]{1,0:T(8,128)S(1)} %shard_map.77.own), channel_id=1, source_target_pairs={{0,8},{8,0},{16,24},{24,16},{32,40},{40,32},{48,56},{56,48},{64,72... | collective-permute-start | bytes 12296 | tf_op jit(solution)/shard_map/ppermute | solution.py:393
  18.6 5.9 %collective-permute-start.1 = (f32[8,128]{1,0:T(8,128)S(1)}, f32[8,128]{1,0:T(8,128)S(1)}, u32[]{:S(2)}, u32[]{:S(2)}) collective-permute-start(f32[8,128]{1,0:T(8,128)S(1)} %shard_map.77.own), channel_id=1, source_target_pairs={{0,1},{1,0},{2,3},{3,2},{4,5},{5,4},{6,7},{7,6},{8,9},{9,8},{10,11... | collective-permute-start | bytes 12296 | tf_op jit(solution)/shard_map/ppermute | solution.py:393
  21.5 5.5 %collective-permute-start = (f32[8,128]{1,0:T(8,128)S(1)}, f32[8,128]{1,0:T(8,128)S(1)}, u32[]{:S(2)}, u32[]{:S(2)}) collective-permute-start(f32[8,128]{1,0:T(8,128)S(1)} %shard_map.77.own), channel_id=1, source_target_pairs={{1,2},{2,1},{3,4},{4,3},{5,6},{6,5},{9,10},{10,9},{11,12},{12,11},... | collective-permute-start | bytes 12296 | tf_op jit(solution)/shard_map/ppermute | solution.py:393
  27.0 0.9 copy-start
  41.0 33.1 %all-to-all-start.1 = ((f32[16,4,128]{2,1,0:T(4,128)}), f32[16,4,128]{2,1,0:T(4,128)S(1)}, u32[]{:S(2)}, u32[]{:S(2)}) async-start(f32[16,4,128]{2,1,0:T(4,128)} %bitcast.4), calls=%async_computation.1 | async-start | bytes 65536 | tf_op jit(solution)/shard_map/all_to_all | solution.py:410
  46.9 16.2 %collective-permute-start.4 = (f32[32,128]{1,0:T(8,128)S(1)}, f32[32,128]{1,0:T(8,128)S(1)}, u32[]{:S(2)}, u32[]{:S(2)}) collective-permute-start(f32[32,128]{1,0:T(8,128)S(1)} %get-tuple-element.24), channel_id=1, source_target_pairs={{8,16},{16,8},{24,32},{32,24},{40,48},{48,40},{56,64},{64,56},{72,... | collective-permute-start | bytes 49160 | tf_op jit(solution)/shard_map/ppermute | solution.py:393
  48.8 15.1 %collective-permute-start.5 = (f32[32,128]{1,0:T(8,128)S(1)}, f32[32,128]{1,0:T(8,128)S(1)}, u32[]{:S(2)}, u32[]{:S(2)}) collective-permute-start(f32[32,128]{1,0:T(8,128)S(1)} %get-tuple-element.25), channel_id=1, source_target_pairs={{0,8},{8,0},{16,24},{24,16},{32,40},{40,32},{48,56},{56,48},{64,72... | collective-permute-start | bytes 49160 | tf_op jit(solution)/shard_map/ppermute | solution.py:393
  63.9 5.6 %collective-permute-start.6 = (f32[32,128]{1,0:T(8,128)S(1)}, f32[32,128]{1,0:T(8,128)S(1)}, u32[]{:S(2)}, u32[]{:S(2)}) collective-permute-start(f32[32,128]{1,0:T(8,128)S(1)} %get-tuple-element.28), channel_id=1, source_target_pairs={{0,1},{1,0},{2,3},{3,2},{4,5},{5,4},{6,7},{7,6},{8,9},{9,8},{10,11... | collective-permute-start | bytes 49160 | tf_op jit(solution)/shard_map/ppermute | solution.py:393
  67.3 6.8 %copy-start.1 = (f32[16,16,128]{2,1,0:T(8,128)S(1)}, f32[16,16,128]{2,1,0:T(8,128)}, u32[]{:S(2)}) copy-start(f32[16,16,128]{2,1,0:T(8,128)} %right.5) | copy-start | bytes 393220
  67.3 5.8 %collective-permute-start.7 = (f32[32,128]{1,0:T(8,128)S(1)}, f32[32,128]{1,0:T(8,128)S(1)}, u32[]{:S(2)}, u32[]{:S(2)}) collective-permute-start(f32[32,128]{1,0:T(8,128)S(1)} %get-tuple-element.29), channel_id=1, source_target_pairs={{1,2},{2,1},{3,4},{4,3},{5,6},{6,5},{9,10},{10,9},{11,12},{12,11},... | collective-permute-start | bytes 49160 | tf_op jit(solution)/shard_map/ppermute | solution.py:393
  87.5 37.0 %all-to-all-start.3 = ((f32[16,4,128]{2,1,0:T(4,128)}), f32[16,4,128]{2,1,0:T(4,128)S(1)}, u32[]{:S(2)}, u32[]{:S(2)}) async-start(f32[16,4,128]{2,1,0:T(4,128)} %bitcast.9), calls=%async_computation.3 | async-start | bytes 65536 | tf_op jit(solution)/shard_map/all_to_all | solution.py:410
  99.3 21.6 %collective-permute-start.8 = (f32[16,128]{1,0:T(8,128)S(1)}, f32[16,128]{1,0:T(8,128)S(1)}, u32[]{:S(2)}, u32[]{:S(2)}) collective-permute-start(f32[16,128]{1,0:T(8,128)S(1)} %get-tuple-element.32), channel_id=1, source_target_pairs={{8,16},{16,8},{24,32},{32,24},{40,48},{48,40},{56,64},{64,56},{72,... | collective-permute-start | bytes 24584 | tf_op jit(solution)/shard_map/ppermute | solution.py:393
  101.2 19.7 %collective-permute-start.9 = (f32[16,128]{1,0:T(8,128)S(1)}, f32[16,128]{1,0:T(8,128)S(1)}, u32[]{:S(2)}, u32[]{:S(2)}) collective-permute-start(f32[16,128]{1,0:T(8,128)S(1)} %get-tuple-element.33), channel_id=1, source_target_pairs={{0,8},{8,0},{16,24},{24,16},{32,40},{40,32},{48,56},{56,48},{64,72... | collective-permute-start | bytes 24584 | tf_op jit(solution)/shard_map/ppermute | solution.py:393
  115.6 5.5 %collective-permute-start.10 = (f32[16,128]{1,0:T(8,128)S(1)}, f32[16,128]{1,0:T(8,128)S(1)}, u32[]{:S(2)}, u32[]{:S(2)}) collective-permute-start(f32[16,128]{1,0:T(8,128)S(1)} %get-tuple-element.34), channel_id=1, source_target_pairs={{0,1},{1,0},{2,3},{3,2},{4,5},{5,4},{6,7},{7,6},{8,9},{9,8},{10,11... | collective-permute-start | bytes 24584 | tf_op jit(solution)/shard_map/ppermute | solution.py:393
  119.0 5.5 %collective-permute-start.11 = (f32[16,128]{1,0:T(8,128)S(1)}, f32[16,128]{1,0:T(8,128)S(1)}, u32[]{:S(2)}, u32[]{:S(2)}) collective-permute-start(f32[16,128]{1,0:T(8,128)S(1)} %get-tuple-element.35), channel_id=1, source_target_pairs={{1,2},{2,1},{3,4},{4,3},{5,6},{6,5},{9,10},{10,9},{11,12},{12,11},... | collective-permute-start | bytes 24584 | tf_op jit(solution)/shard_map/ppermute | solution.py:393
